TPU v7x, 32 devices: a whole 2x2x4 slice. The times are simulated.
32 devices in a mesh: dp: 8 (over y, x, core), seq: 4 (over z).
Axes of the slice: x: 2, y: 2, z: 4, core: 2. Of those that a mesh axis runs over, the one named last changes fastest.
Arguments:
- tokens: bfloat16 [24, 736, 1152], P('dp', 'seq'), may hold values from -6 to 6
- out_grad: bfloat16 [24, 736, 1152], P('dp', 'seq'), may hold values from -6 to 6
- image_count: int32 [8], P('dp'), may hold values from 1 to 3, 18 in all
- adapter_id: int32 [24], P('dp'), may hold values from 0 to 7
- key_live: int32 [24, 736], P('dp'), may hold values from 0 to 1, as said below
- w_qkv: bfloat16 [1152, 3, 1152], P('seq'), may hold values from -0.1875 to 0.1875
- w_out: bfloat16 [1152, 1152], P('seq'), may hold values from -0.75 to 0.75
- w_fc1: bfloat16 [1152, 4304], P('seq'), may hold values from -0.1875 to 0.1875
- w_fc2: bfloat16 [4304, 1152], P('seq'), may hold values from -0.09375 to 0.09375
- norm_gain: float32 [2, 1152], replicated, may hold values from 0.25 to 1.75
- norm_bias: float32 [2, 1152], replicated, may hold values from -2 to 2
- proj_bias: float32 [4, 1152], replicated, may hold values from -2 to 2
- hidden_bias: float32 [4304], replicated, may hold values from -3 to 3
- down_attn: bfloat16 [4, 1152, 128], replicated, may hold values from -0.1875 to 0.1875
- up_attn: bfloat16 [4, 128, 1152], replicated, may hold values from -1.5 to 1.5
- down_fc1: bfloat16 [1152, 128], replicated, may hold values from -0.1875 to 0.1875
- up_fc1: bfloat16 [128, 4304], replicated, may hold values from -1.5 to 1.5
- down_fc2: bfloat16 [4304, 128], replicated, may hold values from -0.09375 to 0.09375
- up_fc2: bfloat16 [128, 1152], replicated, may hold values from -1.5 to 1.5
Outputs:
- layer_out: bfloat16 [24, 736, 1152], P('dp', 'seq')
- input_grad: float32 [24, 736, 1152], P('dp', 'seq')
- down_attn_grad: float32 [4, 1152, 128], replicated
- up_attn_grad: float32 [4, 128, 1152], replicated
- down_fc1_grad: float32 [1152, 128], replicated
- up_fc1_grad: float32 [128, 4304], replicated
- down_fc2_grad: float32 [4304, 128], replicated
- up_fc2_grad: float32 [128, 1152], replicated
Inputs may be any that keep to these rules, and one draw needn't show every extreme that they name: Group g of 3 image slots holds image_count[g] live images, in its first slots; the counts sum to 18, and some group is full. `key_live`: each image has exactly 7 pad slots, at positions drawn per image.
All inputs are finite; a program needn't handle non-finite values.
Results may differ from a plain program's by a relative error of at most 0.015.
The roundings to bfloat16 on the way count: a program that leaves them out, or rounds other values in their place, can miss the bound.
Values may be sent and summed in bfloat16 or wider, within the bound.
No kernel may reach another device: no remote copies, remote signals or barrier semaphores. Data moves between devices by JAX's collectives and lax.ppermute only.
A program may use at most 192 MiB of HBM per device.

v0:
```python
import jax
import jax.numpy as jnp
from jax import lax
from jax.sharding import PartitionSpec as P

HD = 72
RANK = 16


norm_eps = 1e-06


def product(left, right):
    return jnp.dot(left, right, preferred_element_type=jnp.float32)


def product_back(grad, weight):
    return jnp.einsum("itc,dc->itd", grad, weight, preferred_element_type=jnp.float32)


def outer_sum(left, right):
    return jnp.einsum("itd,itc->dc", left, right, preferred_element_type=jnp.float32)


def layer_norm(values, gain, shift):
    average = jnp.mean(values, axis=-1, keepdims=True)
    centred = values - average
    variance = jnp.mean(centred * centred, axis=-1, keepdims=True)
    return centred * lax.rsqrt(variance + norm_eps) * gain + shift


def norm_back(values, gain, shift, grad):

    def local_norm(inner_values):
        return layer_norm(inner_values, gain, shift)

    return jax.vjp(local_norm, values)[1](grad)[0]


def gelu_tanh(values):
    return jax.nn.gelu(values, approximate=True)


def rank_forward(inputs, down_factor, select):
    return (product(inputs, down_factor) * select).astype(jnp.bfloat16)


def adapter_back(inputs, grad, down_factor, up_factor, rank_part, select):
    grad_up = outer_sum(rank_part, grad)
    inner_grad = (product_back(grad, up_factor) * select).astype(jnp.bfloat16)
    grad_down = outer_sum(inputs, inner_grad)
    return (grad_down, grad_up, product_back(inner_grad, down_factor))


def attend_image(operands):
    queries, key_rows, value_rows, key_mask = operands
    scores = jnp.einsum(
        "qhd,khd->hqk", queries, key_rows, preferred_element_type=jnp.float32
    ) * HD ** (-0.5)
    scores = jnp.where(key_mask[None, None, :] > 0, scores, -1e30)
    row_top = jnp.max(scores, axis=-1, keepdims=True)
    exponent = jnp.exp(scores - row_top)
    row_total = jnp.sum(exponent, axis=-1, keepdims=True)
    attn_probs = (exponent / row_total).astype(jnp.bfloat16)
    output = jnp.einsum("hqk,khd->qhd", attn_probs, value_rows, preferred_element_type=jnp.float32)
    return (output, (row_top + jnp.log(row_total))[:, :, 0])


def attend_back(operands):
    queries, key_rows, value_rows, key_mask, log_total, grad_out = operands
    scores = jnp.einsum(
        "qhd,khd->hqk", queries, key_rows, preferred_element_type=jnp.float32
    ) * HD ** (-0.5)
    scores = jnp.where(key_mask[None, None, :] > 0, scores, -1e30)
    attn_probs = jnp.exp(scores - log_total[:, :, None])
    grad_values = jnp.einsum(
        "hqk,qhd->khd",
        attn_probs.astype(jnp.bfloat16),
        grad_out,
        preferred_element_type=jnp.float32,
    )
    grad_probs = jnp.einsum(
        "qhd,khd->hqk", grad_out, value_rows, preferred_element_type=jnp.float32
    )
    row_dot = jnp.sum(attn_probs * grad_probs, axis=-1, keepdims=True)
    grad_scores = (attn_probs * (grad_probs - row_dot)).astype(jnp.bfloat16)
    grad_queries = jnp.einsum(
        "hqk,khd->qhd", grad_scores, key_rows, preferred_element_type=jnp.float32
    ) * HD ** (-0.5)
    grad_keys = jnp.einsum(
        "hqk,qhd->khd", grad_scores, queries, preferred_element_type=jnp.float32
    ) * HD ** (-0.5)
    return (
        grad_queries.astype(jnp.bfloat16),
        grad_keys.astype(jnp.bfloat16),
        grad_values.astype(jnp.bfloat16),
    )


def local(
    tokens,
    out_grad,
    image_count,
    adapter_id,
    key_live,
    w_qkv,
    w_out,
    w_fc1,
    w_fc2,
    norm_gain,
    norm_bias,
    proj_bias,
    hidden_bias,
    down_attn,
    up_attn,
    down_fc1,
    up_fc1,
    down_fc2,
    up_fc2,
):
    images, local_len, width = tokens.shape
    columns = down_attn.shape[-1]
    image_slot = jnp.arange(images, dtype=jnp.int32)
    live = (image_slot < image_count[0]).astype(jnp.float32)[:, None, None]
    column_owner = jnp.arange(columns, dtype=jnp.int32) // RANK
    select = (column_owner[None, :] == adapter_id[:, None]).astype(jnp.float32)[:, None, :]
    full_weights = (
        lax.all_gather(w_qkv, "seq", axis=0, tiled=True),
        lax.all_gather(w_out, "seq", axis=0, tiled=True),
        lax.all_gather(w_fc1, "seq", axis=0, tiled=True),
        lax.all_gather(w_fc2, "seq", axis=0, tiled=True),
    )
    flat = tokens.astype(jnp.float32)
    normed = layer_norm(flat, norm_gain[0], norm_bias[0]).astype(jnp.bfloat16)
    joined = product(normed, full_weights[0].reshape(width, 3 * width))
    rank_parts = []
    projected = []
    for index in range(3):
        rank_part = rank_forward(normed, down_attn[index], select)
        rank_parts.append(rank_part)
        projected.append(
            joined[:, :, index * width : (index + 1) * width] + product(rank_part, up_attn[index])
        )
    queries = (projected[0] + proj_bias[0]).astype(jnp.bfloat16)
    key_rows = projected[1].astype(jnp.bfloat16)
    value_rows = (projected[2] + proj_bias[1]).astype(jnp.bfloat16)
    head_q, head_k, head_v = (
        lax.all_to_all(queries, "seq", split_axis=2, concat_axis=1, tiled=True),
        lax.all_to_all(key_rows, "seq", split_axis=2, concat_axis=1, tiled=True),
        lax.all_to_all(value_rows, "seq", split_axis=2, concat_axis=1, tiled=True),
    )
    full_len = head_q.shape[1]
    local_width = head_q.shape[2]
    local_heads = local_width // HD
    head_shape = (images, full_len, local_heads, HD)
    split_q = head_q.reshape(head_shape)
    split_k = head_k.reshape(head_shape)
    split_v = head_v.reshape(head_shape)
    attended, log_total = lax.map(attend_image, (split_q, split_k, split_v, key_live))
    attended = attended.reshape(images, full_len, local_width).astype(jnp.bfloat16)
    merged = lax.all_to_all(attended, "seq", split_axis=1, concat_axis=2, tiled=True)
    rank_out = rank_forward(merged, down_attn[3], select)
    branch = product(merged, full_weights[1]) + product(rank_out, up_attn[3]) + proj_bias[2]
    resid = flat + branch
    normed_two = layer_norm(resid, norm_gain[1], norm_bias[1]).astype(jnp.bfloat16)
    rank_one = rank_forward(normed_two, down_fc1, select)
    hidden = product(normed_two, full_weights[2]) + product(rank_one, up_fc1) + hidden_bias
    activated = gelu_tanh(hidden).astype(jnp.bfloat16)
    rank_two = rank_forward(activated, down_fc2, select)
    branch_two = product(activated, full_weights[3]) + product(rank_two, up_fc2) + proj_bias[3]
    result = ((resid + branch_two) * live).astype(jnp.bfloat16)
    back_weights = (
        lax.all_gather(w_qkv, "seq", axis=0, tiled=True),
        lax.all_gather(w_out, "seq", axis=0, tiled=True),
        lax.all_gather(w_fc1, "seq", axis=0, tiled=True),
        lax.all_gather(w_fc2, "seq", axis=0, tiled=True),
    )
    top_grad = out_grad.astype(jnp.float32) * live
    two_grad = top_grad.astype(jnp.bfloat16)
    down_fc2_grad, up_fc2_grad, act_grad = adapter_back(
        activated, two_grad, down_fc2, up_fc2, rank_two, select
    )
    act_grad = act_grad + product_back(two_grad, back_weights[3])
    hidden_grad = jax.vjp(gelu_tanh, hidden)[1](act_grad)[0].astype(jnp.bfloat16)
    down_fc1_grad, up_fc1_grad, normed_two_grad = adapter_back(
        normed_two, hidden_grad, down_fc1, up_fc1, rank_one, select
    )
    normed_two_grad = normed_two_grad + product_back(hidden_grad, back_weights[2])
    resid_grad = top_grad + norm_back(resid, norm_gain[1], norm_bias[1], normed_two_grad)
    branch_grad = resid_grad.astype(jnp.bfloat16)
    down_out_grad, up_out_grad, merged_grad = adapter_back(
        merged, branch_grad, down_attn[3], up_attn[3], rank_out, select
    )
    merged_grad = (merged_grad + product_back(branch_grad, back_weights[1])).astype(jnp.bfloat16)
    head_grad = lax.all_to_all(merged_grad, "seq", split_axis=2, concat_axis=1, tiled=True)
    grad_q, grad_k, grad_v = lax.map(
        attend_back, (split_q, split_k, split_v, key_live, log_total, head_grad.reshape(head_shape))
    )
    flat_shape = (images, full_len, local_width)
    token_q, token_k, token_v = (
        lax.all_to_all(grad_q.reshape(flat_shape), "seq", split_axis=1, concat_axis=2, tiled=True),
        lax.all_to_all(grad_k.reshape(flat_shape), "seq", split_axis=1, concat_axis=2, tiled=True),
        lax.all_to_all(grad_v.reshape(flat_shape), "seq", split_axis=1, concat_axis=2, tiled=True),
    )
    proj_grads = (token_q, token_k, token_v)
    joined_grad = jnp.concatenate(proj_grads, axis=2)
    normed_grad = product_back(joined_grad, back_weights[0].reshape(width, 3 * width))
    down_list = []
    up_list = []
    for index in range(3):
        grad_down, grad_up, back_term = adapter_back(
            normed, proj_grads[index], down_attn[index], up_attn[index], rank_parts[index], select
        )
        down_list.append(grad_down)
        up_list.append(grad_up)
        normed_grad = normed_grad + back_term
    down_list.append(down_out_grad)
    up_list.append(up_out_grad)
    down_attn_grad = jnp.stack(down_list)
    up_attn_grad = jnp.stack(up_list)
    input_grad = resid_grad + norm_back(flat, norm_gain[0], norm_bias[0], normed_grad)
    down_attn_sum, up_attn_sum, down_fc1_sum, up_fc1_sum, down_fc2_sum, up_fc2_sum = lax.psum(
        (down_attn_grad, up_attn_grad, down_fc1_grad, up_fc1_grad, down_fc2_grad, up_fc2_grad),
        ("dp", "seq"),
    )
    return (
        result,
        input_grad,
        down_attn_sum,
        up_attn_sum,
        down_fc1_sum,
        up_fc1_sum,
        down_fc2_sum,
        up_fc2_sum,
    )


def solution(mesh):
    in_specs = (
        P("dp", "seq", None),
        P("dp", "seq", None),
        P("dp"),
        P("dp"),
        P("dp", None),
        P("seq", None, None),
        P("seq", None),
        P("seq", None),
        P("seq", None),
        P(),
        P(),
        P(),
        P(),
        P(),
        P(),
        P(),
        P(),
        P(),
        P(),
    )
    out_specs = (P("dp", "seq", None), P("dp", "seq", None), P(), P(), P(), P(), P(), P())
    return jax.shard_map(local, mesh=mesh, in_specs=in_specs, out_specs=out_specs, check_vma=False)
```

profile of v0, /device:TPU:0, one launch (start us, length us, event | category | flops | bytes accessed | tf_op | source)
XLA Modules:
  0.0 1329.5 jit_solution(2850736598524813166)
XLA Ops:
  18.0 137.0 %all-gather.6.cloned.1.call-done = bf16[1152,3,1152]{2,0,1:T(8,128)(2,1)} async-done(((bf16[288,3,1152]{2,0,1:T(8,128)(2,1)}), bf16[1152,3,1152]{2,0,1:T(8,128)(2,1)}) %all-gather.6.cloned.1.call-update) | async-done | bytes 7962640 | tf_op jit(solution)/shard_map/all_gather | solution.py:128
  155.0 13.1 copy.82
  168.1 8.9 fusion.175
  202.3 109.7 %all-to-all-done = bf16[3,184,1152]{1,0,2:T(4,128)(2,1)} async-done(((bf16[3,184,1152]{1,0,2:T(4,128)(2,1)}), bf16[3,184,1152]{1,0,2:T(4,128)(2,1)}, u32[]{:S(2)}, u32[]{:S(2)}) %all-to-all-start) | async-done | bytes 1271840 | tf_op jit(solution)/shard_map/all_to_all | solution.py:150
  325.0 92.0 %all-to-all-done.1 = bf16[3,184,1152]{1,0,2:T(4,128)(2,1)} async-done(((bf16[3,184,1152]{1,0,2:T(4,128)(2,1)}), bf16[3,184,1152]{1,0,2:T(4,128)(2,1)}, u32[]{:S(2)}, u32[]{:S(2)}) %all-to-all-start.1) | async-done | bytes 1271840 | tf_op jit(solution)/shard_map/all_to_all | solution.py:148
  435.4 84.2 %all-to-all-done.2 = bf16[3,184,1152]{1,0,2:T(4,128)(2,1)} async-done(((bf16[3,184,1152]{1,0,2:T(4,128)(2,1)}), bf16[3,184,1152]{1,0,2:T(4,128)(2,1)}, u32[]{:S(2)}, u32[]{:S(2)}) %all-to-all-start.2) | async-done | bytes 1271840 | tf_op jit(solution)/shard_map/all_to_all | solution.py:149
  528.6 29.8 %while.26 = (s32[]{:T(128)}, bf16[3,736,4,72]{1,3,2,0:T(8,128)(2,1)}, f32[3,4,736]{2,1,0:T(4,128)S(1)}, bf16[3,736,4,72]{1,3,2,0:T(8,128)(2,1)}, s32[3,736]{1,0:...) while((s32[]{:T(128)}, ...), condition=%wide.region_5.6_spmd, body=%wide.region_2.5_spmd.sunk | while | flops 650033024 | bytes 38869980 | solution.py:159
  571.5 11.4 reshape.215
  583.0 16.6 %fusion.166 = f32[3,184,4304]{2,1,0:T(8,128)} fusion(bf16[4304,1152,1]{1,0,2:T(8,128)(2,1)} %reshape.215, bf16[3,184,1152]{2,1,0:T(8,128)(2,1)S(1)} %copy-done.13, f32[3]{0:T(128)S(1)} %compare_convert_fusion), kind=kOutput, calls=%fused_computation.242 | convolution fusion | flops 5475769344 | bytes 20691468 | tf_op jit(solution)/shard_map/itc,dc->itd/dot_general | solution.py:18
  599.6 79.9 %all-to-all-done.3 = bf16[3,736,288]{2,0,1:T(4,128)(2,1)} async-done(((bf16[3,736,288]{2,0,1:T(4,128)(2,1)}), bf16[3,736,288]{2,0,1:T(4,128)(2,1)}, u32[]{:S(2)}, u32[]{:S(2)}) %all-to-all-start.3) | async-done | bytes 1271840 | tf_op jit(solution)/shard_map/all_to_all | solution.py:161
  694.5 53.8 %all-gather.10.cloned.1.call-done = bf16[1152,4304]{1,0:T(8,128)(2,1)} async-done(((bf16[288,4304]{1,0:T(8,128)(2,1)}), bf16[1152,4304]{1,0:T(8,128)(2,1)}) %all-gather.10.cloned.1.call-update) | async-done | bytes 9916432 | tf_op jit(solution)/shard_map/all_gather | solution.py:130
  748.3 12.3 fusion.60
  760.6 8.2 multiply_convert_fusion.1
  768.9 9.7 fusion.68
  783.5 14.2 %multiply_reduce_fusion.1 = (f32[3,184]{1,0:T(4,128)S(1)}, f32[3,184,1152]{2,1,0:T(8,128)}) fusion(f32[3,184,1152]{2,1,0:T(8,128)S(1)} %copy-done.3, f32[3,184]{1,0:T(4,128)S(1)} %broadcast_multiply_fusion, f32[1152]{0:T(1024)S(1)} %copy-done.79, f32[3,184,1152]{2,1,0:T(8,128)} %fusion.127, bf16[3,184,4304]{2,1,0:T(8,128)(2,1)} %copy-done.29, ...), kind=kOutput, calls=%fused_computation.129 | convolution fusion | flops 5477040640 | bytes 22307904 | tf_op jit(solution)/shard_map/itc,dc->itd/dot_general | solution.py:18
  814.8 54.2 %all-to-all-done.4 = bf16[3,184,1152]{1,0,2:T(4,128)(2,1)S(1)} async-done(((bf16[3,184,1152]{1,0,2:T(4,128)(2,1)}), bf16[3,184,1152]{1,0,2:T(4,128)(2,1)S(1)}, u32[]{:S(2)}, u32[]{:S(2)}) %all-to-all-start.4) | async-done | bytes 1271840 | tf_op jit(solution)/shard_map/all_to_all | solution.py:195
  876.5 44.6 %while.27 = (s32[]{:T(128)}, bf16[3,736,4,72]{1,3,2,0:T(8,128)(2,1)}, bf16[3,736,4,72]{1,3,2,0:T(8,128)(2,1)}, bf16[3,736,4,72]{1,3,2,0:T(8,128)(2,1)}, bf16[3,7...) while((s32[]{:T(128)}, ...), condition=%wide.region_12.13_spmd, body=%wide.region_10.12_spmd.sunk | while | flops 1593643904 | bytes 85914640 | solution.py:196
  935.1 46.1 %all-to-all-done.7 = bf16[3,736,288]{2,0,1:T(4,128)(2,1)S(1)} async-done(((bf16[3,736,288]{2,0,1:T(4,128)(2,1)}), bf16[3,736,288]{2,0,1:T(4,128)(2,1)S(1)}, u32[]{:S(2)}, u32[]{:S(2)}) %all-to-all-start.7) | async-done | bytes 1271840 | tf_op jit(solution)/shard_map/all_to_all | solution.py:203
  998.7 38.4 %all-to-all-done.6 = bf16[3,736,288]{2,0,1:T(4,128)(2,1)} async-done(((bf16[3,736,288]{2,0,1:T(4,128)(2,1)}), bf16[3,736,288]{2,0,1:T(4,128)(2,1)}, u32[]{:S(2)}, u32[]{:S(2)}) %all-to-all-start.6) | async-done | bytes 1271840 | tf_op jit(solution)/shard_map/all_to_all | solution.py:202
  1048.9 5.9 convolution_bitcast_fusion
  1075.7 17.2 %all-to-all-done.5 = bf16[3,736,288]{2,0,1:T(4,128)(2,1)} async-done(((bf16[3,736,288]{2,0,1:T(4,128)(2,1)}), bf16[3,736,288]{2,0,1:T(4,128)(2,1)}, u32[]{:S(2)}, u32[]{:S(2)}) %all-to-all-start.5) | async-done | bytes 1271840 | tf_op jit(solution)/shard_map/all_to_all | solution.py:201
  1111.4 10.5 fusion.179
  1124.6 8.9 fusion.73
  1140.0 172.6 %all-reduce.3.cloned.1.call-done = (f32[4,1152,128]{2,1,0:T(8,128)}, f32[4,128,1152]{2,1,0:T(8,128)}, f32[1152,128]{1,0:T(8,128)}, f32[128,4304]{0,1:T(8,128)}, f32[4304,128]{1,0:T(8,128)}, /*index=5*/f32[128,1152]{1,0:T(8,128)}) async-done(((f32[4,1152,128]{2,1,0:T(8,128)}, f32[4,128,1152]{2,1,0:T(8,128)}, f32[1152,128]{1,0:T(8,128)}, f32[128,4304]{0,1:T(8,128)}, f32[4304,128]{1,0:T(8,128)}, ...) | async-done | bytes 10305552 | tf_op jit(solution)/shard_map/psum | solution.py:222
  (357 shorter events, 308.3 us)
Async XLA Ops:
  7.2 753.4 %copy-start = (bf16[128,4304]{0,1:T(8,128)(2,1)S(1)}, bf16[128,4304]{0,1:T(8,128)(2,1)}, u32[]{:S(2)}) copy-start(bf16[128,4304]{0,1:T(8,128)(2,1)} %param.39) | copy-start | bytes 3305476
  7.2 147.8 %all-gather.6.cloned.1.call-start = ((), (), s32[]{:S(2)}) async-start(), calls=%async_computation.8 | async-start | bytes 9953280 | tf_op jit(solution)/shard_map/all_gather | solution.py:128
  7.9 563.6 %all-gather.12.cloned.1.call-start = ((), (), s32[]{:S(2)}) async-start(), calls=%async_computation.11 | async-start | bytes 12441600 | tf_op jit(solution)/shard_map/all_gather | solution.py:131
  8.7 677.6 %all-gather.8.cloned.1.call-start = ((), (), s32[]{:S(2)}) async-start(), calls=%async_computation.9 | async-start | bytes 3317760 | tf_op jit(solution)/shard_map/all_gather | solution.py:129
  168.1 12.0 copy-start.48
  168.1 12.0 copy-start.82
  187.4 124.7 %all-to-all-start = ((bf16[3,184,1152]{1,0,2:T(4,128)(2,1)}), bf16[3,184,1152]{1,0,2:T(4,128)(2,1)}, u32[]{:S(2)}, u32[]{:S(2)}) async-start(bf16[3,184,1152]{1,0,2:T(4,128)(2,1)} %copy.84), calls=%async_computation | async-start | bytes 4718592 | tf_op jit(solution)/shard_map/all_to_all | solution.py:150
  312.0 105.0 %all-to-all-start.1 = ((bf16[3,184,1152]{1,0,2:T(4,128)(2,1)}), bf16[3,184,1152]{1,0,2:T(4,128)(2,1)}, u32[]{:S(2)}, u32[]{:S(2)}) async-start(bf16[3,184,1152]{1,0,2:T(4,128)(2,1)} %copy.86), calls=%async_computation.1 | async-start | bytes 4718592 | tf_op jit(solution)/shard_map/all_to_all | solution.py:148
  316.6 431.7 %all-gather.10.cloned.1.call-start = ((), (), s32[]{:S(2)}) async-start(), calls=%async_computation.10 | async-start | bytes 12533760 | tf_op jit(solution)/shard_map/all_gather | solution.py:130
  417.0 102.6 %all-to-all-start.2 = ((bf16[3,184,1152]{1,0,2:T(4,128)(2,1)}), bf16[3,184,1152]{1,0,2:T(4,128)(2,1)}, u32[]{:S(2)}, u32[]{:S(2)}) async-start(bf16[3,184,1152]{1,0,2:T(4,128)(2,1)} %copy.88), calls=%async_computation.2 | async-start | bytes 4718592 | tf_op jit(solution)/shard_map/all_to_all | solution.py:149
  563.8 115.7 %all-to-all-start.3 = ((bf16[3,736,288]{2,0,1:T(4,128)(2,1)}), bf16[3,736,288]{2,0,1:T(4,128)(2,1)}, u32[]{:S(2)}, u32[]{:S(2)}) async-start(bf16[3,736,288]{2,0,1:T(4,128)(2,1)} %copy.90), calls=%async_computation.3 | async-start | bytes 4521984 | tf_op jit(solution)/shard_map/all_to_all | solution.py:161
  571.5 197.4 %copy-start.65 = (bf16[3,184,128]{2,1,0:T(8,128)(2,1)}, bf16[3,184,128]{2,1,0:T(8,128)(2,1)S(1)}, u32[]{:S(2)}) copy-start(bf16[3,184,128]{2,1,0:T(8,128)(2,1)S(1)} %fusion.115) | copy-start | bytes 423940
  693.9 66.7 %copy-start.16 = (bf16[3,184,1152]{2,1,0:T(8,128)(2,1)}, bf16[3,184,1152]{2,1,0:T(8,128)(2,1)S(1)}, u32[]{:S(2)}) copy-start(bf16[3,184,1152]{2,1,0:T(8,128)(2,1)S(1)} %add_convert_fusion) | copy-start | bytes 3815428
  694.5 66.1 %copy-start.46 = (bf16[3,184,128]{2,1,0:T(8,128)(2,1)}, bf16[3,184,128]{2,1,0:T(8,128)(2,1)S(1)}, u32[]{:S(2)}) copy-start(bf16[3,184,128]{2,1,0:T(8,128)(2,1)S(1)} %fusion.114) | copy-start | bytes 423940
  694.5 66.1 %copy-start.91 = (f32[4304]{0:T(1024)S(1)}, f32[4304]{0:T(1024)}, u32[]{:S(2)}) copy-start(f32[4304]{0:T(1024)} %param.35) | copy-start | bytes 51652
  810.7 58.3 %all-to-all-start.4 = ((bf16[3,184,1152]{1,0,2:T(4,128)(2,1)}), bf16[3,184,1152]{1,0,2:T(4,128)(2,1)S(1)}, u32[]{:S(2)}, u32[]{:S(2)}) async-start(bf16[3,184,1152]{1,0,2:T(4,128)(2,1)} %copy.93), calls=%async_computation.4 | async-start | bytes 4718592 | tf_op jit(solution)/shard_map/all_to_all | solution.py:195
  926.2 55.1 %all-to-all-start.7 = ((bf16[3,736,288]{2,0,1:T(4,128)(2,1)}), bf16[3,736,288]{2,0,1:T(4,128)(2,1)S(1)}, u32[]{:S(2)}, u32[]{:S(2)}) async-start(bf16[3,736,288]{2,0,1:T(4,128)(2,1)} %copy.101), calls=%async_computation.7 | async-start | bytes 4521984 | tf_op jit(solution)/shard_map/all_to_all | solution.py:203
  935.1 50.7 %copy-start.17 = (bf16[3,184,1152]{2,1,0:T(8,128)(2,1)S(1)}, bf16[3,184,1152]{2,1,0:T(8,128)(2,1)}, u32[]{:S(2)}) copy-start(bf16[3,184,1152]{2,1,0:T(8,128)(2,1)} %copy-done.16) | copy-start | bytes 3815428
  981.3 55.8 %all-to-all-start.6 = ((bf16[3,736,288]{2,0,1:T(4,128)(2,1)}), bf16[3,736,288]{2,0,1:T(4,128)(2,1)}, u32[]{:S(2)}, u32[]{:S(2)}) async-start(bf16[3,736,288]{2,0,1:T(4,128)(2,1)} %copy.98), calls=%async_computation.6 | async-start | bytes 4521984 | tf_op jit(solution)/shard_map/all_to_all | solution.py:202
  998.7 43.0 %copy-start.15 = (bf16[3,184,1152]{2,1,0:T(8,128)(2,1)S(1)}, bf16[3,184,1152]{2,1,0:T(8,128)(2,1)}, u32[]{:S(2)}) copy-start(bf16[3,184,1152]{2,1,0:T(8,128)(2,1)} %param.24) | copy-start | bytes 3815428
  998.7 44.3 %copy-start.47 = (bf16[3,184,128]{2,1,0:T(8,128)(2,1)S(1)}, bf16[3,184,128]{2,1,0:T(8,128)(2,1)}, u32[]{:S(2)}) copy-start(bf16[3,184,128]{2,1,0:T(8,128)(2,1)} %copy-done.46) | copy-start | bytes 423940
  1037.1 55.8 %all-to-all-start.5 = ((bf16[3,736,288]{2,0,1:T(4,128)(2,1)}), bf16[3,736,288]{2,0,1:T(4,128)(2,1)}, u32[]{:S(2)}, u32[]{:S(2)}) async-start(bf16[3,736,288]{2,0,1:T(4,128)(2,1)} %copy.95), calls=%async_computation.5 | async-start | bytes 4521984 | tf_op jit(solution)/shard_map/all_to_all | solution.py:201
  1041.6 271.0 %all-reduce.3.cloned.1.call-start = ((), (), s32[]{:S(2)}) async-start(), calls=%async_computation.12 | async-start | bytes 20611072 | tf_op jit(solution)/shard_map/psum | solution.py:222
  1060.2 13.0 copy-start.22
  (91 other events, 320.5 us)
Sparse Core Ops, SparseCore 0:
  9.6 145.3 all-gather.5
  156.5 291.6 all-gather.11
  449.9 74.1 all-gather.7
  525.5 222.7 all-gather.9
  1111.5 201.0 all-reduce.2
where the time goes:
time: 1340 us; the launch traced here: 1330 us
  waiting for transfers between devices  888 us (66%)
  matrix products  218 us (16%)
  local copies, waits for them, and re-layouts  144 us (11%)
  starting transfers between devices  35.9 us (3%)
  other arithmetic  27.3 us (2%)
  between operations  15.9 us (1%)
    psum x1, waiting for transfers between devices, local(): lax.psum((down_attn_grad, up_attn_grad, down_fc1_grad, up_fc1_grad, down_...  173 us
    all_gather x1, waiting for transfers between devices, local(): lax.all_gather(w_qkv, 'seq', axis=0, tiled=True)  137 us
    all_to_all x1, waiting for transfers between devices, local(): lax.all_to_all(value_rows, 'seq', split_axis=2, concat_axis=1, tiled=True)  110 us
    all_to_all x1, waiting for transfers between devices, local(): lax.all_to_all(queries, 'seq', split_axis=2, concat_axis=1, tiled=True)  92 us
    all_to_all x1, waiting for transfers between devices, local(): lax.all_to_all(key_rows, 'seq', split_axis=2, concat_axis=1, tiled=True)  84.2 us
    all_to_all x1, waiting for transfers between devices, local(): lax.all_to_all(attended, 'seq', split_axis=1, concat_axis=2, tiled=True)  79.9 us
    dot_general x16, matrix products, product_back(): jnp.einsum('itc,dc->itd', grad, weight, preferred_element_type=jnp.float32)  69.4 us
    dot_general x16, matrix products, product(): return jnp.dot(left, right, preferred_element_type=jnp.float32)  67 us
  transfers between devices with their start and end apart: 13, of which 11 were waited for; matrix products, arithmetic and copies ran while one was open for 17% of the time, Pallas kernels for 0%

commit v1 on v0

v1 whole, which is shorter than its diff:
```python
import jax
import jax.numpy as jnp
from jax import lax
from jax.sharding import PartitionSpec as P

HD = 72
RANK = 16
BF = jnp.bfloat16
F32 = jnp.float32

norm_eps = 1e-06


def dot(left, right, dims):
    return lax.dot_general(left, right, (dims, ((), ())), preferred_element_type=F32)


def product(left, right):
    return dot(left, right, ((1,), (0,)))


def product_back(grad, weight):
    return dot(grad, weight, ((1,), (1,)))


def outer_sum(left, right):
    return dot(left, right, ((0,), (0,)))


def layer_norm(values, gain, shift):
    average = jnp.mean(values, axis=-1, keepdims=True)
    centred = values - average
    variance = jnp.mean(centred * centred, axis=-1, keepdims=True)
    return centred * lax.rsqrt(variance + norm_eps) * gain + shift


def norm_back(values, gain, shift, grad):

    def local_norm(inner_values):
        return layer_norm(inner_values, gain, shift)

    return jax.vjp(local_norm, values)[1](grad)[0]


def gelu_tanh(values):
    return jax.nn.gelu(values, approximate=True)


def attend_heads(operands):
    queries, key_rows, value_rows, key_mask = operands
    scores = jnp.einsum(
        "qhd,khd->hqk", queries, key_rows, preferred_element_type=F32
    ) * HD ** (-0.5)
    scores = jnp.where(key_mask[None, None, :] > 0, scores, -1e30)
    row_top = jnp.max(scores, axis=-1, keepdims=True)
    exponent = jnp.exp(scores - row_top)
    row_total = jnp.sum(exponent, axis=-1, keepdims=True)
    attn_probs = (exponent / row_total).astype(BF)
    output = jnp.einsum("hqk,khd->qhd", attn_probs, value_rows, preferred_element_type=F32)
    return (output, (row_top + jnp.log(row_total))[:, :, 0])


def attend_back(operands):
    queries, key_rows, value_rows, key_mask, log_total, grad_out = operands
    scores = jnp.einsum(
        "qhd,khd->hqk", queries, key_rows, preferred_element_type=F32
    ) * HD ** (-0.5)
    scores = jnp.where(key_mask[None, None, :] > 0, scores, -1e30)
    attn_probs = jnp.exp(scores - log_total[:, :, None])
    grad_values = jnp.einsum(
        "hqk,qhd->khd", attn_probs.astype(BF), grad_out, preferred_element_type=F32
    )
    grad_probs = jnp.einsum("qhd,khd->hqk", grad_out, value_rows, preferred_element_type=F32)
    row_dot = jnp.sum(attn_probs * grad_probs, axis=-1, keepdims=True)
    grad_scores = (attn_probs * (grad_probs - row_dot)).astype(BF)
    grad_queries = jnp.einsum(
        "hqk,khd->qhd", grad_scores, key_rows, preferred_element_type=F32
    ) * HD ** (-0.5)
    grad_keys = jnp.einsum(
        "hqk,qhd->khd", grad_scores, queries, preferred_element_type=F32
    ) * HD ** (-0.5)
    return (grad_queries.astype(BF), grad_keys.astype(BF), grad_values.astype(BF))


class Place:
    def __init__(self, dp_size, seq_size):
        self.dp_size = dp_size
        self.seq_size = seq_size
        self.dp = lax.axis_index("dp")
        self.seq = lax.axis_index("seq")
        self.slot = self.image_of(self.dp, self.seq)

    def image_of(self, dp, seq):
        last = self.seq_size - 1
        if isinstance(dp, int):
            return last - seq if dp % 2 else seq
        return jnp.where(dp % 2 == 1, last - seq, seq)

    def flip(self, values, bit):
        pairs = [(n, n ^ bit) for n in range(self.dp_size)]
        return lax.ppermute(values, "dp", pairs)

    def to_image(self, values):
        images, length, width = values.shape
        size = self.seq_size
        full = jnp.zeros((size, length, width), values.dtype)
        for step in range(size):
            slot = jnp.minimum(self.image_of(self.dp, (self.seq + step) % size), images - 1)
            part = lax.dynamic_slice(values, (slot, 0, 0), (1, length, width))
            if step:
                pairs = []
                for dp in range(self.dp_size):
                    for seq in range(size):
                        target = (seq + step) % size
                        if self.image_of(dp, target) < images:
                            pairs.append((dp * size + seq, dp * size + target))
                part = lax.ppermute(part, ("dp", "seq"), pairs)
            full = lax.dynamic_update_slice(full, part, ((self.seq - step) % size, 0, 0))
        return full.reshape(size * length, width)

    def to_tokens(self, values, images):
        size = self.seq_size
        length = values.shape[0] // size
        width = values.shape[1]
        blocks = values.reshape(size, length, width)
        full = jnp.zeros((size, length, width), values.dtype)
        for step in range(size):
            part = lax.dynamic_slice(
                blocks, ((self.seq + step) % size, 0, 0), (1, length, width)
            )
            if step:
                pairs = []
                for dp in range(self.dp_size):
                    for seq in range(size):
                        if self.image_of(dp, seq) < images:
                            pairs.append((dp * size + seq, dp * size + (seq + step) % size))
                part = lax.ppermute(part, ("dp", "seq"), pairs)
            slot = self.image_of(self.dp, (self.seq - step) % size)
            full = lax.dynamic_update_slice(full, part, (slot, 0, 0))
        return full[:images]

    def gather_pieces(self, piece):
        rows, width = piece.shape
        size = self.seq_size
        half = size // 2
        own = lax.all_gather(piece, "seq", axis=0)
        over_x = self.flip(own, 2)
        over_y = self.flip(own, 4)
        corner_a = self.flip(over_x[:half], 4)
        corner_b = self.flip(over_y[half:], 2)
        full = jnp.zeros((8, size, rows, width), piece.dtype)
        at = self.dp % 8
        for part, mask, start in (
            (own, 0, 0),
            (over_x, 2, 0),
            (over_y, 4, 0),
            (corner_a, 6, 0),
            (corner_b, 6, half),
        ):
            other = self.flip(part, 1)
            full = lax.dynamic_update_slice(full, part[None], (at ^ mask, start, 0, 0))
            full = lax.dynamic_update_slice(full, other[None], (at ^ mask ^ 1, start, 0, 0))
        return full


def pad_blocks(values, axis, blocks, padded):
    shape = values.shape
    size = shape[axis] // blocks
    values = values.reshape(shape[:axis] + (blocks, size) + shape[axis + 1 :])
    pads = [(0, 0)] * values.ndim
    pads[axis + 1] = (0, padded - size)
    values = jnp.pad(values, pads)
    return values.reshape(shape[:axis] + (blocks * padded,) + shape[axis + 1 :])


def cut_blocks(values, axis, blocks, size):
    shape = values.shape
    padded = shape[axis] // blocks
    values = values.reshape(shape[:axis] + (blocks, padded) + shape[axis + 1 :])
    values = lax.slice_in_dim(values, 0, size, axis=axis + 1)
    return values.reshape(shape[:axis] + (blocks * size,) + shape[axis + 1 :])


def sum_images(parts, owner, devices):
    joined = jnp.concatenate(parts, axis=1).astype(BF)
    rank, total = joined.shape
    width = -(-total // (devices * 128)) * 128
    joined = jnp.pad(joined, ((0, 0), (0, devices * width - total)))
    pieces = joined.reshape(rank, devices, width).transpose(1, 0, 2)
    pieces = lax.all_to_all(pieces, ("dp", "seq"), split_axis=0, concat_axis=0, tiled=True)
    sums = dot(owner, pieces.reshape(devices, rank * width), ((0,), (0,))).astype(BF)
    sums = sums.reshape(-1, width)
    full = lax.all_gather(sums, ("dp", "seq"), axis=0)
    full = full.transpose(1, 0, 2).reshape(sums.shape[0], devices * width).astype(F32)
    out = []
    start = 0
    for part in parts:
        out.append(full[:, start : start + part.shape[1]])
        start += part.shape[1]
    return out


def local(
    dp_size,
    seq_size,
    tokens,
    out_grad,
    image_count,
    adapter_id,
    key_live,
    w_qkv,
    w_out,
    w_fc1,
    w_fc2,
    norm_gain,
    norm_bias,
    proj_bias,
    hidden_bias,
    down_attn,
    up_attn,
    down_fc1,
    up_fc1,
    down_fc2,
    up_fc2,
):
    images, local_len, width = tokens.shape
    rows = width // seq_size
    hidden_size = hidden_bias.shape[0]
    columns = down_attn.shape[-1]
    adapters = columns // RANK
    devices = dp_size * seq_size
    place = Place(dp_size, seq_size)
    own_slot = jnp.minimum(place.slot, images - 1)
    is_live = (place.slot < image_count[0]) & (place.slot < images)
    live = is_live.astype(F32)
    adapter = lax.dynamic_index_in_dim(adapter_id, own_slot, keepdims=False)
    key_mask = lax.dynamic_index_in_dim(key_live, own_slot, keepdims=False)
    owner = jnp.where(is_live & (jnp.arange(adapters) == adapter), 1.0, 0.0)
    owner = lax.all_gather(owner.astype(BF)[None], ("dp", "seq"), axis=0, tiled=True)

    part8 = place.dp % 8
    core = part8 % 2
    plane = part8 // 2
    joined = jnp.concatenate([w_qkv, w_out[:, None, :]], axis=1)
    piece = lax.dynamic_slice(joined, (core * (rows // 2), plane, 0), (rows // 2, 1, width))
    attn_full = place.gather_pieces(piece.reshape(rows // 2, width))
    attn_full = attn_full.reshape(4, 2, seq_size, rows // 2, width).transpose(0, 2, 1, 3, 4)
    attn_full = attn_full.reshape(4, width, width)

    shard = hidden_size // seq_size
    padded = -(-shard // 64) * 64
    hidden_pad = padded * seq_size
    fc1 = pad_blocks(w_fc1, 1, seq_size, padded)
    piece = lax.dynamic_slice(
        fc1, (plane * (rows // 4), core * (hidden_pad // 2)), (rows // 4, hidden_pad // 2)
    )
    fc1_full = place.gather_pieces(piece)
    fc1_full = fc1_full.reshape(4, 2, seq_size, rows // 4, hidden_pad // 2)
    fc1_full = fc1_full.transpose(2, 0, 3, 1, 4).reshape(width, hidden_pad)
    fc2 = jnp.pad(w_fc2, ((0, padded - shard), (0, 0)))
    piece = lax.dynamic_slice(fc2, (part8 * (padded // 8), 0), (padded // 8, width))
    fc2_full = place.gather_pieces(piece).transpose(1, 0, 2, 3).reshape(hidden_pad, width)

    def take(values, axis):
        return lax.dynamic_slice_in_dim(values, adapter * RANK, RANK, axis=axis)

    down_a = take(down_attn, 2)
    up_a = take(up_attn, 1)
    down_1 = take(down_fc1, 1)
    up_1 = pad_blocks(take(up_fc1, 0), 1, seq_size, padded)
    down_2 = pad_blocks(take(down_fc2, 1), 0, seq_size, padded)
    up_2 = take(up_fc2, 0)
    bias_1 = pad_blocks(hidden_bias, 0, seq_size, padded)

    flat = place.to_image(tokens).astype(F32)
    top_grad = place.to_image(out_grad).astype(F32) * live
    full_len = flat.shape[0]
    heads = width // HD

    normed = layer_norm(flat, norm_gain[0], norm_bias[0]).astype(BF)
    rank_parts = []
    projected = []
    for index in range(3):
        rank_part = product(normed, down_a[index]).astype(BF)
        rank_parts.append(rank_part)
        projected.append(product(normed, attn_full[index]) + product(rank_part, up_a[index]))
    queries = (projected[0] + proj_bias[0]).astype(BF)
    key_rows = projected[1].astype(BF)
    value_rows = (projected[2] + proj_bias[1]).astype(BF)

    groups = 4

    def split_heads(values):
        values = values.reshape(full_len, groups, heads // groups, HD)
        return values.transpose(1, 0, 2, 3)

    def join_heads(values):
        return values.transpose(1, 0, 2, 3).reshape(full_len, width)

    split_q, split_k, split_v = split_heads(queries), split_heads(key_rows), split_heads(value_rows)
    masks = jnp.broadcast_to(key_mask[None], (groups, full_len))
    attended, log_total = lax.map(attend_heads, (split_q, split_k, split_v, masks))
    merged = join_heads(attended).astype(BF)
    rank_out = product(merged, down_a[3]).astype(BF)
    resid = flat + product(merged, attn_full[3]) + product(rank_out, up_a[3]) + proj_bias[2]
    normed_two = layer_norm(resid, norm_gain[1], norm_bias[1]).astype(BF)
    rank_one = product(normed_two, down_1).astype(BF)
    hidden = product(normed_two, fc1_full) + product(rank_one, up_1) + bias_1
    activated = gelu_tanh(hidden).astype(BF)
    rank_two = product(activated, down_2).astype(BF)
    branch_two = product(activated, fc2_full) + product(rank_two, up_2) + proj_bias[3]
    result = place.to_tokens(((resid + branch_two) * live).astype(BF), images)

    two_grad = top_grad.astype(BF)
    inner_two = product_back(two_grad, up_2).astype(BF)
    up_2_grad = outer_sum(rank_two, two_grad)
    down_2_grad = outer_sum(inner_two, activated)
    act_grad = product_back(two_grad, fc2_full) + product_back(inner_two, down_2)
    hidden_grad = jax.vjp(gelu_tanh, hidden)[1](act_grad)[0].astype(BF)
    inner_one = product_back(hidden_grad, up_1).astype(BF)
    up_1_grad = outer_sum(rank_one, hidden_grad)
    down_1_grad = outer_sum(inner_one, normed_two)
    normed_two_grad = product_back(hidden_grad, fc1_full) + product_back(inner_one, down_1)
    resid_grad = top_grad + norm_back(resid, norm_gain[1], norm_bias[1], normed_two_grad)
    branch_grad = resid_grad.astype(BF)
    inner_o = product_back(branch_grad, up_a[3]).astype(BF)
    up_o_grad = outer_sum(rank_out, branch_grad)
    down_o_grad = outer_sum(inner_o, merged)
    merged_grad = product_back(branch_grad, attn_full[3]) + product_back(inner_o, down_a[3])
    merged_grad = merged_grad.astype(BF)
    early = sum_images(
        [down_2_grad, up_1_grad, up_2_grad, down_1_grad, down_o_grad, up_o_grad], owner, devices
    )

    grad_q, grad_k, grad_v = lax.map(
        attend_back, (split_q, split_k, split_v, masks, log_total, split_heads(merged_grad))
    )
    proj_grads = (join_heads(grad_q), join_heads(grad_k), join_heads(grad_v))
    normed_grad = 0.0
    late_parts = []
    for index in range(3):
        inner = product_back(proj_grads[index], up_a[index]).astype(BF)
        late_parts.append(outer_sum(inner, normed))
        late_parts.append(outer_sum(rank_parts[index], proj_grads[index]))
        normed_grad = (
            normed_grad
            + product_back(proj_grads[index], attn_full[index])
            + product_back(inner, down_a[index])
        )
    late = sum_images(late_parts, owner, devices)
    input_grad = resid_grad + norm_back(flat, norm_gain[0], norm_bias[0], normed_grad)
    input_grad = place.to_tokens(input_grad.astype(BF), images).astype(F32)

    down_2_sum = cut_blocks(early[0], 1, seq_size, shard).T
    up_1_sum = cut_blocks(early[1], 1, seq_size, shard)
    down_attn_sum = jnp.stack([late[0].T, late[2].T, late[4].T, early[4].T])
    up_attn_sum = jnp.stack([late[1], late[3], late[5], early[5]])
    return (
        result,
        input_grad,
        down_attn_sum,
        up_attn_sum,
        early[3].T,
        up_1_sum,
        down_2_sum,
        early[2],
    )


def solution(mesh):
    in_specs = (
        P("dp", "seq", None),
        P("dp", "seq", None),
        P("dp"),
        P("dp"),
        P("dp", None),
        P("seq", None, None),
        P("seq", None),
        P("seq", None),
        P("seq", None),
        P(),
        P(),
        P(),
        P(),
        P(),
        P(),
        P(),
        P(),
        P(),
        P(),
    )
    out_specs = (P("dp", "seq", None), P("dp", "seq", None), P(), P(), P(), P(), P(), P())

    def run(*args):
        return local(mesh.shape["dp"], mesh.shape["seq"], *args)

    return jax.shard_map(run, mesh=mesh, in_specs=in_specs, out_specs=out_specs, check_vma=False)
```

time: 1340 us -> 864 us (0.64)
  the two profiles are of different devices: /device:TPU:0 before, /device:TPU:13 now
where the time goes in v1:
time: 864 us; the launch traced here: 854 us
  matrix products  237 us (27%)
  local copies, waits for them, and re-layouts  202 us (23%)
  waiting for transfers between devices  193 us (22%)
  blocking collectives  86.5 us (10%)
  starting transfers between devices  65.3 us (8%)
  other arithmetic  52.7 us (6%)
  between operations  17.3 us (2%)
    dot_general x50, matrix products, dot(): lax.dot_general(left, right, (dims, ((), ())), preferred_element_type=F32)  149 us
    ppermute x27, waiting for transfers between devices, flip(): return lax.ppermute(values, 'dp', pairs)  66.1 us
    ppermute x6, waiting for transfers between devices, to_tokens(): part = lax.ppermute(part, ('dp', 'seq'), pairs)  64.5 us
    ppermute x6, waiting for transfers between devices, to_image(): part = lax.ppermute(part, ('dp', 'seq'), pairs)  62.2 us
    all_gather x1, blocking collectives, local(): lax.all_gather(owner.astype(BF)[None], ('dp', 'seq'), axis=0, tiled=True)  59.4 us
    ppermute x27, starting transfers between devices, flip(): return lax.ppermute(values, 'dp', pairs)  32.1 us
    unnamed x197, local copies, waits for them, and re-layouts  29.6 us
    all_to_all x1, blocking collectives, sum_images(): lax.all_to_all(pieces, ('dp', 'seq'), split_axis=0, concat_axis=0, tiled=...  27.1 us
  transfers between devices with their start and end apart: 45, of which 13 were waited for; matrix products, arithmetic and copies ran while one was open for 20% of the time, Pallas kernels for 0%

profile of v1, /device:TPU:13, one launch (start us, length us, event | category | flops | bytes accessed | tf_op | source)
XLA Modules:
  0.0 854.2 jit_solution(6321014789204560685)
XLA Ops:
  7.3 6.6 reshape.387
  64.4 47.0 %collective-permute-done.33 = bf16[1,184,1152]{2,1,0:T(8,128)(2,1)} collective-permute-done((bf16[1,184,1152]{2,1,0:T(8,128)(2,1)}, bf16[1,184,1152]{2,1,0:T(8,128)(2,1)}, u32[]{:S(2)}, u32[]{:S(2)}) %collective-permute-start.33) | collective-permute-done | bytes 423968 | tf_op jit(solution)/shard_map/ppermute | solution.py:117
  114.3 15.2 %collective-permute-done.34 = bf16[1,184,1152]{2,1,0:T(8,128)(2,1)} collective-permute-done((bf16[1,184,1152]{2,1,0:T(8,128)(2,1)}, bf16[1,184,1152]{2,1,0:T(8,128)(2,1)}, u32[]{:S(2)}, u32[]{:S(2)}) %collective-permute-start.34) | collective-permute-done | bytes 423968 | tf_op jit(solution)/shard_map/ppermute | solution.py:117
  138.9 6.6 fusion.137
  174.1 12.7 %collective-permute-done.13 = bf16[4,72,2176]{2,1,0:T(8,128)(2,1)S(1)} collective-permute-done((bf16[4,72,2176]{2,1,0:T(8,128)(2,1)}, bf16[4,72,2176]{2,1,0:T(8,128)(2,1)S(1)}, u32[]{:S(2)}, u32[]{:S(2)}) %collective-permute-start.13) | collective-permute-done | bytes 1253408 | tf_op jit(solution)/shard_map/ppermute | solution.py:101
  194.5 19.1 %collective-permute-done.22 = bf16[4,136,1152]{2,1,0:T(8,128)(2,1)} collective-permute-done((bf16[4,136,1152]{2,1,0:T(8,128)(2,1)}, bf16[4,136,1152]{2,1,0:T(8,128)(2,1)}, u32[]{:S(2)}, u32[]{:S(2)}) %collective-permute-start.22) | collective-permute-done | bytes 1253408 | tf_op jit(solution)/shard_map/ppermute | solution.py:101
  220.0 24.2 %collective-permute-done.24 = bf16[4,136,1152]{2,1,0:T(8,128)(2,1)S(1)} collective-permute-done((bf16[4,136,1152]{2,1,0:T(8,128)(2,1)S(1)}, bf16[4,136,1152]{2,1,0:T(8,128)(2,1)S(1)}, u32[]{:S(2)}, u32[]{:S(2)}) %collective-permute-start.24) | collective-permute-done | bytes 1253408 | tf_op jit(solution)/shard_map/ppermute | solution.py:101
  257.4 6.1 collective-permute-start.23
  290.9 11.9 %copy.107 = bf16[4,4,72,2,2176]{4,3,2,1,0:T(2,128)(2,1)} copy(bf16[4,4,72,2,2176]{4,2,0,3,1:T(8,128)(2,1)S(1)} %bitcast.420) | data formatting | bytes 20054016 | tf_op jit(solution)/shard_map/transpose | solution.py:259
  302.8 9.5 %copy.132 = bf16[144,8,2,2176]{3,1,2,0:T(8,128)(2,1)} copy(bf16[144,8,2,2176]{3,2,1,0:T(2,128)(2,1)} %bitcast.419) | data formatting | bytes 20054016
  325.3 7.2 fusion.128
  362.8 38.6 %while.26 = (s32[]{:T(128)}, bf16[4,736,4,72]{1,3,2,0:T(8,128)(2,1)}, f32[4,4,736]{2,1,0:T(4,128)S(1)}, bf16[4,736,4,72]{1,3,2,0:T(8,128)(2,1)}, s32[4,736]{1,0:...) while((s32[]{:T(128)}, ...), condition=%wide.region_5.6_spmd, body=%wide.region_2.5_spmd.sunk | while | flops 650033024 | bytes 28317308 | solution.py:302
  413.5 8.5 fusion.136
  422.8 9.6 %multiply_convert_fusion.1 = (bf16[736,4352]{1,0:T(8,128)(2,1)}, f32[736,4352]{1,0:T(8,128)}) fusion(f32[4352]{0:T(1024)S(1)} %copy-done.84, f32[736,4352]{1,0:T(8,128)S(1)} %fusion.136, bf16[736,16]{0,1:T(8,128)(2,1)S(1)} %convolution_convert_fusion.21, bf16[16,4352]{1,0:T(8,128)(2,1)S(1)} %copy-done.58), kind=kOutput, calls=%fused_computation.72 | convolution fusion | flops 137732096 | bytes 32210944 | tf_op jit(solution)/shard_map/dot_general | solution.py:15
  432.4 23.2 %fusion.64 = bf16[736,4352]{1,0:T(8,128)(2,1)} fusion(f32[736,4352]{1,0:T(8,128)} %get-tuple-element.228, f32[736,4352]{1,0:T(8,128)} %fusion.137, bf16[736,1152]{1,0:T(8,128)(2,1)} %bitcast.463, bf16[4352,1152]{1,0:T(8,128)(2,1)} %bitcast.89), kind=kOutput, calls=%fused_computation.71 | convolution fusion | flops 7447142400 | bytes 43753472 | tf_op jit(solution)/shard_map/dot_general | solution.py:15
  455.6 12.9 %fusion.138 = f32[736,1152]{1,0:T(8,128)S(1)} fusion(bf16[736,4352]{1,0:T(8,128)(2,1)} %fusion.64, bf16[1152,4352]{1,0:T(8,128)(2,1)} %bitcast.434), kind=kOutput, calls=%fused_computation.304 | convolution fusion | flops 7379877888 | bytes 19824640 | tf_op jit(solution)/shard_map/dot_general | solution.py:15
  485.6 71.4 %while.27 = (s32[]{:T(128)}, bf16[4,736,4,72]{1,3,2,0:T(8,128)(2,1)}, bf16[4,736,4,72]{1,3,2,0:T(8,128)(2,1)}, bf16[4,736,4,72]{1,3,2,0:T(8,128)(2,1)}, bf16[4,7...) while((s32[]{:T(128)}, ...), condition=%wide.region_12.13_spmd, body=%wide.region_10.12_spmd.sunk | while | flops 1593643904 | bytes 77247440 | solution.py:335
  589.3 59.4 %all-gather.3 = bf16[32,1,8]{2,1,0:T(2,128)(2,1)S(1)} all-gather(bf16[1,1,8]{2,1,0:T(2,128)(2,1)S(1)} %convert_bitcast_fusion.2), channel_id=1, replica_groups=mesh['dp'=8,'seq'=4] {'dp','seq'}, dimensions={0}, use_global_device_ids=true | all-gather | bytes 528 | tf_op jit(solution)/shard_map/all_gather | solution.py:239
  663.7 27.1 %all_to_all.10 = bf16[32,16,512]{2,1,0:T(8,128)(2,1)S(1)} all-to-all(bf16[32,16,512]{2,1,0:T(8,128)(2,1)S(1)} %bitcast.460), channel_id=1, replica_groups=mesh['dp'=8,'seq'=4] {'dp','seq'}, dimensions={0} | all-to-all | bytes 1048576 | tf_op jit(solution)/shard_map/all_to_all | solution.py:190
  696.2 13.9 %fusion.82 = bf16[736,1152]{1,0:T(8,128)(2,1)S(1)} fusion(f32[736,1152]{1,0:T(8,128)S(1)} %copy-done.9, f32[736,1152]{1,0:T(8,128)S(1)} %fusion.99, bf16[736,4352]{1,0:T(8,128)(2,1)} %get-tuple-element.227, bf16[4352,1152]{1,0:T(8,128)(2,1)} %bitcast.89, f32[]{:T(128)S(6)} %convert_element_type.222, f32[1152]{0:T(1024)S(1)} %copy-done.89), kind=kOutput, calls=%fused_computation.121 | convolution fusion | flops 7384117248 | bytes 24916484 | tf_op jit(solution)/shard_map/dot_general | solution.py:15
  727.4 23.2 %collective-permute-done.31 = bf16[1,184,1152]{2,1,0:T(8,128)(2,1)S(1)} collective-permute-done((bf16[1,184,1152]{2,1,0:T(8,128)(2,1)S(1)}, bf16[1,184,1152]{2,1,0:T(8,128)(2,1)S(1)}, u32[]{:S(2)}, u32[]{:S(2)}) %collective-permute-start.31) | collective-permute-done | bytes 423968 | tf_op jit(solution)/shard_map/ppermute | solution.py:137
  750.7 40.9 %collective-permute-done.32 = bf16[1,184,1152]{2,1,0:T(8,128)(2,1)S(1)} collective-permute-done((bf16[1,184,1152]{2,1,0:T(8,128)(2,1)S(1)}, bf16[1,184,1152]{2,1,0:T(8,128)(2,1)S(1)}, u32[]{:S(2)}, u32[]{:S(2)}) %collective-permute-start.32) | collective-permute-done | bytes 423968 | tf_op jit(solution)/shard_map/ppermute | solution.py:137
  808.1 6.6 convert_bitcast_fusion
  814.7 9.0 %copy.123 = f32[128,32,512]{0,2,1:T(8,128)} copy(f32[128,32,512]{2,0,1:T(8,128)} %convert_bitcast_fusion) | data formatting | bytes 16777216 | tf_op jit(solution)/shard_map/convert_element_type | solution.py:194
  (528 shorter events, 435.7 us)
Async XLA Ops:
  7.2 143.9 %all-gather.16.cloned.1.call-start = ((), (), s32[]{:S(2)}) async-start(), calls=%async_computation.5 | async-start | bytes 1566720 | tf_op jit(solution)/shard_map/all_gather | solution.py:146
  25.8 133.1 %all-gather.18.cloned.1.call-start = ((), (), s32[]{:S(2)}) async-start(), calls=%async_computation.6 | async-start | bytes 1566720 | tf_op jit(solution)/shard_map/all_gather | solution.py:146
  27.6 141.2 %all-gather.14.cloned.1.call-start = ((), (), s32[]{:S(2)}) async-start(), calls=%async_computation.4 | async-start | bytes 1658880 | tf_op jit(solution)/shard_map/all_gather | solution.py:146
  33.8 79.4 %collective-permute-start.1 = (bf16[1,184,1152]{2,1,0:T(8,128)(2,1)}, bf16[1,184,1152]{2,1,0:T(8,128)(2,1)}, u32[]{:S(2)}, u32[]{:S(2)}) collective-permute-start(bf16[1,184,1152]{2,1,0:T(8,128)(2,1)} %get-tuple-element.220), channel_id=1, source_target_pairs={{0,2},{2,0},{3,1},{4,6},{5,7},{7,5},{8,10},{10,8},{11,9},{12,14},{... | collective-permute-start | bytes 1271816 | tf_op jit(solution)/shard_map/ppermute | solution.py:117
  38.7 72.7 %collective-permute-start.33 = (bf16[1,184,1152]{2,1,0:T(8,128)(2,1)}, bf16[1,184,1152]{2,1,0:T(8,128)(2,1)}, u32[]{:S(2)}, u32[]{:S(2)}) collective-permute-start(bf16[1,184,1152]{2,1,0:T(8,128)(2,1)} %get-tuple-element.214), channel_id=1, source_target_pairs={{0,1},{1,2},{3,0},{4,5},{5,6},{6,7},{8,9},{9,10},{11,8},{12,13},{1... | collective-permute-start | bytes 1271816 | tf_op jit(solution)/shard_map/ppermute | solution.py:117
  40.9 88.5 %collective-permute-start.34 = (bf16[1,184,1152]{2,1,0:T(8,128)(2,1)}, bf16[1,184,1152]{2,1,0:T(8,128)(2,1)}, u32[]{:S(2)}, u32[]{:S(2)}) collective-permute-start(bf16[1,184,1152]{2,1,0:T(8,128)(2,1)} %get-tuple-element.216), channel_id=1, source_target_pairs={{0,2},{2,0},{3,1},{4,6},{5,7},{7,5},{8,10},{10,8},{11,9},{12,14},{... | collective-permute-start | bytes 1271816 | tf_op jit(solution)/shard_map/ppermute | solution.py:117
  43.9 87.3 %collective-permute-start.2 = (bf16[1,184,1152]{2,1,0:T(8,128)(2,1)}, bf16[1,184,1152]{2,1,0:T(8,128)(2,1)}, u32[]{:S(2)}, u32[]{:S(2)}) collective-permute-start(bf16[1,184,1152]{2,1,0:T(8,128)(2,1)} %get-tuple-element.217), channel_id=1, source_target_pairs={{1,0},{2,1},{3,2},{4,7},{6,5},{7,6},{9,8},{10,9},{11,10},{12,15},{... | collective-permute-start | bytes 1271816 | tf_op jit(solution)/shard_map/ppermute | solution.py:117
  61.9 69.3 %collective-permute-start.35 = (bf16[1,184,1152]{2,1,0:T(8,128)(2,1)}, bf16[1,184,1152]{2,1,0:T(8,128)(2,1)S(1)}, u32[]{:S(2)}, u32[]{:S(2)}) collective-permute-start(bf16[1,184,1152]{2,1,0:T(8,128)(2,1)} %get-tuple-element.213), channel_id=1, source_target_pairs={{1,0},{2,1},{3,2},{4,7},{6,5},{7,6},{9,8},{10,9},{11,10},{12,15},{... | collective-permute-start | bytes 1271816 | tf_op jit(solution)/shard_map/ppermute | solution.py:117
  159.5 54.2 %collective-permute-start.22 = (bf16[4,136,1152]{2,1,0:T(8,128)(2,1)}, bf16[4,136,1152]{2,1,0:T(8,128)(2,1)}, u32[]{:S(2)}, u32[]{:S(2)}) collective-permute-start(bf16[4,136,1152]{2,1,0:T(8,128)(2,1)} %bitcast.469), channel_id=1, source_target_pairs={{0,8},{4,12},{8,0},{12,4},{16,24},{20,28},{24,16},{28,20},{1,9},{5... | collective-permute-start | bytes 3760136 | tf_op jit(solution)/shard_map/ppermute | solution.py:101
  171.3 76.9 %collective-permute-start.3 = (bf16[4,144,1152]{2,1,0:T(8,128)(2,1)}, bf16[4,144,1152]{2,1,0:T(8,128)(2,1)S(1)}, u32[]{:S(2)}, u32[]{:S(2)}) collective-permute-start(bf16[4,144,1152]{2,1,0:T(8,128)(2,1)} %bitcast.465), channel_id=1, source_target_pairs={{0,4},{4,0},{8,12},{12,8},{16,20},{20,16},{24,28},{28,24},{1,5},{5... | collective-permute-start | bytes 3981320 | tf_op jit(solution)/shard_map/ppermute | solution.py:101
  186.8 57.6 %collective-permute-start.4 = (bf16[4,144,1152]{2,1,0:T(8,128)(2,1)S(1)}, bf16[4,144,1152]{2,1,0:T(8,128)(2,1)}, u32[]{:S(2)}, u32[]{:S(2)}) collective-permute-start(bf16[4,144,1152]{2,1,0:T(8,128)(2,1)S(1)} %bitcast.466), channel_id=1, source_target_pairs={{0,8},{4,12},{8,0},{12,4},{16,24},{20,28},{24,16},{28,20},{1,9},{5... | collective-permute-start | bytes 3981320 | tf_op jit(solution)/shard_map/ppermute | solution.py:101
  188.1 58.8 %collective-permute-start.6 = (bf16[4,144,1152]{2,1,0:T(8,128)(2,1)S(1)}, bf16[4,144,1152]{2,1,0:T(8,128)(2,1)S(1)}, u32[]{:S(2)}, u32[]{:S(2)}) collective-permute-start(bf16[4,144,1152]{2,1,0:T(8,128)(2,1)S(1)} %bitcast.467), channel_id=1, source_target_pairs={{0,16},{4,20},{8,24},{12,28},{16,0},{20,4},{24,8},{28,12},{1,17},{... | collective-permute-start | bytes 3981320 | tf_op jit(solution)/shard_map/ppermute | solution.py:101
  190.9 53.3 %collective-permute-start.24 = (bf16[4,136,1152]{2,1,0:T(8,128)(2,1)S(1)}, bf16[4,136,1152]{2,1,0:T(8,128)(2,1)S(1)}, u32[]{:S(2)}, u32[]{:S(2)}) collective-permute-start(bf16[4,136,1152]{2,1,0:T(8,128)(2,1)S(1)} %bitcast.471), channel_id=1, source_target_pairs={{0,16},{4,20},{8,24},{12,28},{16,0},{20,4},{24,8},{28,12},{1,17},{... | collective-permute-start | bytes 3760136 | tf_op jit(solution)/shard_map/ppermute | solution.py:101
  213.7 36.6 %collective-permute-start.14 = (bf16[4,72,2176]{2,1,0:T(8,128)(2,1)S(1)}, bf16[4,72,2176]{2,1,0:T(8,128)(2,1)S(1)}, u32[]{:S(2)}, u32[]{:S(2)}) collective-permute-start(bf16[4,72,2176]{2,1,0:T(8,128)(2,1)S(1)} %copy-done.34), channel_id=1, source_target_pairs={{0,4},{4,0},{8,12},{12,8},{16,20},{20,16},{24,28},{28,24},{1,5},{5... | collective-permute-start | bytes 3760136 | tf_op jit(solution)/shard_map/ppermute | solution.py:101
  271.4 40.9 %collective-permute-start.5 = (bf16[4,144,1152]{2,1,0:T(8,128)(2,1)}, bf16[4,144,1152]{2,1,0:T(8,128)(2,1)}, u32[]{:S(2)}, u32[]{:S(2)}) collective-permute-start(bf16[4,144,1152]{2,1,0:T(8,128)(2,1)} %collective-permute-done.4), channel_id=1, source_target_pairs={{0,4},{4,0},{8,12},{12,8},{16,20},{20,16},{24,28},{28,24},{1,5},{5... | collective-permute-start | bytes 3981320 | tf_op jit(solution)/shard_map/ppermute | solution.py:101
  288.8 34.5 %collective-permute-start.11 = (bf16[2,144,1152]{2,1,0:T(8,128)(2,1)}, bf16[2,144,1152]{2,1,0:T(8,128)(2,1)}, u32[]{:S(2)}, u32[]{:S(2)}) collective-permute-start(bf16[2,144,1152]{2,1,0:T(8,128)(2,1)} %collective-permute-done.10), channel_id=1, source_target_pairs={{0,4},{4,0},{8,12},{12,8},{16,20},{20,16},{24,28},{28,24},{1,5},{5... | collective-permute-start | bytes 1990664 | tf_op jit(solution)/shard_map/ppermute | solution.py:101
  584.5 64.3 %all-to-all-start = ((bf16[32,16,256]{2,1,0:T(8,128)(2,1)}), bf16[32,16,256]{2,1,0:T(8,128)(2,1)}, u32[]{:S(2)}, u32[]{:S(2)}) async-start(bf16[32,16,256]{2,1,0:T(8,128)(2,1)} %bitcast.477), calls=%async_computation | async-start | bytes 524288 | tf_op jit(solution)/shard_map/all_to_all | solution.py:190
  588.6 206.0 %all-gather.10.cloned.1.call-start = ((), (), s32[]{:S(2)}) async-start(), calls=%async_computation.2 | async-start | bytes 2162688 | tf_op jit(solution)/shard_map/all_gather | solution.py:193
  650.7 157.4 %all-gather.12.cloned.1.call-start = ((), (), s32[]{:S(2)}) async-start(), calls=%async_computation.3 | async-start | bytes 4325376 | tf_op jit(solution)/shard_map/all_gather | solution.py:193
  713.2 37.4 %collective-permute-start.31 = (bf16[1,184,1152]{2,1,0:T(8,128)(2,1)S(1)}, bf16[1,184,1152]{2,1,0:T(8,128)(2,1)S(1)}, u32[]{:S(2)}, u32[]{:S(2)}) collective-permute-start(bf16[1,184,1152]{2,1,0:T(8,128)(2,1)S(1)} %get-tuple-element.210), channel_id=1, source_target_pairs={{0,2},{1,3},{2,0},{5,7},{6,4},{7,5},{8,10},{9,11},{10,8},{13,15},{... | collective-permute-start | bytes 1271816 | tf_op jit(solution)/shard_map/ppermute | solution.py:137
  719.1 73.7 %collective-permute-start.36 = (bf16[1,184,1152]{2,1,0:T(8,128)(2,1)S(1)}, bf16[1,184,1152]{2,1,0:T(8,128)(2,1)S(1)}, u32[]{:S(2)}, u32[]{:S(2)}) collective-permute-start(bf16[1,184,1152]{2,1,0:T(8,128)(2,1)S(1)} %get-tuple-element.205), channel_id=1, source_target_pairs={{0,1},{1,2},{2,3},{5,6},{6,7},{7,4},{8,9},{9,10},{10,11},{13,14},{... | collective-permute-start | bytes 1271816 | tf_op jit(solution)/shard_map/ppermute | solution.py:137
  720.4 72.4 %collective-permute-start.37 = (bf16[1,184,1152]{2,1,0:T(8,128)(2,1)S(1)}, bf16[1,184,1152]{2,1,0:T(8,128)(2,1)S(1)}, u32[]{:S(2)}, u32[]{:S(2)}) collective-permute-start(bf16[1,184,1152]{2,1,0:T(8,128)(2,1)S(1)} %get-tuple-element.204), channel_id=1, source_target_pairs={{0,2},{1,3},{2,0},{5,7},{6,4},{7,5},{8,10},{9,11},{10,8},{13,15},{... | collective-permute-start | bytes 1271816 | tf_op jit(solution)/shard_map/ppermute | solution.py:137
  722.9 69.9 %collective-permute-start.38 = (bf16[1,184,1152]{2,1,0:T(8,128)(2,1)S(1)}, bf16[1,184,1152]{2,1,0:T(8,128)(2,1)S(1)}, u32[]{:S(2)}, u32[]{:S(2)}) collective-permute-start(bf16[1,184,1152]{2,1,0:T(8,128)(2,1)S(1)} %get-tuple-element.203), channel_id=1, source_target_pairs={{0,3},{1,0},{2,1},{5,4},{6,5},{7,6},{8,11},{9,8},{10,9},{13,12},{1... | collective-permute-start | bytes 1271816 | tf_op jit(solution)/shard_map/ppermute | solution.py:137
  725.2 66.3 %collective-permute-start.32 = (bf16[1,184,1152]{2,1,0:T(8,128)(2,1)S(1)}, bf16[1,184,1152]{2,1,0:T(8,128)(2,1)S(1)}, u32[]{:S(2)}, u32[]{:S(2)}) collective-permute-start(bf16[1,184,1152]{2,1,0:T(8,128)(2,1)S(1)} %get-tuple-element.209), channel_id=1, source_target_pairs={{0,3},{1,0},{2,1},{5,4},{6,5},{7,6},{8,11},{9,8},{10,9},{13,12},{1... | collective-permute-start | bytes 1271816 | tf_op jit(solution)/shard_map/ppermute | solution.py:137
  (121 other events, 2261.1 us)
Sparse Core Ops, SparseCore 0:
  25.9 60.4 all-gather.15
  88.0 40.4 all-gather.17
  130.1 33.6 all-gather.13
  650.8 61.0 all-gather.9
  715.4 75.9 all-gather.11

commit v2 on v1

--- a/solution.py
+++ b/solution.py
@@ -1,6 +1,8 @@
 import jax
 import jax.numpy as jnp
 from jax import lax
+from jax.experimental import pallas as pl
+from jax.experimental.pallas import tpu as pltpu
 from jax.sharding import PartitionSpec as P
 
 HD = 72
@@ -139,28 +141,46 @@
             full = lax.dynamic_update_slice(full, part, (slot, 0, 0))
         return full[:images]
 
-    def gather_pieces(self, piece):
-        rows, width = piece.shape
-        size = self.seq_size
-        half = size // 2
-        own = lax.all_gather(piece, "seq", axis=0)
+    def gather_own(self, piece):
+        return lax.all_gather(piece, "seq", axis=0)
+
+    def gather_rest(self, own, shape, index):
+        half = self.seq_size // 2
         over_x = self.flip(own, 2)
         over_y = self.flip(own, 4)
         corner_a = self.flip(over_x[:half], 4)
         corner_b = self.flip(over_y[half:], 2)
-        full = jnp.zeros((8, size, rows, width), piece.dtype)
-        at = self.dp % 8
-        for part, mask, start in (
-            (own, 0, 0),
-            (over_x, 2, 0),
-            (over_y, 4, 0),
-            (corner_a, 6, 0),
-            (corner_b, 6, half),
-        ):
-            other = self.flip(part, 1)
-            full = lax.dynamic_update_slice(full, part[None], (at ^ mask, start, 0, 0))
-            full = lax.dynamic_update_slice(full, other[None], (at ^ mask ^ 1, start, 0, 0))
-        return full
+        parts = [own, over_x, over_y, corner_a, corner_b]
+        masks = [0, 2, 4, 6, 6]
+        starts = [0, 0, 0, 0, half]
+        others = [self.flip(part, 1) for part in parts]
+        at = (self.dp % 8).astype(jnp.int32).reshape(1)
+
+        def body(at_ref, *refs):
+            out_ref, sems = refs[-2], refs[-1]
+            copies = []
+            for n in range(10):
+                part = at_ref[0] ^ (masks[n % 5] ^ (n // 5))
+                rows = pl.ds(starts[n % 5], parts[n % 5].shape[0])
+                target = out_ref.at[index(part, rows)]
+                copies.append(pltpu.make_async_copy(refs[n], target, sems.at[n]))
+            for copy in copies:
+                copy.start()
+            for copy in copies:
+                copy.wait()
+
+        return pl.pallas_call(
+            body,
+            grid_spec=pltpu.PrefetchScalarGridSpec(
+                num_scalar_prefetch=1,
+                grid=(),
+                in_specs=[pl.BlockSpec(memory_space=pl.ANY)] * 10,
+                out_specs=pl.BlockSpec(memory_space=pl.ANY),
+                scratch_shapes=[pltpu.SemaphoreType.DMA((10,))],
+            ),
+            out_shape=jax.ShapeDtypeStruct(shape, own.dtype),
+            name="assemble",
+        )(at, *parts, *others)
 
 
 def pad_blocks(values, axis, blocks, padded):
@@ -181,23 +201,63 @@
     return values.reshape(shape[:axis] + (blocks * size,) + shape[axis + 1 :])
 
 
-def sum_images(parts, owner, devices):
-    joined = jnp.concatenate(parts, axis=1).astype(BF)
+def tiles_of(size):
+    return -(-size // 128)
+
+
+def exchange(parts, owner, devices):
+    padded = [jnp.pad(part, ((0, 0), (0, -part.shape[1] % 128))) for part in parts]
+    joined = jnp.concatenate(padded, axis=1).astype(BF)
     rank, total = joined.shape
     width = -(-total // (devices * 128)) * 128
     joined = jnp.pad(joined, ((0, 0), (0, devices * width - total)))
     pieces = joined.reshape(rank, devices, width).transpose(1, 0, 2)
     pieces = lax.all_to_all(pieces, ("dp", "seq"), split_axis=0, concat_axis=0, tiled=True)
     sums = dot(owner, pieces.reshape(devices, rank * width), ((0,), (0,))).astype(BF)
-    sums = sums.reshape(-1, width)
-    full = lax.all_gather(sums, ("dp", "seq"), axis=0)
-    full = full.transpose(1, 0, 2).reshape(sums.shape[0], devices * width).astype(F32)
-    out = []
-    start = 0
-    for part in parts:
-        out.append(full[:, start : start + part.shape[1]])
-        start += part.shape[1]
-    return out
+    return sums.reshape(-1, width)
+
+
+def write_grads(early, late, width, hidden_size):
+    columns = early.shape[1]
+
+    def body(early_ref, late_ref, down_a, up_a, down_1, up_1, down_2, up_2):
+        def spread(ref, start, target, size, turned):
+            per = ref.shape[2] // 128
+            for n in range(tiles_of(size)):
+                device, tile = divmod(start + n, per)
+                count = min(128, size - n * 128)
+                block = ref[device, :, tile * 128 : (tile + 1) * 128].astype(F32)
+                if turned:
+                    block = jnp.transpose(block)
+                    target[n * 128 : n * 128 + count, :] = block[:count, :]
+                else:
+                    target[:, n * 128 : n * 128 + count] = block[:, :count]
+            return start + tiles_of(size)
+
+        at = spread(early_ref, 0, down_2, hidden_size, True)
+        at = spread(early_ref, at, up_1, hidden_size, False)
+        at = spread(early_ref, at, up_2, width, False)
+        at = spread(early_ref, at, down_1, width, True)
+        at = spread(early_ref, at, down_a.at[3], width, True)
+        spread(early_ref, at, up_a.at[3], width, False)
+        at = 0
+        for index in range(3):
+            at = spread(late_ref, at, down_a.at[index], width, True)
+            at = spread(late_ref, at, up_a.at[index], width, False)
+
+    shapes = (
+        (4, width, columns),
+        (4, columns, width),
+        (width, columns),
+        (columns, hidden_size),
+        (hidden_size, columns),
+        (columns, width),
+    )
+    return pl.pallas_call(
+        body,
+        out_shape=[jax.ShapeDtypeStruct(shape, F32) for shape in shapes],
+        name="write_grads",
+    )(early, late)
 
 
 def local(
@@ -238,28 +298,48 @@
     owner = jnp.where(is_live & (jnp.arange(adapters) == adapter), 1.0, 0.0)
     owner = lax.all_gather(owner.astype(BF)[None], ("dp", "seq"), axis=0, tiled=True)
 
+    flat = place.to_image(tokens).astype(F32)
+
     part8 = place.dp % 8
     core = part8 % 2
     plane = part8 // 2
-    joined = jnp.concatenate([w_qkv, w_out[:, None, :]], axis=1)
-    piece = lax.dynamic_slice(joined, (core * (rows // 2), plane, 0), (rows // 2, 1, width))
-    attn_full = place.gather_pieces(piece.reshape(rows // 2, width))
-    attn_full = attn_full.reshape(4, 2, seq_size, rows // 2, width).transpose(0, 2, 1, 3, 4)
-    attn_full = attn_full.reshape(4, width, width)
-
+    half = rows // 2
+    quarter = rows // 4
+    piece = jnp.concatenate(
+        [
+            lax.dynamic_slice(w_qkv, (core * half, 0, 0), (half, 3, width)),
+            lax.dynamic_slice(w_out, (core * half, 0), (half, width))[:, None, :],
+        ],
+        axis=1,
+    )
+    piece = lax.dynamic_slice(piece, (0, plane, 0), (half, 1, width)).reshape(half, width)
+    attn_own = place.gather_own(piece)
     shard = hidden_size // seq_size
     padded = -(-shard // 64) * 64
     hidden_pad = padded * seq_size
-    fc1 = pad_blocks(w_fc1, 1, seq_size, padded)
-    piece = lax.dynamic_slice(
-        fc1, (plane * (rows // 4), core * (hidden_pad // 2)), (rows // 4, hidden_pad // 2)
-    )
-    fc1_full = place.gather_pieces(piece)
-    fc1_full = fc1_full.reshape(4, 2, seq_size, rows // 4, hidden_pad // 2)
-    fc1_full = fc1_full.transpose(2, 0, 3, 1, 4).reshape(width, hidden_pad)
+    piece = lax.dynamic_slice(w_fc1, (plane * quarter, 0), (quarter, hidden_size))
+    piece = pad_blocks(piece, 1, seq_size, padded)
+    piece = lax.dynamic_slice(piece, (0, core * (hidden_pad // 2)), (quarter, hidden_pad // 2))
+    attn_own, piece = lax.optimization_barrier((attn_own, piece))
+    fc1_own = place.gather_own(piece)
     fc2 = jnp.pad(w_fc2, ((0, padded - shard), (0, 0)))
     piece = lax.dynamic_slice(fc2, (part8 * (padded // 8), 0), (padded // 8, width))
-    fc2_full = place.gather_pieces(piece).transpose(1, 0, 2, 3).reshape(hidden_pad, width)
+    fc1_own, piece = lax.optimization_barrier((fc1_own, piece))
+    fc2_own = place.gather_own(piece)
+
+    attn_full = place.gather_rest(
+        attn_own,
+        (4, seq_size, 2, half, width),
+        lambda part, at: (part // 2, at, part % 2),
+    ).reshape(4, width, width)
+    fc1_full = place.gather_rest(
+        fc1_own,
+        (2, seq_size, 4, quarter, hidden_pad // 2),
+        lambda part, at: (part % 2, at, part // 2),
+    ).reshape(2, width, hidden_pad // 2)
+    fc2_full = place.gather_rest(
+        fc2_own, (seq_size, 8, padded // 8, width), lambda part, at: (at, part)
+    ).reshape(2, hidden_pad // 2, width)
 
     def take(values, axis):
         return lax.dynamic_slice_in_dim(values, adapter * RANK, RANK, axis=axis)
@@ -272,12 +352,13 @@
     up_2 = take(up_fc2, 0)
     bias_1 = pad_blocks(hidden_bias, 0, seq_size, padded)
 
-    flat = place.to_image(tokens).astype(F32)
-    top_grad = place.to_image(out_grad).astype(F32) * live
     full_len = flat.shape[0]
     heads = width // HD
 
+    flat, owner = lax.optimization_barrier((flat, owner))
     normed = layer_norm(flat, norm_gain[0], norm_bias[0]).astype(BF)
+    normed, out_grad = lax.optimization_barrier((normed, out_grad))
+    top_grad = place.to_image(out_grad).astype(F32) * live
     rank_parts = []
     projected = []
     for index in range(3):
@@ -305,22 +386,36 @@
     resid = flat + product(merged, attn_full[3]) + product(rank_out, up_a[3]) + proj_bias[2]
     normed_two = layer_norm(resid, norm_gain[1], norm_bias[1]).astype(BF)
     rank_one = product(normed_two, down_1).astype(BF)
-    hidden = product(normed_two, fc1_full) + product(rank_one, up_1) + bias_1
-    activated = gelu_tanh(hidden).astype(BF)
-    rank_two = product(activated, down_2).astype(BF)
-    branch_two = product(activated, fc2_full) + product(rank_two, up_2) + proj_bias[3]
-    result = place.to_tokens(((resid + branch_two) * live).astype(BF), images)
-
     two_grad = top_grad.astype(BF)
     inner_two = product_back(two_grad, up_2).astype(BF)
+    branch_two = proj_bias[3]
+    rank_two = 0.0
+    inner_one = 0.0
+    normed_two_grad = 0.0
+    down_2_halves = []
+    up_1_halves = []
+    side = hidden_pad // 2
+    for index in range(2):
+        at = slice(index * side, (index + 1) * side)
+        hidden = product(normed_two, fc1_full[index]) + product(rank_one, up_1[:, at]) + bias_1[at]
+        activated = gelu_tanh(hidden).astype(BF)
+        rank_two = rank_two + product(activated, down_2[at])
+        branch_two = branch_two + product(activated, fc2_full[index])
+        down_2_halves.append(outer_sum(inner_two, activated))
+        act_grad = product_back(two_grad, fc2_full[index]) + product_back(inner_two, down_2[at])
+        hidden_grad = jax.vjp(gelu_tanh, hidden)[1](act_grad)[0].astype(BF)
+        inner_one = inner_one + product_back(hidden_grad, up_1[:, at])
+        up_1_halves.append(outer_sum(rank_one, hidden_grad))
+        normed_two_grad = normed_two_grad + product_back(hidden_grad, fc1_full[index])
+    rank_two = rank_two.astype(BF)
+    branch_two = branch_two + product(rank_two, up_2)
+    result = ((resid + branch_two) * live).astype(BF)
     up_2_grad = outer_sum(rank_two, two_grad)
-    down_2_grad = outer_sum(inner_two, activated)
-    act_grad = product_back(two_grad, fc2_full) + product_back(inner_two, down_2)
-    hidden_grad = jax.vjp(gelu_tanh, hidden)[1](act_grad)[0].astype(BF)
-    inner_one = product_back(hidden_grad, up_1).astype(BF)
-    up_1_grad = outer_sum(rank_one, hidden_grad)
+    down_2_grad = cut_blocks(jnp.concatenate(down_2_halves, axis=1), 1, seq_size, shard)
+    inner_one = inner_one.astype(BF)
+    up_1_grad = cut_blocks(jnp.concatenate(up_1_halves, axis=1), 1, seq_size, shard)
     down_1_grad = outer_sum(inner_one, normed_two)
-    normed_two_grad = product_back(hidden_grad, fc1_full) + product_back(inner_one, down_1)
+    normed_two_grad = normed_two_grad + product_back(inner_one, down_1)
     resid_grad = top_grad + norm_back(resid, norm_gain[1], norm_bias[1], normed_two_grad)
     branch_grad = resid_grad.astype(BF)
     inner_o = product_back(branch_grad, up_a[3]).astype(BF)
@@ -328,9 +423,12 @@
     down_o_grad = outer_sum(inner_o, merged)
     merged_grad = product_back(branch_grad, attn_full[3]) + product_back(inner_o, down_a[3])
     merged_grad = merged_grad.astype(BF)
-    early = sum_images(
+    early = exchange(
         [down_2_grad, up_1_grad, up_2_grad, down_1_grad, down_o_grad, up_o_grad], owner, devices
     )
+    early, merged_grad, result = lax.optimization_barrier((early, merged_grad, result))
+    early = lax.all_gather(early, ("dp", "seq"), axis=0)
+    result = place.to_tokens(result, images)
 
     grad_q, grad_k, grad_v = lax.map(
         attend_back, (split_q, split_k, split_v, masks, log_total, split_heads(merged_grad))
@@ -347,24 +445,11 @@
             + product_back(proj_grads[index], attn_full[index])
             + product_back(inner, down_a[index])
         )
-    late = sum_images(late_parts, owner, devices)
+    late = exchange(late_parts, owner, devices)
+    late = lax.all_gather(late, ("dp", "seq"), axis=0)
     input_grad = resid_grad + norm_back(flat, norm_gain[0], norm_bias[0], normed_grad)
     input_grad = place.to_tokens(input_grad.astype(BF), images).astype(F32)
-
-    down_2_sum = cut_blocks(early[0], 1, seq_size, shard).T
-    up_1_sum = cut_blocks(early[1], 1, seq_size, shard)
-    down_attn_sum = jnp.stack([late[0].T, late[2].T, late[4].T, early[4].T])
-    up_attn_sum = jnp.stack([late[1], late[3], late[5], early[5]])
-    return (
-        result,
-        input_grad,
-        down_attn_sum,
-        up_attn_sum,
-        early[3].T,
-        up_1_sum,
-        down_2_sum,
-        early[2],
-    )
+    return (result, input_grad, *write_grads(early, late, width, hidden_size))
 
 
 def solution(mesh):

time: 864 us -> 1710 us (1.98)
  the two profiles are of different devices: /device:TPU:13 before, /device:TPU:0 now
where the time goes in v2:
time: 1710 us
  Pallas kernels  940 us (55%)
  matrix products  269 us (16%)
  waiting for transfers between devices  156 us (9%)
  blocking collectives  118 us (7%)
  local copies, waits for them, and re-layouts  109 us (6%)
  starting transfers between devices  48 us (3%)
  other arithmetic  40.1 us (2%)
  between operations  17.2 us (1%)
    pallas_call x3, Pallas kernels, gather_rest(): pl.pallas_call(body, grid_spec=pltpu.PrefetchScalarGridSpec(num_scalar_pr...  933 us
    dot_general x60, matrix products, dot(): lax.dot_general(left, right, (dims, ((), ())), preferred_element_type=F32)  181 us
    all_gather x1, blocking collectives, local(): lax.all_gather(owner.astype(BF)[None], ('dp', 'seq'), axis=0, tiled=True)  102 us
    all_gather x1, waiting for transfers between devices, local(): early = lax.all_gather(early, ('dp', 'seq'), axis=0)  61.9 us
    ppermute x27, waiting for transfers between devices, flip(): return lax.ppermute(values, 'dp', pairs)  51.3 us
  transfers between devices with their start and end apart: 45, of which 10 were waited for; matrix products, arithmetic and copies ran while one was open for 14% of the time, Pallas kernels for 37%

profile of v2, /device:TPU:0, one launch (start us, length us, event | category | flops | bytes accessed | tf_op | source)
XLA Modules:
  0.0 1705.7 jit_solution(10280843521055125725)
XLA Ops:
  27.5 101.8 %all-gather.4 = bf16[32,1,8]{2,1,0:T(2,128)(2,1)S(1)} all-gather(bf16[1,1,8]{2,1,0:T(2,128)(2,1)S(1)} %convert_bitcast_fusion), channel_id=1, replica_groups=mesh['dp'=8,'seq'=4] {'dp','seq'}, dimensions={0}, use_global_device_ids=true | all-gather | bytes 528 | tf_op jit(solution)/shard_map/all_gather | solution.py:299
  172.9 9.5 collective-permute-done.4
  189.5 11.5 collective-permute-done.6.refs_1_
  207.1 12.2 collective-permute-done.8.refs_3_
  230.0 322.8 %assemble.3 = bf16[4,4,2,144,1152]{4,3,2,1,0:T(8,128)(2,1)} custom-call(s32[1]{0:T(128)} %bitcast.23.at_ref, bf16[4,144,1152]{2,1,0:T(8,128)(2,1)} %bitcast.25.refs_0_, bf16[4,144,1152]{2,1,0:T(8,128)(2,1)} %collective-permute-done.6.refs_1_, bf16[4,144,1152]{2,1,0:T(8,128)(2,1)} %collective-permute-done.7.refs_2_, ...), custom_call_target="tpu_custom_call" | custom-call | tf_op jit(solution)/shard_map/assemble/pallas_call | solution.py:172
  552.9 7.5 fusion.152
  591.2 49.4 %while.26 = (s32[]{:T(128)}, bf16[4,736,4,72]{1,3,2,0:T(8,128)(2,1)}, f32[4,4,736]{2,1,0:T(4,128)}, bf16[4,736,4,72]{1,3,2,0:T(8,128)(2,1)}, s32[4,736]{1,0:T(4,...) while((s32[]{:T(128)}, bf16[4,736,4,72]{1,3,2,0:T(8,128)(2,1)}, ...), condition=%wide.region_5.6_spmd, body=%wide.region_2.5_spmd.sunk | while | flops 650033024 | bytes 28316504 | solution.py:383
  655.9 11.6 collective-permute-done.17.refs_3_
  679.8 305.0 %assemble.4 = bf16[2,4,4,72,2176]{4,3,2,1,0:T(8,128)(2,1)} custom-call(s32[1]{0:T(128)} %bitcast.23.at_ref, bf16[4,72,2176]{2,1,0:T(8,128)(2,1)} %bitcast.359, bf16[4,72,2176]{2,1,0:T(8,128)(2,1)} %collective-permute-done.15.refs_1_, bf16[4,72,2176]{2,1,0:T(8,128)(2,1)} %collective-permute-done.16.refs_2_, ...), custom_call_target="tpu_custom_call" | custom-call | tf_op jit(solution)/shard_map/assemble/pallas_call | solution.py:172
  984.7 8.6 fusion.154
  993.4 10.5 multiply_convert_fusion.2
  1017.4 11.7 collective-permute-done.26.refs_3_
  1036.2 304.9 %assemble.5 = bf16[4,8,136,1152]{3,2,1,0:T(8,128)(2,1)} custom-call(s32[1]{0:T(128)} %bitcast.23.at_ref, bf16[4,136,1152]{2,1,0:T(8,128)(2,1)} %bitcast.355, bf16[4,136,1152]{2,1,0:T(8,128)(2,1)} %copy-done.33, bf16[4,136,1152]{2,1,0:T(8,128)(2,1)} %collective-permute-done.25.refs_2_, bf16[2,136,1152]{2,1,0:T(8,128)(2,1)} %collective-permute-done.26.refs_3_, ...), custom_call_target="tpu_custom_call" | custom-call | tf_op jit(solution)/shard_map/assemble/pallas_call | solution.py:172
  1341.1 8.5 fusion.153
  1349.7 12.1 fusion.64
  1364.6 8.9 fusion.160
  1373.5 11.5 fusion.71
  1392.7 7.5 multiply_reduce_fusion.2
  1423.7 11.3 fusion.86
  1446.1 76.6 %while.27 = (s32[]{:T(128)}, bf16[4,736,4,72]{1,3,2,0:T(8,128)(2,1)}, bf16[4,736,4,72]{1,3,2,0:T(8,128)(2,1)}, bf16[4,736,4,72]{1,3,2,0:T(8,128)(2,1)}, bf16[4,7...) while((s32[]{:T(128)}, ...), condition=%wide.region_12.13_spmd, body=%wide.region_10.12_spmd.sunk | while | flops 1593643904 | bytes 77247440 | solution.py:433
  1532.1 15.8 all_to_all.10
  1591.1 32.2 %collective-permute-done.35 = bf16[1,184,1152]{2,1,0:T(8,128)(2,1)S(1)} collective-permute-done((bf16[1,184,1152]{2,1,0:T(8,128)(2,1)S(1)}, bf16[1,184,1152]{2,1,0:T(8,128)(2,1)S(1)}, u32[]{:S(2)}, u32[]{:S(2)}) %collective-permute-start.35) | collective-permute-done | bytes 423968 | tf_op jit(solution)/shard_map/ppermute | solution.py:139
  1626.3 61.9 %all-gather.19.cloned.1.call-done = bf16[4096,512]{1,0:T(8,128)(2,1)} async-done(((bf16[128,512]{1,0:T(8,128)(2,1)}), bf16[4096,512]{1,0:T(8,128)(2,1)}) %all-gather.19.cloned.1.call-update) | async-done | bytes 4194320 | tf_op jit(solution)/shard_map/all_gather | solution.py:430
  1688.2 7.7 write_grads.1
  (506 shorter events, 385.3 us)
Async XLA Ops:
  7.2 161.5 %all-gather.13.cloned.1.call-start = ((), (), s32[]{:S(2)}) async-start(), calls=%async_computation.3 | async-start | bytes 1658880 | tf_op jit(solution)/shard_map/all_gather | solution.py:145
  11.3 216.5 %all-gather.15.cloned.1.call-start = ((), (), s32[]{:S(2)}) async-start(), calls=%async_computation.4 | async-start | bytes 1566720 | tf_op jit(solution)/shard_map/all_gather | solution.py:145
  15.4 125.5 %collective-permute-start = (bf16[1,184,1152]{2,1,0:T(8,128)(2,1)}, bf16[1,184,1152]{2,1,0:T(8,128)(2,1)}, u32[]{:S(2)}, u32[]{:S(2)}) collective-permute-start(bf16[1,184,1152]{2,1,0:T(8,128)(2,1)} %get-tuple-element.244), channel_id=1, source_target_pairs={{0,1},{1,2},{3,0},{4,5},{5,6},{6,7},{8,9},{9,10},{11,8},{12,13},{1... | collective-permute-start | bytes 1271816 | tf_op jit(solution)/shard_map/ppermute | solution.py:119
  20.5 122.2 %collective-permute-start.1 = (bf16[1,184,1152]{2,1,0:T(8,128)(2,1)}, bf16[1,184,1152]{2,1,0:T(8,128)(2,1)}, u32[]{:S(2)}, u32[]{:S(2)}) collective-permute-start(bf16[1,184,1152]{2,1,0:T(8,128)(2,1)} %get-tuple-element.246), channel_id=1, source_target_pairs={{0,2},{2,0},{3,1},{4,6},{5,7},{7,5},{8,10},{10,8},{11,9},{12,14},{... | collective-permute-start | bytes 1271816 | tf_op jit(solution)/shard_map/ppermute | solution.py:119
  22.8 121.7 %collective-permute-start.2 = (bf16[1,184,1152]{2,1,0:T(8,128)(2,1)}, bf16[1,184,1152]{2,1,0:T(8,128)(2,1)}, u32[]{:S(2)}, u32[]{:S(2)}) collective-permute-start(bf16[1,184,1152]{2,1,0:T(8,128)(2,1)} %get-tuple-element.243), channel_id=1, source_target_pairs={{1,0},{2,1},{3,2},{4,7},{6,5},{7,6},{9,8},{10,9},{11,10},{12,15},{... | collective-permute-start | bytes 1271816 | tf_op jit(solution)/shard_map/ppermute | solution.py:119
  168.7 32.2 %collective-permute-start.6 = (bf16[4,144,1152]{2,1,0:T(8,128)(2,1)}, bf16[4,144,1152]{2,1,0:T(8,128)(2,1)}, u32[]{:S(2)}, u32[]{:S(2)}) collective-permute-start(bf16[4,144,1152]{2,1,0:T(8,128)(2,1)} %bitcast.25.refs_0_), channel_id=1, source_target_pairs={{0,8},{4,12},{8,0},{12,4},{16,24},{20,28},{24,16},{28,20},{1,9},{5... | collective-permute-start | bytes 3981320 | tf_op jit(solution)/shard_map/ppermute | solution.py:103
  168.7 33.4 %collective-permute-start.7 = (bf16[4,144,1152]{2,1,0:T(8,128)(2,1)}, bf16[4,144,1152]{2,1,0:T(8,128)(2,1)}, u32[]{:S(2)}, u32[]{:S(2)}) collective-permute-start(bf16[4,144,1152]{2,1,0:T(8,128)(2,1)} %bitcast.25.refs_0_), channel_id=1, source_target_pairs={{0,16},{4,20},{8,24},{12,28},{16,0},{20,4},{24,8},{28,12},{1,17},{... | collective-permute-start | bytes 3981320 | tf_op jit(solution)/shard_map/ppermute | solution.py:103
  186.0 490.4 %all-gather.17.cloned.1.call-start = ((), (), s32[]{:S(2)}) async-start(), calls=%async_computation.5 | async-start | bytes 1566720 | tf_op jit(solution)/shard_map/all_gather | solution.py:145
  189.5 38.4 %collective-permute-start.10 = (bf16[4,144,1152]{2,1,0:T(8,128)(2,1)}, bf16[4,144,1152]{2,1,0:T(8,128)(2,1)}, u32[]{:S(2)}, u32[]{:S(2)}) collective-permute-start(bf16[4,144,1152]{2,1,0:T(8,128)(2,1)} %bitcast.25.refs_0_), channel_id=1, source_target_pairs={{0,4},{4,0},{8,12},{12,8},{16,20},{20,16},{24,28},{28,24},{1,5},{5... | collective-permute-start | bytes 3981320 | tf_op jit(solution)/shard_map/ppermute | solution.py:103
  227.9 421.3 %collective-permute-start.15 = (bf16[4,72,2176]{2,1,0:T(8,128)(2,1)}, bf16[4,72,2176]{2,1,0:T(8,128)(2,1)}, u32[]{:S(2)}, u32[]{:S(2)}) collective-permute-start(bf16[4,72,2176]{2,1,0:T(8,128)(2,1)} %bitcast.356), channel_id=1, source_target_pairs={{0,8},{4,12},{8,0},{12,4},{16,24},{20,28},{24,16},{28,20},{1,9},{5... | collective-permute-start | bytes 3760136 | tf_op jit(solution)/shard_map/ppermute | solution.py:103
  228.4 422.9 %collective-permute-start.16 = (bf16[4,72,2176]{2,1,0:T(8,128)(2,1)}, bf16[4,72,2176]{2,1,0:T(8,128)(2,1)}, u32[]{:S(2)}, u32[]{:S(2)}) collective-permute-start(bf16[4,72,2176]{2,1,0:T(8,128)(2,1)} %bitcast.357), channel_id=1, source_target_pairs={{0,16},{4,20},{8,24},{12,28},{16,0},{20,4},{24,8},{28,12},{1,17},{... | collective-permute-start | bytes 3760136 | tf_op jit(solution)/shard_map/ppermute | solution.py:103
  230.0 446.4 %collective-permute-start.19 = (bf16[4,72,2176]{2,1,0:T(8,128)(2,1)}, bf16[4,72,2176]{2,1,0:T(8,128)(2,1)}, u32[]{:S(2)}, u32[]{:S(2)}) collective-permute-start(bf16[4,72,2176]{2,1,0:T(8,128)(2,1)} %bitcast.358), channel_id=1, source_target_pairs={{0,4},{4,0},{8,12},{12,8},{16,20},{20,16},{24,28},{28,24},{1,5},{5... | collective-permute-start | bytes 3760136 | tf_op jit(solution)/shard_map/ppermute | solution.py:103
  654.1 25.7 %collective-permute-start.21 = (bf16[4,72,2176]{2,1,0:T(8,128)(2,1)}, bf16[4,72,2176]{2,1,0:T(8,128)(2,1)}, u32[]{:S(2)}, u32[]{:S(2)}) collective-permute-start(bf16[4,72,2176]{2,1,0:T(8,128)(2,1)} %collective-permute-done.16.refs_2_), channel_id=1, source_target_pairs={{0,4},{4,0},{8,12},{12,8},{16,20},{20,16},{24,28},{28,24},{1,5},{5... | collective-permute-start | bytes 3760136 | tf_op jit(solution)/shard_map/ppermute | solution.py:103
  676.4 336.1 %collective-permute-start.24 = (bf16[4,136,1152]{2,1,0:T(8,128)(2,1)}, bf16[4,136,1152]{2,1,0:T(8,128)(2,1)S(1)}, u32[]{:S(2)}, u32[]{:S(2)}) collective-permute-start(bf16[4,136,1152]{2,1,0:T(8,128)(2,1)} %bitcast.352), channel_id=1, source_target_pairs={{0,8},{4,12},{8,0},{12,4},{16,24},{20,28},{24,16},{28,20},{1,9},{5... | collective-permute-start | bytes 3760136 | tf_op jit(solution)/shard_map/ppermute | solution.py:103
  678.0 334.9 %collective-permute-start.25 = (bf16[4,136,1152]{2,1,0:T(8,128)(2,1)}, bf16[4,136,1152]{2,1,0:T(8,128)(2,1)}, u32[]{:S(2)}, u32[]{:S(2)}) collective-permute-start(bf16[4,136,1152]{2,1,0:T(8,128)(2,1)} %bitcast.353), channel_id=1, source_target_pairs={{0,16},{4,20},{8,24},{12,28},{16,0},{20,4},{24,8},{28,12},{1,17},{... | collective-permute-start | bytes 3760136 | tf_op jit(solution)/shard_map/ppermute | solution.py:103
  679.8 355.3 %collective-permute-start.28 = (bf16[4,136,1152]{2,1,0:T(8,128)(2,1)}, bf16[4,136,1152]{2,1,0:T(8,128)(2,1)}, u32[]{:S(2)}, u32[]{:S(2)}) collective-permute-start(bf16[4,136,1152]{2,1,0:T(8,128)(2,1)} %bitcast.354), channel_id=1, source_target_pairs={{0,4},{4,0},{8,12},{12,8},{16,20},{20,16},{24,28},{28,24},{1,5},{5... | collective-permute-start | bytes 3760136 | tf_op jit(solution)/shard_map/ppermute | solution.py:103
  1423.4 202.9 %all-gather.11.cloned.1.call-start = ((), (), s32[]{:S(2)}) async-start(), calls=%async_computation.2 | async-start | bytes 2162688 | tf_op jit(solution)/shard_map/all_gather | solution.py:449
  1548.8 139.4 %all-gather.19.cloned.1.call-start = ((), (), s32[]{:S(2)}) async-start(), calls=%async_computation.6 | async-start | bytes 4325376 | tf_op jit(solution)/shard_map/all_gather | solution.py:430
  1551.9 35.2 %collective-permute-start.33 = (bf16[1,184,1152]{2,1,0:T(8,128)(2,1)}, bf16[1,184,1152]{2,1,0:T(8,128)(2,1)}, u32[]{:S(2)}, u32[]{:S(2)}) collective-permute-start(bf16[1,184,1152]{2,1,0:T(8,128)(2,1)} %get-tuple-element.235), channel_id=1, source_target_pairs={{0,1},{1,2},{2,3},{5,6},{6,7},{7,4},{8,9},{9,10},{10,11},{13,14},{... | collective-permute-start | bytes 1271816 | tf_op jit(solution)/shard_map/ppermute | solution.py:139
  1555.3 34.8 %collective-permute-start.34 = (bf16[1,184,1152]{2,1,0:T(8,128)(2,1)S(1)}, bf16[1,184,1152]{2,1,0:T(8,128)(2,1)}, u32[]{:S(2)}, u32[]{:S(2)}) collective-permute-start(bf16[1,184,1152]{2,1,0:T(8,128)(2,1)S(1)} %get-tuple-element.234), channel_id=1, source_target_pairs={{0,2},{1,3},{2,0},{5,7},{6,4},{7,5},{8,10},{9,11},{10,8},{13,15},{... | collective-permute-start | bytes 1271816 | tf_op jit(solution)/shard_map/ppermute | solution.py:139
  1579.2 45.4 %collective-permute-start.36 = (bf16[1,184,1152]{2,1,0:T(8,128)(2,1)S(1)}, bf16[1,184,1152]{2,1,0:T(8,128)(2,1)S(1)}, u32[]{:S(2)}, u32[]{:S(2)}) collective-permute-start(bf16[1,184,1152]{2,1,0:T(8,128)(2,1)S(1)} %get-tuple-element.231), channel_id=1, source_target_pairs={{0,1},{1,2},{2,3},{5,6},{6,7},{7,4},{8,9},{9,10},{10,11},{13,14},{... | collective-permute-start | bytes 1271816 | tf_op jit(solution)/shard_map/ppermute | solution.py:139
  1581.2 43.4 %collective-permute-start.37 = (bf16[1,184,1152]{2,1,0:T(8,128)(2,1)S(1)}, bf16[1,184,1152]{2,1,0:T(8,128)(2,1)S(1)}, u32[]{:S(2)}, u32[]{:S(2)}) collective-permute-start(bf16[1,184,1152]{2,1,0:T(8,128)(2,1)S(1)} %get-tuple-element.230), channel_id=1, source_target_pairs={{0,2},{1,3},{2,0},{5,7},{6,4},{7,5},{8,10},{9,11},{10,8},{13,15},{... | collective-permute-start | bytes 1271816 | tf_op jit(solution)/shard_map/ppermute | solution.py:139
  1585.1 39.5 %collective-permute-start.38 = (bf16[1,184,1152]{2,1,0:T(8,128)(2,1)S(1)}, bf16[1,184,1152]{2,1,0:T(8,128)(2,1)S(1)}, u32[]{:S(2)}, u32[]{:S(2)}) collective-permute-start(bf16[1,184,1152]{2,1,0:T(8,128)(2,1)S(1)} %get-tuple-element.229), channel_id=1, source_target_pairs={{0,3},{1,0},{2,1},{5,4},{6,5},{7,6},{8,11},{9,8},{10,9},{13,12},{1... | collective-permute-start | bytes 1271816 | tf_op jit(solution)/shard_map/ppermute | solution.py:139
  1587.1 36.3 %collective-permute-start.35 = (bf16[1,184,1152]{2,1,0:T(8,128)(2,1)S(1)}, bf16[1,184,1152]{2,1,0:T(8,128)(2,1)S(1)}, u32[]{:S(2)}, u32[]{:S(2)}) collective-permute-start(bf16[1,184,1152]{2,1,0:T(8,128)(2,1)S(1)} %get-tuple-element.233), channel_id=1, source_target_pairs={{0,3},{1,0},{2,1},{5,4},{6,5},{7,6},{8,11},{9,8},{10,9},{13,12},{1... | collective-permute-start | bytes 1271816 | tf_op jit(solution)/shard_map/ppermute | solution.py:139
  (122 other events, 2541.7 us)
Sparse Core Ops, SparseCore 0:
  11.5 57.2 all-gather.12
  186.1 32.3 all-gather.14
  228.0 29.1 all-gather.16
  1548.9 75.2 all-gather.10
  1627.7 60.5 all-gather.18

commit v3 on v2

--- a/solution.py
+++ b/solution.py
@@ -144,7 +144,7 @@
     def gather_own(self, piece):
         return lax.all_gather(piece, "seq", axis=0)
 
-    def gather_rest(self, own, shape, index):
+    def gather_rest(self, own, shapes, index):
         half = self.seq_size // 2
         over_x = self.flip(own, 2)
         over_y = self.flip(own, 4)
@@ -157,16 +157,20 @@
         at = (self.dp % 8).astype(jnp.int32).reshape(1)
 
         def body(at_ref, *refs):
-            out_ref, sems = refs[-2], refs[-1]
-            copies = []
+            outs, sems = refs[10:-1], refs[-1]
+            waits = []
             for n in range(10):
                 part = at_ref[0] ^ (masks[n % 5] ^ (n // 5))
                 rows = pl.ds(starts[n % 5], parts[n % 5].shape[0])
-                target = out_ref.at[index(part, rows)]
-                copies.append(pltpu.make_async_copy(refs[n], target, sems.at[n]))
-            for copy in copies:
-                copy.start()
-            for copy in copies:
+                which, place = index(part, rows)
+                copies = [pltpu.make_async_copy(refs[n], out.at[place], sems.at[n]) for out in outs]
+                if len(outs) == 1:
+                    copies[0].start()
+                else:
+                    for m, copy in enumerate(copies):
+                        pl.when(which == m)(copy.start)
+                waits.append(copies[0])
+            for copy in waits:
                 copy.wait()
 
         return pl.pallas_call(
@@ -174,13 +178,24 @@
             grid_spec=pltpu.PrefetchScalarGridSpec(
                 num_scalar_prefetch=1,
                 grid=(),
-                in_specs=[pl.BlockSpec(memory_space=pl.ANY)] * 10,
-                out_specs=pl.BlockSpec(memory_space=pl.ANY),
+                in_specs=[pl.BlockSpec(memory_space=pltpu.VMEM)] * 10,
+                out_specs=[pl.BlockSpec(memory_space=pl.ANY)] * len(shapes),
                 scratch_shapes=[pltpu.SemaphoreType.DMA((10,))],
             ),
-            out_shape=jax.ShapeDtypeStruct(shape, own.dtype),
+            out_shape=[jax.ShapeDtypeStruct(shape, own.dtype) for shape in shapes],
             name="assemble",
         )(at, *parts, *others)
+
+    def gather_all(self, values):
+        rows, width = values.shape
+        if self.dp_size != 8:
+            return lax.all_gather(values, ("dp", "seq"), axis=0)
+        full = self.gather_rest(
+            self.gather_own(values),
+            [(8, self.seq_size, rows, width)],
+            lambda part, at: (0, (part, at)),
+        )
+        return full[0].reshape(8 * self.seq_size, rows, width)
 
 
 def pad_blocks(values, axis, blocks, padded):
@@ -205,16 +220,22 @@
     return -(-size // 128)
 
 
-def exchange(parts, owner, devices):
+def exchange(parts, devices, owner=None, info=None):
     padded = [jnp.pad(part, ((0, 0), (0, -part.shape[1] % 128))) for part in parts]
     joined = jnp.concatenate(padded, axis=1).astype(BF)
     rank, total = joined.shape
     width = -(-total // (devices * 128)) * 128
     joined = jnp.pad(joined, ((0, 0), (0, devices * width - total)))
     pieces = joined.reshape(rank, devices, width).transpose(1, 0, 2)
+    if owner is None:
+        tile = jnp.pad(info, (0, 128 - info.shape[0])).astype(BF)
+        tile = jnp.broadcast_to(tile, (devices, rank, 128))
+        pieces = jnp.concatenate([pieces, tile], axis=2)
     pieces = lax.all_to_all(pieces, ("dp", "seq"), split_axis=0, concat_axis=0, tiled=True)
-    sums = dot(owner, pieces.reshape(devices, rank * width), ((0,), (0,))).astype(BF)
-    return sums.reshape(-1, width)
+    if owner is None:
+        owner = pieces[:, 0, width : width + info.shape[0]]
+    sums = dot(owner, pieces[:, :, :width].reshape(devices, rank * width), ((0,), (0,)))
+    return sums.astype(BF).reshape(-1, width), owner
 
 
 def write_grads(early, late, width, hidden_size):
@@ -295,8 +316,7 @@
     live = is_live.astype(F32)
     adapter = lax.dynamic_index_in_dim(adapter_id, own_slot, keepdims=False)
     key_mask = lax.dynamic_index_in_dim(key_live, own_slot, keepdims=False)
-    owner = jnp.where(is_live & (jnp.arange(adapters) == adapter), 1.0, 0.0)
-    owner = lax.all_gather(owner.astype(BF)[None], ("dp", "seq"), axis=0, tiled=True)
+    info = jnp.where(is_live & (jnp.arange(adapters) == adapter), 1.0, 0.0)
 
     flat = place.to_image(tokens).astype(F32)
 
@@ -329,17 +349,22 @@
 
     attn_full = place.gather_rest(
         attn_own,
-        (4, seq_size, 2, half, width),
-        lambda part, at: (part // 2, at, part % 2),
-    ).reshape(4, width, width)
+        [(seq_size, 2, half, width)] * 4,
+        lambda part, at: (part // 2, (at, part % 2)),
+    )
+    attn_full = [values.reshape(width, width) for values in attn_full]
+    side = hidden_pad // 2
     fc1_full = place.gather_rest(
         fc1_own,
-        (2, seq_size, 4, quarter, hidden_pad // 2),
-        lambda part, at: (part % 2, at, part // 2),
-    ).reshape(2, width, hidden_pad // 2)
+        [(seq_size, 4, quarter, side)] * 2,
+        lambda part, at: (part % 2, (at, part // 2)),
+    )
+    fc1_full = [values.reshape(width, side) for values in fc1_full]
     fc2_full = place.gather_rest(
-        fc2_own, (seq_size, 8, padded // 8, width), lambda part, at: (at, part)
-    ).reshape(2, hidden_pad // 2, width)
+        fc2_own,
+        [(seq_size, 8, padded // 8, width)],
+        lambda part, at: (0, (at, part)),
+    )[0].reshape(2, side, width)
 
     def take(values, axis):
         return lax.dynamic_slice_in_dim(values, adapter * RANK, RANK, axis=axis)
@@ -355,7 +380,6 @@
     full_len = flat.shape[0]
     heads = width // HD
 
-    flat, owner = lax.optimization_barrier((flat, owner))
     normed = layer_norm(flat, norm_gain[0], norm_bias[0]).astype(BF)
     normed, out_grad = lax.optimization_barrier((normed, out_grad))
     top_grad = place.to_image(out_grad).astype(F32) * live
@@ -394,7 +418,6 @@
     normed_two_grad = 0.0
     down_2_halves = []
     up_1_halves = []
-    side = hidden_pad // 2
     for index in range(2):
         at = slice(index * side, (index + 1) * side)
         hidden = product(normed_two, fc1_full[index]) + product(rank_one, up_1[:, at]) + bias_1[at]
@@ -423,11 +446,11 @@
     down_o_grad = outer_sum(inner_o, merged)
     merged_grad = product_back(branch_grad, attn_full[3]) + product_back(inner_o, down_a[3])
     merged_grad = merged_grad.astype(BF)
-    early = exchange(
-        [down_2_grad, up_1_grad, up_2_grad, down_1_grad, down_o_grad, up_o_grad], owner, devices
+    early, owner = exchange(
+        [down_2_grad, up_1_grad, up_2_grad, down_1_grad, down_o_grad, up_o_grad], devices, info=info
     )
     early, merged_grad, result = lax.optimization_barrier((early, merged_grad, result))
-    early = lax.all_gather(early, ("dp", "seq"), axis=0)
+    early = place.gather_all(early)
     result = place.to_tokens(result, images)
 
     grad_q, grad_k, grad_v = lax.map(
@@ -445,8 +468,8 @@
             + product_back(proj_grads[index], attn_full[index])
             + product_back(inner, down_a[index])
         )
-    late = exchange(late_parts, owner, devices)
-    late = lax.all_gather(late, ("dp", "seq"), axis=0)
+    late, _ = exchange(late_parts, devices, owner=owner)
+    late = place.gather_all(late)
     input_grad = resid_grad + norm_back(flat, norm_gain[0], norm_bias[0], normed_grad)
     input_grad = place.to_tokens(input_grad.astype(BF), images).astype(F32)
     return (result, input_grad, *write_grads(early, late, width, hidden_size))

time: 1710 us -> 729 us (0.43)
  Pallas kernels: 940 us -> 38.7 us
  blocking collectives: 118 us -> 51 us
  waiting for transfers between devices: 156 us -> 96.3 us
  starting transfers between devices: 48 us -> 81.2 us
    pallas_call x3 -> x5, Pallas kernels: 933 us -> 30.9 us  [gather_rest(): pl.pallas_call(body, grid_spec=pltpu.PrefetchScalarGridSpec(num_scalar_pr...]
    all_gather x2 -> x0, waiting for transfers between devices: 61.9 us -> none  [the longest x1 61.9 us: local(): early = lax.all_gather(early, ('dp', 'seq'), axis=0)]
    all_gather x1 -> x2, blocking collectives: 102 us -> 51 us  [gather_own(): return lax.all_gather(piece, 'seq', axis=0)]
    ppermute x6, waiting for transfers between devices: 9.47 us -> 35.7 us  [to_image(): part = lax.ppermute(part, ('dp', 'seq'), pairs)]
    ppermute x6, waiting for transfers between devices: 32.2 us -> 6.79 us  [to_tokens(): part = lax.ppermute(part, ('dp', 'seq'), pairs)]
    ppermute x27 -> x45, starting transfers between devices: 14.2 us -> 36 us  [flip(): return lax.ppermute(values, 'dp', pairs)]
    dot_general x60, matrix products: 181 us -> 198 us  [dot(): lax.dot_general(left, right, (dims, ((), ())), preferred_element_type=F32)]
    ppermute x27 -> x45, waiting for transfers between devices: 51.3 us -> 48.1 us  [flip(): return lax.ppermute(values, 'dp', pairs)]
  transfers between devices with their start and end apart: 45 -> 62, of which waited for: 10 -> 13; matrix products, arithmetic and copies ran while one was open for 14% -> 32% of each run, Pallas kernels for 37% -> 3%
where the time goes in v3:
time: 729 us; the launch traced here: 717 us
  matrix products  278 us (38%)
  local copies, waits for them, and re-layouts  100 us (14%)
  waiting for transfers between devices  96.3 us (13%)
  starting transfers between devices  81.2 us (11%)
  other arithmetic  53.6 us (7%)
  blocking collectives  51 us (7%)
  Pallas kernels  38.7 us (5%)
  between operations  17.3 us (2%)
    dot_general x60, matrix products, dot(): lax.dot_general(left, right, (dims, ((), ())), preferred_element_type=F32)  198 us
    all_gather x2, blocking collectives, gather_own(): return lax.all_gather(piece, 'seq', axis=0)  51 us
    ppermute x45, waiting for transfers between devices, flip(): return lax.ppermute(values, 'dp', pairs)  48.1 us
    ppermute x45, starting transfers between devices, flip(): return lax.ppermute(values, 'dp', pairs)  36 us
    ppermute x6, waiting for transfers between devices, to_image(): part = lax.ppermute(part, ('dp', 'seq'), pairs)  35.7 us
    pallas_call x5, Pallas kernels, gather_rest(): pl.pallas_call(body, grid_spec=pltpu.PrefetchScalarGridSpec(num_scalar_pr...  30.9 us
    ppermute x6, starting transfers between devices, to_image(): part = lax.ppermute(part, ('dp', 'seq'), pairs)  19.6 us
    ppermute x6, starting transfers between devices, to_tokens(): part = lax.ppermute(part, ('dp', 'seq'), pairs)  17.5 us
  transfers between devices with their start and end apart: 62, of which 13 were waited for; matrix products, arithmetic and copies ran while one was open for 32% of the time, Pallas kernels for 3%

profile of v3, /device:TPU:0, one launch (start us, length us, event | category | flops | bytes accessed | tf_op | source)
XLA Modules:
  0.0 716.9 jit_solution(10082608649096575434)
XLA Ops:
  40.6 24.8 %collective-permute-done.1 = bf16[1,184,1152]{2,1,0:T(8,128)(2,1)} collective-permute-done((bf16[1,184,1152]{2,1,0:T(8,128)(2,1)}, bf16[1,184,1152]{2,1,0:T(8,128)(2,1)}, u32[]{:S(2)}, u32[]{:S(2)}) %collective-permute-start.1) | collective-permute-done | bytes 423968 | tf_op jit(solution)/shard_map/ppermute | solution.py:119
  78.8 7.7 %collective-permute-start.3 = (bf16[1,184,1152]{2,1,0:T(8,128)(2,1)}, bf16[1,184,1152]{2,1,0:T(8,128)(2,1)}, u32[]{:S(2)}, u32[]{:S(2)}) collective-permute-start(bf16[1,184,1152]{2,1,0:T(8,128)(2,1)} %get-tuple-element.243), channel_id=1, source_target_pairs={{0,1},{1,2},{3,0},{4,5},{5,6},{6,7},{8,9},{9,10},{11,8},{12,13},{1... | collective-permute-start | bytes 1271816 | tf_op jit(solution)/shard_map/ppermute | solution.py:119
  107.3 10.8 %collective-permute-done.4 = bf16[1,184,1152]{2,1,0:T(8,128)(2,1)} collective-permute-done((bf16[1,184,1152]{2,1,0:T(8,128)(2,1)}, bf16[1,184,1152]{2,1,0:T(8,128)(2,1)}, u32[]{:S(2)}, u32[]{:S(2)}) %collective-permute-start.4) | collective-permute-done | bytes 423968 | tf_op jit(solution)/shard_map/ppermute | solution.py:119
  122.2 9.2 %collective-permute-done.6.refs_1_ = bf16[4,144,1152]{2,1,0:T(8,128)(2,1)} collective-permute-done((bf16[4,144,1152]{2,1,0:T(8,128)(2,1)}, bf16[4,144,1152]{2,1,0:T(8,128)(2,1)}, u32[]{:S(2)}, u32[]{:S(2)}) %collective-permute-start.6) | collective-permute-done | bytes 1327136 | tf_op jit(solution)/shard_map/ppermute | solution.py:103
  142.1 7.3 %collective-permute-done.8.refs_3_ = bf16[2,144,1152]{2,1,0:T(8,128)(2,1)} collective-permute-done((bf16[2,144,1152]{2,1,0:T(8,128)(2,1)S(1)}, bf16[2,144,1152]{2,1,0:T(8,128)(2,1)}, u32[]{:S(2)}, u32[]{:S(2)}) %collective-permute-start.8) | collective-permute-done | bytes 663584 | tf_op jit(solution)/shard_map/ppermute | solution.py:103
  164.4 8.2 %assemble.5 = (bf16[4,2,144,1152]{3,2,1,0:T(8,128)(2,1)}, bf16[4,2,144,1152]{3,2,1,0:T(8,128)(2,1)}, bf16[4,2,144,1152]{3,2,1,0:T(8,128)(2,1)}, bf16[4,2,144,1152]{3,2,1,0:T(8,128)(2,1)}) custom-call(s32[1]{0:T(128)} %bitcast.21.at_ref, bf16[4,144,1152]{2,1,0:T(8,128)(2,1)} %bitcast.23.refs_0_, bf16[4,144,1152]{2,1,0:T(8,128)(2,1)} %collective-permute-done.6.refs_1_, ...), custom_call_target="tpu_custom_call" | custom-call | tf_op jit(solution)/shard_map/assemble/pallas_call | solution.py:176
  198.4 41.0 %while.26 = (s32[]{:T(128)}, bf16[4,736,4,72]{1,3,2,0:T(8,128)(2,1)}, f32[4,4,736]{2,1,0:T(4,128)}, bf16[4,736,4,72]{1,3,2,0:T(8,128)(2,1)}, s32[4,736]{1,0:T(4,...) while((s32[]{:T(128)}, bf16[4,736,4,72]{1,3,2,0:T(8,128)(2,1)}, ...), condition=%wide.region_5.6_spmd, body=%wide.region_2.5_spmd.sunk | while | flops 650033024 | bytes 28316792 | solution.py:407
  255.3 11.9 %collective-permute-done.17.refs_3_ = bf16[2,72,2176]{2,1,0:T(8,128)(2,1)} collective-permute-done((bf16[2,72,2176]{2,1,0:T(8,128)(2,1)S(1)}, bf16[2,72,2176]{2,1,0:T(8,128)(2,1)}, u32[]{:S(2)}, u32[]{:S(2)}) %collective-permute-start.17) | collective-permute-done | bytes 626720 | tf_op jit(solution)/shard_map/ppermute | solution.py:103
  278.7 7.7 %assemble.6 = (bf16[4,4,72,2176]{3,2,1,0:T(8,128)(2,1)}, bf16[4,4,72,2176]{3,2,1,0:T(8,128)(2,1)}) custom-call(s32[1]{0:T(128)} %bitcast.21.at_ref, bf16[4,72,2176]{2,1,0:T(8,128)(2,1)} %bitcast.345, bf16[4,72,2176]{2,1,0:T(8,128)(2,1)} %collective-permute-done.15.refs_1_, bf16[4,72,2176]{2,1,0:T(8,128)(2,1)} %collective-permute-done.16.refs_2_, ...), custom_call_target="tpu_custom_call" | custom-call | tf_op jit(solution)/shard_map/assemble/pallas_call | solution.py:176
  286.4 12.9 %multiply_convert_fusion.2 = (bf16[736,2176]{1,0:T(8,128)(2,1)S(1)}, f32[736,2176]{1,0:T(8,128)}) fusion(f32[2176]{0:T(1024)} %add.479, f32[736,2176]{1,0:T(8,128)} %fusion.118, bf16[736,1152]{1,0:T(8,128)(2,1)} %copy-done.14, bf16[1152,2176]{1,0:T(8,128)(2,1)} %bitcast.354), kind=kOutput, calls=%fused_computation.84 | convolution fusion | flops 3707555840 | bytes 22733312 | tf_op jit(solution)/shard_map/dot_general | solution.py:17
  301.9 8.9 %multiply_convert_fusion.1 = (bf16[736,2176]{1,0:T(8,128)(2,1)S(1)}, f32[736,2176]{1,0:T(8,128)}) fusion(f32[2176]{0:T(1024)S(1)} %copy-done.85, f32[736,2176]{1,0:T(8,128)} %fusion.114, bf16[736,1152]{1,0:T(8,128)(2,1)S(1)} %copy-done.15, bf16[1152,2176]{1,0:T(8,128)(2,1)S(1)} %bitcast.357), kind=kOutput, calls=%fused_computation.82 | convolution fusion | flops 3707555840 | bytes 22733312 | tf_op jit(solution)/shard_map/dot_general | solution.py:17
  320.0 9.6 %collective-permute-done.26.refs_3_ = bf16[2,136,1152]{2,1,0:T(8,128)(2,1)} collective-permute-done((bf16[2,136,1152]{2,1,0:T(8,128)(2,1)S(1)}, bf16[2,136,1152]{2,1,0:T(8,128)(2,1)}, u32[]{:S(2)}, u32[]{:S(2)}) %collective-permute-start.26) | collective-permute-done | bytes 626720 | tf_op jit(solution)/shard_map/ppermute | solution.py:103
  339.8 8.0 %assemble.7 = bf16[4,8,136,1152]{3,2,1,0:T(8,128)(2,1)} custom-call(s32[1]{0:T(128)} %bitcast.21.at_ref, bf16[4,136,1152]{2,1,0:T(8,128)(2,1)} %bitcast.349, bf16[4,136,1152]{2,1,0:T(8,128)(2,1)} %collective-permute-done.24.refs_1_, bf16[4,136,1152]{2,1,0:T(8,128)(2,1)} %collective-permute-done.25.refs_2_, ...), custom_call_target="tpu_custom_call" | custom-call | tf_op jit(solution)/shard_map/assemble/pallas_call | solution.py:176
  347.8 8.5 %fusion.154 = (bf16[2,8,136,1152]{3,2,1,0:T(8,128)(2,1)}, bf16[2,8,136,1152]{3,2,1,0:T(8,128)(2,1)}) fusion(bf16[4,8,136,1152]{3,2,1,0:T(8,128)(2,1)} %assemble.7), kind=kLoop, calls=%fused_computation.293 | loop fusion | bytes 20054016 | tf_op jit(solution)/shard_map/slice | solution.py:428
  356.3 12.3 %fusion.64 = bf16[736,2176]{1,0:T(8,128)(2,1)S(1)} fusion(f32[736,2176]{1,0:T(8,128)} %get-tuple-element.258, f32[736,2176]{1,0:T(8,128)} %fusion.156, bf16[736,1152]{1,0:T(8,128)(2,1)S(1)} %bitcast.340, bf16[2176,1152]{1,0:T(8,128)(2,1)} %bitcast.331), kind=kOutput, calls=%fused_computation.74 | convolution fusion | flops 3723571200 | bytes 22724608 | tf_op jit(solution)/shard_map/dot_general | solution.py:17
  370.6 9.0 %fusion.160 = f32[736,1152]{1,0:T(8,128)} fusion(bf16[736,2176]{1,0:T(8,128)(2,1)S(1)} %copy-done.13, bf16[2176,1152]{1,0:T(8,128)(2,1)} %bitcast.333), kind=kOutput, calls=%fused_computation.299 | convolution fusion | flops 3689938944 | bytes 11608064 | tf_op jit(solution)/shard_map/dot_general | solution.py:17
  379.5 11.5 %fusion.71 = bf16[736,2176]{1,0:T(8,128)(2,1)S(1)} fusion(f32[736,2176]{1,0:T(8,128)} %get-tuple-element.256, f32[736,2176]{1,0:T(8,128)S(1)} %bitcast.319, bf16[736,1152]{1,0:T(8,128)(2,1)S(1)} %bitcast.341, bf16[2176,1152]{1,0:T(8,128)(2,1)} %bitcast.334), kind=kOutput, calls=%fused_computation.81 | convolution fusion | flops 3723571200 | bytes 22724608 | tf_op jit(solution)/shard_map/dot_general | solution.py:17
  400.3 7.5 %multiply_reduce_fusion.2 = (f32[736]{0:T(1024)S(1)}, f32[736,1152]{1,0:T(8,128)S(1)}) fusion(f32[736,1152]{1,0:T(8,128)S(1)} %get-tuple-element.254, f32[736]{0:T(1024)S(1)} %copy-done.65, f32[1152]{0:T(1024)S(1)} %copy-done.79, f32[736,1152]{1,0:T(8,128)S(1)} %fusion.107, f32[736,1152]{1,0:T(8,128)S(1)} %fusion.159, bf16[736,2176]{1,0:T(8,128)(2,1)S(1)} %fusion.64, ...), kind=kOutput, calls=%fused_computation.117 | convolution fusion | flops 3695025408 | bytes 21793024 | tf_op jit(solution)/shard_map/dot_general | solution.py:17
  436.4 11.1 %fusion.86 = bf16[736,1152]{1,0:T(8,128)(2,1)} fusion(f32[736,1152]{1,0:T(8,128)S(1)} %get-tuple-element.254, f32[736,1152]{1,0:T(8,128)} %fusion.121, f32[736,1152]{1,0:T(8,128)} %fusion.160, bf16[736,2176]{1,0:T(8,128)(2,1)} %copy-done.11, bf16[2176,1152]{1,0:T(8,128)(2,1)} %bitcast.332, f32[]{:T(128)S(6)} %convert_element_type.178, f32[1152]{0:T(1024)S(1)} %copy-done.89), kind=kOutput, calls=%fused_computation.127 | convolution fusion | flops 3695026176 | bytes 20091396 | tf_op jit(solution)/shard_map/dot_general | solution.py:17
  464.2 68.5 %while.27 = (s32[]{:T(128)}, bf16[4,736,4,72]{1,3,2,0:T(8,128)(2,1)}, bf16[4,736,4,72]{1,3,2,0:T(8,128)(2,1)}, bf16[4,736,4,72]{1,3,2,0:T(8,128)(2,1)}, bf16[4,7...) while((s32[]{:T(128)}, ...), condition=%wide.region_12.13_spmd, body=%wide.region_10.12_spmd.sunk | while | flops 1593643904 | bytes 77435856 | solution.py:456
  561.4 20.1 %all-gather.3 = bf16[512,512]{1,0:T(8,128)(2,1)} all-gather(bf16[128,512]{1,0:T(8,128)(2,1)S(1)} %copy-done.43), channel_id=5, replica_groups=mesh['dp'=8,'seq'=4] {'seq'}, dimensions={0}, use_global_device_ids=true | all-gather | bytes 655360 | tf_op jit(solution)/shard_map/all_gather | solution.py:145
  583.0 7.7 %fusion.75 = f32[736,1152]{1,0:T(8,128)S(1)} fusion(f32[736,1152]{1,0:T(8,128)} %fusion.111, f32[736,1152]{1,0:T(8,128)} %fusion.161, f32[736,1152]{1,0:T(8,128)} %fusion.106, bf16[736,1152]{0,1:T(8,128)(2,1)S(1)} %bitcast.329, bf16[1152,1152]{1,0:T(8,128)(2,1)} %bitcast.361), kind=kOutput, calls=%fused_computation.96 | convolution fusion | flops 1956040704 | bytes 17915904 | tf_op jit(solution)/shard_map/dot_general | solution.py:17
  624.6 30.8 %all_gather.31.refs_0_ = bf16[4,128,256]{2,1,0:T(8,128)(2,1)} all-gather(bf16[1,128,256]{2,1,0:T(8,128)(2,1)S(1)} %all_gather_reshape.7), channel_id=1, replica_groups=mesh['dp'=8,'seq'=4] {'seq'}, dimensions={0}, use_global_device_ids=true | all-gather | bytes 327680 | tf_op jit(solution)/shard_map/all_gather | solution.py:145
  699.4 7.7 %write_grads.1 = (f32[4,1152,128]{2,1,0:T(8,128)}, f32[4,128,1152]{2,1,0:T(8,128)}, f32[1152,128]{1,0:T(8,128)}, f32[128,4304]{1,0:T(8,128)}, f32[4304,128]{1,0:T(8,128)}, /*index=5*/f32[128,1152]{1,0:T(8,128)}) custom-call(bf16[32,128,512]{2,1,0:T(8,128)(2,1)} %bitcast.320, bf16[32,128,256]{2,1,0:T(8,128)(2,1)} %bitcast.323), custom_call_target="tpu_custom_call" | custom-call | tf_op jit(solution)/shard_map/write_grads/pallas_call | solution.py:277
  (552 shorter events, 445.6 us)
Async XLA Ops:
  7.2 94.2 %all-gather.8.cloned.1.call-start = ((), (), s32[]{:S(2)}) async-start(), calls=%async_computation.2 | async-start | bytes 1658880 | tf_op jit(solution)/shard_map/all_gather | solution.py:145
  11.3 150.7 %all-gather.10.cloned.1.call-start = ((), (), s32[]{:S(2)}) async-start(), calls=%async_computation.3 | async-start | bytes 1566720 | tf_op jit(solution)/shard_map/all_gather | solution.py:145
  20.6 44.8 %collective-permute-start.1 = (bf16[1,184,1152]{2,1,0:T(8,128)(2,1)}, bf16[1,184,1152]{2,1,0:T(8,128)(2,1)}, u32[]{:S(2)}, u32[]{:S(2)}) collective-permute-start(bf16[1,184,1152]{2,1,0:T(8,128)(2,1)} %get-tuple-element.248), channel_id=1, source_target_pairs={{0,2},{2,0},{3,1},{4,6},{5,7},{7,5},{8,10},{10,8},{11,9},{12,14},{... | collective-permute-start | bytes 1271816 | tf_op jit(solution)/shard_map/ppermute | solution.py:119
  22.9 44.3 %collective-permute-start.2 = (bf16[1,184,1152]{2,1,0:T(8,128)(2,1)}, bf16[1,184,1152]{2,1,0:T(8,128)(2,1)}, u32[]{:S(2)}, u32[]{:S(2)}) collective-permute-start(bf16[1,184,1152]{2,1,0:T(8,128)(2,1)} %get-tuple-element.245), channel_id=1, source_target_pairs={{1,0},{2,1},{3,2},{4,7},{6,5},{7,6},{9,8},{10,9},{11,10},{12,15},{... | collective-permute-start | bytes 1271816 | tf_op jit(solution)/shard_map/ppermute | solution.py:119
  78.8 27.4 %collective-permute-start.3 = (bf16[1,184,1152]{2,1,0:T(8,128)(2,1)}, bf16[1,184,1152]{2,1,0:T(8,128)(2,1)}, u32[]{:S(2)}, u32[]{:S(2)}) collective-permute-start(bf16[1,184,1152]{2,1,0:T(8,128)(2,1)} %get-tuple-element.243), channel_id=1, source_target_pairs={{0,1},{1,2},{3,0},{4,5},{5,6},{6,7},{8,9},{9,10},{11,8},{12,13},{1... | collective-permute-start | bytes 1271816 | tf_op jit(solution)/shard_map/ppermute | solution.py:119
  101.4 30.0 %collective-permute-start.6 = (bf16[4,144,1152]{2,1,0:T(8,128)(2,1)}, bf16[4,144,1152]{2,1,0:T(8,128)(2,1)}, u32[]{:S(2)}, u32[]{:S(2)}) collective-permute-start(bf16[4,144,1152]{2,1,0:T(8,128)(2,1)} %bitcast.23.refs_0_), channel_id=1, source_target_pairs={{0,8},{4,12},{8,0},{12,4},{16,24},{20,28},{24,16},{28,20},{1,9},{5... | collective-permute-start | bytes 3981320 | tf_op jit(solution)/shard_map/ppermute | solution.py:103
  103.7 31.7 %collective-permute-start.7 = (bf16[4,144,1152]{2,1,0:T(8,128)(2,1)}, bf16[4,144,1152]{2,1,0:T(8,128)(2,1)}, u32[]{:S(2)}, u32[]{:S(2)}) collective-permute-start(bf16[4,144,1152]{2,1,0:T(8,128)(2,1)} %bitcast.23.refs_0_), channel_id=1, source_target_pairs={{0,16},{4,20},{8,24},{12,28},{16,0},{20,4},{24,8},{28,12},{1,17},{... | collective-permute-start | bytes 3981320 | tf_op jit(solution)/shard_map/ppermute | solution.py:103
  120.3 157.0 %all-gather.12.cloned.1.call-start = ((), (), s32[]{:S(2)}) async-start(), calls=%async_computation.4 | async-start | bytes 1566720 | tf_op jit(solution)/shard_map/all_gather | solution.py:145
  122.2 39.9 %collective-permute-start.10 = (bf16[4,144,1152]{2,1,0:T(8,128)(2,1)}, bf16[4,144,1152]{2,1,0:T(8,128)(2,1)S(1)}, u32[]{:S(2)}, u32[]{:S(2)}) collective-permute-start(bf16[4,144,1152]{2,1,0:T(8,128)(2,1)} %bitcast.23.refs_0_), channel_id=1, source_target_pairs={{0,4},{4,0},{8,12},{12,8},{16,20},{20,16},{24,28},{28,24},{1,5},{5... | collective-permute-start | bytes 3981320 | tf_op jit(solution)/shard_map/ppermute | solution.py:103
  138.9 25.5 %collective-permute-start.11 = (bf16[4,144,1152]{2,1,0:T(8,128)(2,1)}, bf16[4,144,1152]{2,1,0:T(8,128)(2,1)}, u32[]{:S(2)}, u32[]{:S(2)}) collective-permute-start(bf16[4,144,1152]{2,1,0:T(8,128)(2,1)} %collective-permute-done.6.refs_1_), channel_id=1, source_target_pairs={{0,4},{4,0},{8,12},{12,8},{16,20},{20,16},{24,28},{28,24},{1,5},{5... | collective-permute-start | bytes 3981320 | tf_op jit(solution)/shard_map/ppermute | solution.py:103
  162.1 87.2 %collective-permute-start.15 = (bf16[4,72,2176]{2,1,0:T(8,128)(2,1)}, bf16[4,72,2176]{2,1,0:T(8,128)(2,1)}, u32[]{:S(2)}, u32[]{:S(2)}) collective-permute-start(bf16[4,72,2176]{2,1,0:T(8,128)(2,1)} %bitcast.342), channel_id=1, source_target_pairs={{0,8},{4,12},{8,0},{12,4},{16,24},{20,28},{24,16},{28,20},{1,9},{5... | collective-permute-start | bytes 3760136 | tf_op jit(solution)/shard_map/ppermute | solution.py:103
  164.1 88.2 %collective-permute-start.16 = (bf16[4,72,2176]{2,1,0:T(8,128)(2,1)}, bf16[4,72,2176]{2,1,0:T(8,128)(2,1)}, u32[]{:S(2)}, u32[]{:S(2)}) collective-permute-start(bf16[4,72,2176]{2,1,0:T(8,128)(2,1)} %bitcast.343), channel_id=1, source_target_pairs={{0,16},{4,20},{8,24},{12,28},{16,0},{20,4},{24,8},{28,12},{1,17},{... | collective-permute-start | bytes 3760136 | tf_op jit(solution)/shard_map/ppermute | solution.py:103
  164.4 112.9 %collective-permute-start.19 = (bf16[4,72,2176]{2,1,0:T(8,128)(2,1)}, bf16[4,72,2176]{2,1,0:T(8,128)(2,1)}, u32[]{:S(2)}, u32[]{:S(2)}) collective-permute-start(bf16[4,72,2176]{2,1,0:T(8,128)(2,1)} %bitcast.344), channel_id=1, source_target_pairs={{0,4},{4,0},{8,12},{12,8},{16,20},{20,16},{24,28},{28,24},{1,5},{5... | collective-permute-start | bytes 3760136 | tf_op jit(solution)/shard_map/ppermute | solution.py:103
  253.4 25.2 %collective-permute-start.20 = (bf16[4,72,2176]{2,1,0:T(8,128)(2,1)}, bf16[4,72,2176]{2,1,0:T(8,128)(2,1)}, u32[]{:S(2)}, u32[]{:S(2)}) collective-permute-start(bf16[4,72,2176]{2,1,0:T(8,128)(2,1)} %collective-permute-done.15.refs_1_), channel_id=1, source_target_pairs={{0,4},{4,0},{8,12},{12,8},{16,20},{20,16},{24,28},{28,24},{1,5},{5... | collective-permute-start | bytes 3760136 | tf_op jit(solution)/shard_map/ppermute | solution.py:103
  253.7 24.9 %collective-permute-start.21 = (bf16[4,72,2176]{2,1,0:T(8,128)(2,1)}, bf16[4,72,2176]{2,1,0:T(8,128)(2,1)}, u32[]{:S(2)}, u32[]{:S(2)}) collective-permute-start(bf16[4,72,2176]{2,1,0:T(8,128)(2,1)} %collective-permute-done.16.refs_2_), channel_id=1, source_target_pairs={{0,4},{4,0},{8,12},{12,8},{16,20},{20,16},{24,28},{28,24},{1,5},{5... | collective-permute-start | bytes 3760136 | tf_op jit(solution)/shard_map/ppermute | solution.py:103
  277.3 34.0 %collective-permute-start.24 = (bf16[4,136,1152]{2,1,0:T(8,128)(2,1)}, bf16[4,136,1152]{2,1,0:T(8,128)(2,1)}, u32[]{:S(2)}, u32[]{:S(2)}) collective-permute-start(bf16[4,136,1152]{2,1,0:T(8,128)(2,1)} %bitcast.346), channel_id=1, source_target_pairs={{0,8},{4,12},{8,0},{12,4},{16,24},{20,28},{24,16},{28,20},{1,9},{5... | collective-permute-start | bytes 3760136 | tf_op jit(solution)/shard_map/ppermute | solution.py:103
  277.6 36.3 %collective-permute-start.25 = (bf16[4,136,1152]{2,1,0:T(8,128)(2,1)}, bf16[4,136,1152]{2,1,0:T(8,128)(2,1)}, u32[]{:S(2)}, u32[]{:S(2)}) collective-permute-start(bf16[4,136,1152]{2,1,0:T(8,128)(2,1)} %bitcast.347), channel_id=1, source_target_pairs={{0,16},{4,20},{8,24},{12,28},{16,0},{20,4},{24,8},{28,12},{1,17},{... | collective-permute-start | bytes 3760136 | tf_op jit(solution)/shard_map/ppermute | solution.py:103
  278.7 61.2 %collective-permute-start.28 = (bf16[4,136,1152]{2,1,0:T(8,128)(2,1)}, bf16[4,136,1152]{2,1,0:T(8,128)(2,1)}, u32[]{:S(2)}, u32[]{:S(2)}) collective-permute-start(bf16[4,136,1152]{2,1,0:T(8,128)(2,1)} %bitcast.348), channel_id=1, source_target_pairs={{0,4},{4,0},{8,12},{12,8},{16,20},{20,16},{24,28},{28,24},{1,5},{5... | collective-permute-start | bytes 3760136 | tf_op jit(solution)/shard_map/ppermute | solution.py:103
  556.9 64.9 %all-to-all-start.1 = ((bf16[32,16,256]{2,1,0:T(8,128)(2,1)}), bf16[32,16,256]{2,1,0:T(8,128)(2,1)}, u32[]{:S(2)}, u32[]{:S(2)}) async-start(bf16[32,16,256]{2,1,0:T(8,128)(2,1)} %bitcast.276), calls=%async_computation.1 | async-start | bytes 524288 | tf_op jit(solution)/shard_map/all_to_all | solution.py:234
  581.5 75.9 %collective-permute-start.39 = (bf16[4,128,512]{2,1,0:T(8,128)(2,1)}, bf16[4,128,512]{2,1,0:T(8,128)(2,1)}, u32[]{:S(2)}, u32[]{:S(2)}) collective-permute-start(bf16[4,128,512]{2,1,0:T(8,128)(2,1)} %bitcast.70.refs_0_), channel_id=1, source_target_pairs={{0,8},{4,12},{8,0},{12,4},{16,24},{20,28},{24,16},{28,20},{1,9},{5... | collective-permute-start | bytes 1572872 | tf_op jit(solution)/shard_map/ppermute | solution.py:103
  610.7 44.7 %collective-permute-start.37 = (bf16[1,184,1152]{2,1,0:T(8,128)(2,1)}, bf16[1,184,1152]{2,1,0:T(8,128)(2,1)}, u32[]{:S(2)}, u32[]{:S(2)}) collective-permute-start(bf16[1,184,1152]{2,1,0:T(8,128)(2,1)} %get-tuple-element.232), channel_id=1, source_target_pairs={{0,2},{1,3},{2,0},{5,7},{6,4},{7,5},{8,10},{9,11},{10,8},{13,15},{... | collective-permute-start | bytes 1271816 | tf_op jit(solution)/shard_map/ppermute | solution.py:139
  613.9 42.0 %collective-permute-start.38 = (bf16[1,184,1152]{2,1,0:T(8,128)(2,1)}, bf16[1,184,1152]{2,1,0:T(8,128)(2,1)}, u32[]{:S(2)}, u32[]{:S(2)}) collective-permute-start(bf16[1,184,1152]{2,1,0:T(8,128)(2,1)} %get-tuple-element.231), channel_id=1, source_target_pairs={{0,3},{1,0},{2,1},{5,4},{6,5},{7,6},{8,11},{9,8},{10,9},{13,12},{1... | collective-permute-start | bytes 1271816 | tf_op jit(solution)/shard_map/ppermute | solution.py:139
  617.1 44.9 %collective-permute-start.33 = (bf16[1,184,1152]{2,1,0:T(8,128)(2,1)}, bf16[1,184,1152]{2,1,0:T(8,128)(2,1)}, u32[]{:S(2)}, u32[]{:S(2)}) collective-permute-start(bf16[1,184,1152]{2,1,0:T(8,128)(2,1)} %get-tuple-element.237), channel_id=1, source_target_pairs={{0,1},{1,2},{2,3},{5,6},{6,7},{7,4},{8,9},{9,10},{10,11},{13,14},{... | collective-permute-start | bytes 1271816 | tf_op jit(solution)/shard_map/ppermute | solution.py:139
  623.0 50.6 %collective-permute-start.40 = (bf16[4,128,512]{2,1,0:T(8,128)(2,1)}, bf16[4,128,512]{2,1,0:T(8,128)(2,1)}, u32[]{:S(2)}, u32[]{:S(2)}) collective-permute-start(bf16[4,128,512]{2,1,0:T(8,128)(2,1)} %bitcast.70.refs_0_), channel_id=1, source_target_pairs={{0,16},{4,20},{8,24},{12,28},{16,0},{20,4},{24,8},{28,12},{1,17},{... | collective-permute-start | bytes 1572872 | tf_op jit(solution)/shard_map/ppermute | solution.py:103
  (141 other events, 1753.8 us)
Sparse Core Ops, SparseCore 0:
  11.5 57.3 all-gather.7
  120.4 34.2 all-gather.9
  162.2 30.5 all-gather.11

commit v4 on v3

--- a/solution.py
+++ b/solution.py
@@ -48,40 +48,86 @@
     return jax.nn.gelu(values, approximate=True)
 
 
-def attend_heads(operands):
-    queries, key_rows, value_rows, key_mask = operands
-    scores = jnp.einsum(
-        "qhd,khd->hqk", queries, key_rows, preferred_element_type=F32
-    ) * HD ** (-0.5)
-    scores = jnp.where(key_mask[None, None, :] > 0, scores, -1e30)
-    row_top = jnp.max(scores, axis=-1, keepdims=True)
-    exponent = jnp.exp(scores - row_top)
-    row_total = jnp.sum(exponent, axis=-1, keepdims=True)
-    attn_probs = (exponent / row_total).astype(BF)
-    output = jnp.einsum("hqk,khd->qhd", attn_probs, value_rows, preferred_element_type=F32)
-    return (output, (row_top + jnp.log(row_total))[:, :, 0])
-
-
-def attend_back(operands):
-    queries, key_rows, value_rows, key_mask, log_total, grad_out = operands
-    scores = jnp.einsum(
-        "qhd,khd->hqk", queries, key_rows, preferred_element_type=F32
-    ) * HD ** (-0.5)
-    scores = jnp.where(key_mask[None, None, :] > 0, scores, -1e30)
-    attn_probs = jnp.exp(scores - log_total[:, :, None])
-    grad_values = jnp.einsum(
-        "hqk,qhd->khd", attn_probs.astype(BF), grad_out, preferred_element_type=F32
-    )
-    grad_probs = jnp.einsum("qhd,khd->hqk", grad_out, value_rows, preferred_element_type=F32)
-    row_dot = jnp.sum(attn_probs * grad_probs, axis=-1, keepdims=True)
-    grad_scores = (attn_probs * (grad_probs - row_dot)).astype(BF)
-    grad_queries = jnp.einsum(
-        "hqk,khd->qhd", grad_scores, key_rows, preferred_element_type=F32
-    ) * HD ** (-0.5)
-    grad_keys = jnp.einsum(
-        "hqk,qhd->khd", grad_scores, queries, preferred_element_type=F32
-    ) * HD ** (-0.5)
-    return (grad_queries.astype(BF), grad_keys.astype(BF), grad_values.astype(BF))
+def masked_scores(key_rows, queries, mask):
+    scores = lax.dot_general(key_rows, queries, (((0,), (0,)), ((), ())), preferred_element_type=F32)
+    return jnp.where(mask > 0, scores * HD ** (-0.5), -1e30)
+
+
+def attend(queries, key_rows, value_rows, mask):
+    width, length = queries.shape
+    pairs = width // (2 * HD)
+
+    def body(q_ref, k_ref, v_ref, mask_ref, out_ref, log_ref):
+        for n in range(2):
+            at = slice(n * HD, (n + 1) * HD)
+            scores = masked_scores(k_ref[at, :], q_ref[at, :], mask_ref[...])
+            top = jnp.max(scores, axis=0, keepdims=True)
+            exponent = jnp.exp(scores - top)
+            total = jnp.sum(exponent, axis=0, keepdims=True)
+            probs = (exponent * (1.0 / total)).astype(BF)
+            out = lax.dot_general(
+                v_ref[at, :], probs, (((1,), (0,)), ((), ())), preferred_element_type=F32
+            )
+            out_ref[at, :] = out.astype(BF)
+            log_ref[0, n : n + 1, :] = top + jnp.log(total)
+
+    block = pl.BlockSpec((2 * HD, length), lambda n: (n, 0))
+    return pl.pallas_call(
+        body,
+        grid=(pairs,),
+        in_specs=[block, block, block, pl.BlockSpec((length, 1), lambda n: (0, 0))],
+        out_specs=[block, pl.BlockSpec((1, 2, length), lambda n: (n, 0, 0))],
+        out_shape=[
+            jax.ShapeDtypeStruct((width, length), BF),
+            jax.ShapeDtypeStruct((pairs, 2, length), F32),
+        ],
+        name="attend",
+    )(queries, key_rows, value_rows, mask)
+
+
+def attend_grads(queries, key_rows, value_rows, mask, log_total, grad_out):
+    width, length = queries.shape
+    pairs = width // (2 * HD)
+
+    def body(q_ref, k_ref, v_ref, mask_ref, log_ref, grad_ref, dq_ref, dk_ref, dv_ref):
+        for n in range(2):
+            at = slice(n * HD, (n + 1) * HD)
+            q, k, v, grad = q_ref[at, :], k_ref[at, :], v_ref[at, :], grad_ref[at, :]
+            probs = jnp.exp(masked_scores(k, q, mask_ref[...]) - log_ref[0, n : n + 1, :])
+            dv = lax.dot_general(
+                grad, probs.astype(BF), (((1,), (1,)), ((), ())), preferred_element_type=F32
+            )
+            dv_ref[at, :] = dv.astype(BF)
+            grad_probs = lax.dot_general(
+                v, grad, (((0,), (0,)), ((), ())), preferred_element_type=F32
+            )
+            row_dot = jnp.sum(probs * grad_probs, axis=0, keepdims=True)
+            grad_scores = (probs * (grad_probs - row_dot)).astype(BF)
+            dq = lax.dot_general(
+                k, grad_scores, (((1,), (0,)), ((), ())), preferred_element_type=F32
+            )
+            dq_ref[at, :] = (dq * HD ** (-0.5)).astype(BF)
+            dk = lax.dot_general(
+                q, grad_scores, (((1,), (1,)), ((), ())), preferred_element_type=F32
+            )
+            dk_ref[at, :] = (dk * HD ** (-0.5)).astype(BF)
+
+    block = pl.BlockSpec((2 * HD, length), lambda n: (n, 0))
+    return pl.pallas_call(
+        body,
+        grid=(pairs,),
+        in_specs=[
+            block,
+            block,
+            block,
+            pl.BlockSpec((length, 1), lambda n: (0, 0)),
+            pl.BlockSpec((1, 2, length), lambda n: (n, 0, 0)),
+            block,
+        ],
+        out_specs=[block] * 3,
+        out_shape=[jax.ShapeDtypeStruct((width, length), BF)] * 3,
+        name="attend_grads",
+    )(queries, key_rows, value_rows, mask, log_total, grad_out)
 
 
 class Place:
@@ -190,8 +236,16 @@
         rows, width = values.shape
         if self.dp_size != 8:
             return lax.all_gather(values, ("dp", "seq"), axis=0)
+        own = jnp.zeros((self.seq_size, rows, width), values.dtype)
+        for step in range(self.seq_size):
+            part = values
+            if step:
+                pairs = [(n, (n + step) % self.seq_size) for n in range(self.seq_size)]
+                part = lax.ppermute(values, "seq", pairs)
+            place = ((self.seq - step) % self.seq_size, 0, 0)
+            own = lax.dynamic_update_slice(own, part[None], place)
         full = self.gather_rest(
-            self.gather_own(values),
+            own,
             [(8, self.seq_size, rows, width)],
             lambda part, at: (0, (part, at)),
         )
@@ -377,9 +431,6 @@
     up_2 = take(up_fc2, 0)
     bias_1 = pad_blocks(hidden_bias, 0, seq_size, padded)
 
-    full_len = flat.shape[0]
-    heads = width // HD
-
     normed = layer_norm(flat, norm_gain[0], norm_bias[0]).astype(BF)
     normed, out_grad = lax.optimization_barrier((normed, out_grad))
     top_grad = place.to_image(out_grad).astype(F32) * live
@@ -393,19 +444,9 @@
     key_rows = projected[1].astype(BF)
     value_rows = (projected[2] + proj_bias[1]).astype(BF)
 
-    groups = 4
-
-    def split_heads(values):
-        values = values.reshape(full_len, groups, heads // groups, HD)
-        return values.transpose(1, 0, 2, 3)
-
-    def join_heads(values):
-        return values.transpose(1, 0, 2, 3).reshape(full_len, width)
-
-    split_q, split_k, split_v = split_heads(queries), split_heads(key_rows), split_heads(value_rows)
-    masks = jnp.broadcast_to(key_mask[None], (groups, full_len))
-    attended, log_total = lax.map(attend_heads, (split_q, split_k, split_v, masks))
-    merged = join_heads(attended).astype(BF)
+    turned = (queries.T, key_rows.T, value_rows.T, key_mask[:, None])
+    attended, log_total = attend(*turned)
+    merged = attended.T
     rank_out = product(merged, down_a[3]).astype(BF)
     resid = flat + product(merged, attn_full[3]) + product(rank_out, up_a[3]) + proj_bias[2]
     normed_two = layer_norm(resid, norm_gain[1], norm_bias[1]).astype(BF)
@@ -453,10 +494,7 @@
     early = place.gather_all(early)
     result = place.to_tokens(result, images)
 
-    grad_q, grad_k, grad_v = lax.map(
-        attend_back, (split_q, split_k, split_v, masks, log_total, split_heads(merged_grad))
-    )
-    proj_grads = (join_heads(grad_q), join_heads(grad_k), join_heads(grad_v))
+    proj_grads = [grad.T for grad in attend_grads(*turned, log_total, merged_grad.T)]
     normed_grad = 0.0
     late_parts = []
     for index in range(3):

time: 729 us -> 659 us (0.904)
  matrix products: 278 us -> 189 us
  Pallas kernels: 38.7 us -> 94 us
  blocking collectives: 51 us -> 0 us
  waiting for transfers between devices: 96.3 us -> 123 us
  other arithmetic: 53.6 us -> 33.8 us
  starting transfers between devices: 81.2 us -> 90.1 us
    dot_general x28 -> x0, matrix products: 79.6 us -> none  [the longest x4 16.8 us: attend_heads(): jnp.einsum('hqk,khd->qhd', attn_probs, value_rows, preferred_element_type...]
    pallas_call x0 -> x2, Pallas kernels: none -> 55.5 us  [the longest x1 34 us: attend_grads(): pl.pallas_call(body, grid=(pairs,), in_specs=[block, block, block, pl.Blo...]
    all_gather x2 -> x0, blocking collectives: 51 us -> none  [gather_own(): return lax.all_gather(piece, 'seq', axis=0)]
    ppermute x0 -> x6, waiting for transfers between devices: none -> 12.7 us  [gather_all(): part = lax.ppermute(values, 'seq', pairs)]
    add x0 -> x3, local copies, waits for them, and re-layouts: none -> 12.7 us  [local(): product(normed, attn_full[index]) + product(rank_part, up_a[index])]
    ppermute x6, waiting for transfers between devices: 6.79 us -> 18.5 us  [to_tokens(): part = lax.ppermute(part, ('dp', 'seq'), pairs)]
    reduce_sum x4 -> x0, other arithmetic: 9.08 us -> none  [attend_heads(): row_total = jnp.sum(exponent, axis=-1, keepdims=True)]
    dot_general x60, matrix products: 198 us -> 189 us  [dot(): lax.dot_general(left, right, (dims, ((), ())), preferred_element_type=F32)]
  transfers between devices with their start and end apart: 62 -> 68, of which waited for: 13 -> 22; matrix products, arithmetic and copies ran while one was open for 32% -> 34% of each run, Pallas kernels for 3% -> 11%
where the time goes in v4:
time: 659 us; the launch traced here: 648 us
  matrix products  189 us (29%)
  waiting for transfers between devices  123 us (19%)
  local copies, waits for them, and re-layouts  101 us (15%)
  Pallas kernels  94 us (14%)
  starting transfers between devices  90.1 us (14%)
  other arithmetic  33.8 us (5%)
  between operations  17.5 us (3%)
    dot_general x60, matrix products, dot(): lax.dot_general(left, right, (dims, ((), ())), preferred_element_type=F32)  189 us
    ppermute x45, waiting for transfers between devices, flip(): return lax.ppermute(values, 'dp', pairs)  55.8 us
    ppermute x6, waiting for transfers between devices, to_image(): part = lax.ppermute(part, ('dp', 'seq'), pairs)  34.7 us
    pallas_call x1, Pallas kernels, attend_grads(): pl.pallas_call(body, grid=(pairs,), in_specs=[block, block, block, pl.Blo...  34 us
    ppermute x45, starting transfers between devices, flip(): return lax.ppermute(values, 'dp', pairs)  32.7 us
    pallas_call x5, Pallas kernels, gather_rest(): pl.pallas_call(body, grid_spec=pltpu.PrefetchScalarGridSpec(num_scalar_pr...  30.7 us
    ppermute x6, starting transfers between devices, to_tokens(): part = lax.ppermute(part, ('dp', 'seq'), pairs)  25.4 us
    pallas_call x1, Pallas kernels, attend(): pl.pallas_call(body, grid=(pairs,), in_specs=[block, block, block, pl.Blo...  21.5 us
  transfers between devices with their start and end apart: 68, of which 22 were waited for; matrix products, arithmetic and copies ran while one was open for 34% of the time, Pallas kernels for 11%

profile of v4, /device:TPU:0, one launch (start us, length us, event | category | flops | bytes accessed | tf_op | source)
XLA Modules:
  0.0 648.2 jit_solution(11434307661743901790)
XLA Ops:
  40.9 16.3 %collective-permute-done = bf16[1,184,1152]{2,1,0:T(8,128)(2,1)} collective-permute-done((bf16[1,184,1152]{2,1,0:T(8,128)(2,1)}, bf16[1,184,1152]{2,1,0:T(8,128)(2,1)}, u32[]{:S(2)}, u32[]{:S(2)}) %collective-permute-start) | collective-permute-done | bytes 423968 | tf_op jit(solution)/shard_map/ppermute | solution.py:165
  59.0 12.1 %collective-permute-done.1 = bf16[1,184,1152]{2,1,0:T(8,128)(2,1)} collective-permute-done((bf16[1,184,1152]{2,1,0:T(8,128)(2,1)}, bf16[1,184,1152]{2,1,0:T(8,128)(2,1)}, u32[]{:S(2)}, u32[]{:S(2)}) %collective-permute-start.1) | collective-permute-done | bytes 423968 | tf_op jit(solution)/shard_map/ppermute | solution.py:165
  119.5 14.1 %collective-permute-done.7.refs_2_ = bf16[4,144,1152]{2,1,0:T(8,128)(2,1)} collective-permute-done((bf16[4,144,1152]{2,1,0:T(8,128)(2,1)}, bf16[4,144,1152]{2,1,0:T(8,128)(2,1)}, u32[]{:S(2)}, u32[]{:S(2)}) %collective-permute-start.7) | collective-permute-done | bytes 1327136 | tf_op jit(solution)/shard_map/ppermute | solution.py:149
  143.7 7.0 %collective-permute-done.9.refs_4_ = bf16[2,144,1152]{2,1,0:T(8,128)(2,1)} collective-permute-done((bf16[2,144,1152]{2,1,0:T(8,128)(2,1)S(1)}, bf16[2,144,1152]{2,1,0:T(8,128)(2,1)}, u32[]{:S(2)}, u32[]{:S(2)}) %collective-permute-start.9) | collective-permute-done | bytes 663584 | tf_op jit(solution)/shard_map/ppermute | solution.py:149
  165.5 8.1 %assemble.5 = (bf16[4,2,144,1152]{3,2,1,0:T(8,128)(2,1)}, bf16[4,2,144,1152]{3,2,1,0:T(8,128)(2,1)}, bf16[4,2,144,1152]{3,2,1,0:T(8,128)(2,1)}, bf16[4,2,144,1152]{3,2,1,0:T(8,128)(2,1)}) custom-call(s32[1]{0:T(128)} %bitcast.4.at_ref, bf16[4,144,1152]{2,1,0:T(8,128)(2,1)} %bitcast.6.refs_0_, bf16[4,144,1152]{2,1,0:T(8,128)(2,1)} %collective-permute-done.6.refs_1_, ...), custom_call_target="tpu_custom_call" | custom-call | tf_op jit(solution)/shard_map/assemble/pallas_call | solution.py:222
  208.2 21.5 %attend.1 = (bf16[1152,736]{1,0:T(8,128)(2,1)}, f32[8,2,736]{2,1,0:T(2,128)}) custom-call(bf16[1152,736]{1,0:T(8,128)(2,1)} %get-tuple-element.145.q_ref, bf16[1152,736]{1,0:T(8,128)(2,1)} %copy.83.k_ref, bf16[1152,736]{1,0:T(8,128)(2,1)} %get-tuple-element.144.v_ref, s32[736,1]{1,0:T(8,128)} %copy.85.mask_ref), custom_call_target="tpu_custom_call" | custom-call | tf_op jit(solution)/shard_map/attend/pallas_call | solution.py:75
  245.3 11.2 %collective-permute-done.18.refs_4_ = bf16[2,72,2176]{2,1,0:T(8,128)(2,1)} collective-permute-done((bf16[2,72,2176]{2,1,0:T(8,128)(2,1)S(1)}, bf16[2,72,2176]{2,1,0:T(8,128)(2,1)}, u32[]{:S(2)}, u32[]{:S(2)}) %collective-permute-start.18) | collective-permute-done | bytes 626720 | tf_op jit(solution)/shard_map/ppermute | solution.py:149
  268.3 7.8 %assemble.6 = (bf16[4,4,72,2176]{3,2,1,0:T(8,128)(2,1)}, bf16[4,4,72,2176]{3,2,1,0:T(8,128)(2,1)}) custom-call(s32[1]{0:T(128)} %bitcast.4.at_ref, bf16[4,72,2176]{2,1,0:T(8,128)(2,1)} %bitcast.229, bf16[4,72,2176]{2,1,0:T(8,128)(2,1)} %collective-permute-done.15.refs_1_, bf16[4,72,2176]{2,1,0:T(8,128)(2,1)} %collective-permute-done.16.refs_2_, ...), custom_call_target="tpu_custom_call" | custom-call | tf_op jit(solution)/shard_map/assemble/pallas_call | solution.py:222
  276.1 12.7 %multiply_convert_fusion = (bf16[736,2176]{1,0:T(8,128)(2,1)S(1)}, f32[736,2176]{1,0:T(8,128)}) fusion(f32[2176]{0:T(1024)} %add.485, f32[736,2176]{1,0:T(8,128)} %fusion.51, bf16[736,1152]{1,0:T(8,128)(2,1)} %copy-done.16, bf16[1152,2176]{1,0:T(8,128)(2,1)} %bitcast.241), kind=kOutput, calls=%fused_computation.19 | convolution fusion | flops 3707555840 | bytes 22733312 | tf_op jit(solution)/shard_map/dot_general | solution.py:17
  307.8 8.3 %collective-permute-done.27.refs_4_ = bf16[2,136,1152]{2,1,0:T(8,128)(2,1)} collective-permute-done((bf16[2,136,1152]{2,1,0:T(8,128)(2,1)S(1)}, bf16[2,136,1152]{2,1,0:T(8,128)(2,1)}, u32[]{:S(2)}, u32[]{:S(2)}) %collective-permute-start.27) | collective-permute-done | bytes 626720 | tf_op jit(solution)/shard_map/ppermute | solution.py:149
  326.7 7.7 %assemble.7 = bf16[4,8,136,1152]{3,2,1,0:T(8,128)(2,1)} custom-call(s32[1]{0:T(128)} %bitcast.4.at_ref, bf16[4,136,1152]{2,1,0:T(8,128)(2,1)} %bitcast.233, bf16[4,136,1152]{2,1,0:T(8,128)(2,1)} %collective-permute-done.24.refs_1_, bf16[4,136,1152]{2,1,0:T(8,128)(2,1)} %collective-permute-done.25.refs_2_, ...), custom_call_target="tpu_custom_call" | custom-call | tf_op jit(solution)/shard_map/assemble/pallas_call | solution.py:222
  334.4 8.5 %fusion.91 = (bf16[2,8,136,1152]{3,2,1,0:T(8,128)(2,1)}, bf16[2,8,136,1152]{3,2,1,0:T(8,128)(2,1)}) fusion(bf16[4,8,136,1152]{3,2,1,0:T(8,128)(2,1)} %assemble.7), kind=kLoop, calls=%fused_computation.235 | loop fusion | bytes 20054016 | tf_op jit(solution)/shard_map/slice | solution.py:469
  342.9 9.8 %fusion.97 = f32[736,1152]{1,0:T(8,128)} fusion(bf16[736,2176]{1,0:T(8,128)(2,1)} %copy-done.12, bf16[2176,1152]{1,0:T(8,128)(2,1)} %bitcast.216), kind=kOutput, calls=%fused_computation.241 | convolution fusion | flops 3689938944 | bytes 11608064 | tf_op jit(solution)/shard_map/dot_general | solution.py:17
  352.7 12.3 %fusion.13 = bf16[736,2176]{1,0:T(8,128)(2,1)S(1)} fusion(f32[736,2176]{1,0:T(8,128)} %get-tuple-element.139, f32[736,2176]{1,0:T(8,128)S(1)} %bitcast.210, bf16[736,1152]{1,0:T(8,128)(2,1)} %bitcast.224, bf16[2176,1152]{1,0:T(8,128)(2,1)} %bitcast.217), kind=kOutput, calls=%fused_computation.18 | convolution fusion | flops 3723571200 | bytes 22724608 | tf_op jit(solution)/shard_map/dot_general | solution.py:17
  365.0 10.0 %fusion.96 = f32[736,1152]{1,0:T(8,128)} fusion(bf16[736,2176]{1,0:T(8,128)(2,1)S(1)} %fusion.13, bf16[1152,2176]{1,0:T(8,128)(2,1)} %bitcast.242), kind=kOutput, calls=%fused_computation.240 | convolution fusion | flops 3689938944 | bytes 11608064 | tf_op jit(solution)/shard_map/dot_general | solution.py:17
  376.4 9.6 %fusion.6 = bf16[736,2176]{1,0:T(8,128)(2,1)S(1)} fusion(f32[736,2176]{1,0:T(8,128)} %get-tuple-element.141, f32[736,2176]{1,0:T(8,128)S(1)} %bitcast.208, bf16[736,1152]{1,0:T(8,128)(2,1)S(1)} %bitcast.225, bf16[2176,1152]{1,0:T(8,128)(2,1)S(1)} %bitcast.215), kind=kOutput, calls=%fused_computation.11 | convolution fusion | flops 3723571200 | bytes 22724608 | tf_op jit(solution)/shard_map/dot_general | solution.py:17
  398.0 7.5 %multiply_reduce_fusion.1 = (f32[736]{0:T(1024)S(1)}, f32[736,1152]{1,0:T(8,128)S(1)}) fusion(f32[736,1152]{1,0:T(8,128)S(1)} %get-tuple-element.137, f32[736]{0:T(1024)S(1)} %copy-done.81, f32[1152]{0:T(1024)S(1)} %copy-done.93, f32[736,1152]{1,0:T(8,128)S(1)} %fusion.44, f32[736,1152]{1,0:T(8,128)S(1)} %copy-done.110, ...), kind=kOutput, calls=%fused_computation.54 | convolution fusion | flops 3695025408 | bytes 21793024 | tf_op jit(solution)/shard_map/dot_general | solution.py:17
  421.6 7.2 %fusion.26 = bf16[736,1152]{0,1:T(8,128)(2,1)} fusion(f32[736,1152]{0,1:T(8,128)} %fusion.49, bf16[736,1152]{1,0:T(8,128)(2,1)} %copy-done.21, bf16[1152,1152]{1,0:T(8,128)(2,1)} %bitcast.249), kind=kOutput, calls=%fused_computation.60 | convolution fusion | flops 1955192832 | bytes 9437184 | tf_op jit(solution)/shard_map/dot_general | solution.py:17
  429.2 8.3 %fusion.27 = bf16[736,1152]{1,0:T(8,128)(2,1)} fusion(f32[736,1152]{1,0:T(8,128)S(1)} %copy-done.7, f32[736,1152]{1,0:T(8,128)S(1)} %copy-done.36, f32[736,1152]{1,0:T(8,128)S(1)} %copy-done.109, bf16[736,2176]{1,0:T(8,128)(2,1)S(1)} %copy-done.11, bf16[2176,1152]{1,0:T(8,128)(2,1)} %bitcast.214, f32[]{:T(128)S(6)} %convert_element_type.142, ...), kind=kOutput, calls=%fused_computation.65 | convolution fusion | flops 3695026176 | bytes 20091396 | tf_op jit(solution)/shard_map/dot_general | solution.py:17
  445.9 34.0 %attend_grads.1 = (bf16[1152,736]{1,0:T(8,128)(2,1)}, bf16[1152,736]{1,0:T(8,128)(2,1)}, bf16[1152,736]{1,0:T(8,128)(2,1)}) custom-call(bf16[1152,736]{1,0:T(8,128)(2,1)} %get-tuple-element.145.q_ref, bf16[1152,736]{1,0:T(8,128)(2,1)} %copy.83.k_ref, bf16[1152,736]{1,0:T(8,128)(2,1)} %get-tuple-element.144.v_ref, s32[736,1]{1,0:T(8,128)} %copy.85.mask_ref, ...), custom_call_target="tpu_custom_call" | custom-call | tf_op jit(solution)/shard_map/attend_grads/pallas_call | solution.py:116
  569.9 7.5 %collective-permute-done.38 = bf16[1,184,1152]{2,1,0:T(8,128)(2,1)} collective-permute-done((bf16[1,184,1152]{2,1,0:T(8,128)(2,1)}, bf16[1,184,1152]{2,1,0:T(8,128)(2,1)}, u32[]{:S(2)}, u32[]{:S(2)}) %collective-permute-start.38) | collective-permute-done | bytes 423968 | tf_op jit(solution)/shard_map/ppermute | solution.py:185
  577.4 9.7 %collective-permute-start.34 = (bf16[1,184,1152]{2,1,0:T(8,128)(2,1)}, bf16[1,184,1152]{2,1,0:T(8,128)(2,1)S(1)}, u32[]{:S(2)}, u32[]{:S(2)}) collective-permute-start(bf16[1,184,1152]{2,1,0:T(8,128)(2,1)} %get-tuple-element.119), channel_id=1, source_target_pairs={{0,2},{1,3},{2,0},{5,7},{6,4},{7,5},{8,10},{9,11},{10,8},{13,15},{... | collective-permute-start | bytes 1271816 | tf_op jit(solution)/shard_map/ppermute | solution.py:185
  587.2 11.0 %collective-permute-done.37 = bf16[1,184,1152]{2,1,0:T(8,128)(2,1)} collective-permute-done((bf16[1,184,1152]{2,1,0:T(8,128)(2,1)}, bf16[1,184,1152]{2,1,0:T(8,128)(2,1)}, u32[]{:S(2)}, u32[]{:S(2)}) %collective-permute-start.37) | collective-permute-done | bytes 423968 | tf_op jit(solution)/shard_map/ppermute | solution.py:185
  630.8 7.7 %write_grads.1 = (f32[4,1152,128]{2,1,0:T(8,128)}, f32[4,128,1152]{2,1,0:T(8,128)}, f32[1152,128]{1,0:T(8,128)}, f32[128,4304]{1,0:T(8,128)}, f32[4304,128]{1,0:T(8,128)}, /*index=5*/f32[128,1152]{1,0:T(8,128)}) custom-call(bf16[32,128,512]{2,1,0:T(8,128)(2,1)} %bitcast.211, bf16[32,128,256]{2,1,0:T(8,128)(2,1)} %bitcast.212), custom_call_target="tpu_custom_call" | custom-call | tf_op jit(solution)/shard_map/write_grads/pallas_call | solution.py:331
  (541 shorter events, 360.8 us)
Async XLA Ops:
  7.2 96.7 %all-gather.7.cloned.1.call-start = ((), (), s32[]{:S(2)}) async-start(), calls=%async_computation.2 | async-start | bytes 1658880 | tf_op jit(solution)/shard_map/all_gather | solution.py:191
  11.4 151.9 %all-gather.9.cloned.1.call-start = ((), (), s32[]{:S(2)}) async-start(), calls=%async_computation.3 | async-start | bytes 1566720 | tf_op jit(solution)/shard_map/all_gather | solution.py:191
  15.5 57.5 %collective-permute-start.2 = (bf16[1,184,1152]{2,1,0:T(8,128)(2,1)}, bf16[1,184,1152]{2,1,0:T(8,128)(2,1)}, u32[]{:S(2)}, u32[]{:S(2)}) collective-permute-start(bf16[1,184,1152]{2,1,0:T(8,128)(2,1)} %get-tuple-element.128), channel_id=1, source_target_pairs={{1,0},{2,1},{3,2},{4,7},{6,5},{7,6},{9,8},{10,9},{11,10},{12,15},{... | collective-permute-start | bytes 1271816 | tf_op jit(solution)/shard_map/ppermute | solution.py:165
  16.8 40.5 %collective-permute-start = (bf16[1,184,1152]{2,1,0:T(8,128)(2,1)}, bf16[1,184,1152]{2,1,0:T(8,128)(2,1)}, u32[]{:S(2)}, u32[]{:S(2)}) collective-permute-start(bf16[1,184,1152]{2,1,0:T(8,128)(2,1)} %get-tuple-element.129), channel_id=1, source_target_pairs={{0,1},{1,2},{3,0},{4,5},{5,6},{6,7},{8,9},{9,10},{11,8},{12,13},{1... | collective-permute-start | bytes 1271816 | tf_op jit(solution)/shard_map/ppermute | solution.py:165
  22.4 48.8 %collective-permute-start.1 = (bf16[1,184,1152]{2,1,0:T(8,128)(2,1)}, bf16[1,184,1152]{2,1,0:T(8,128)(2,1)}, u32[]{:S(2)}, u32[]{:S(2)}) collective-permute-start(bf16[1,184,1152]{2,1,0:T(8,128)(2,1)} %get-tuple-element.131), channel_id=1, source_target_pairs={{0,2},{2,0},{3,1},{4,6},{5,7},{7,5},{8,10},{10,8},{11,9},{12,14},{... | collective-permute-start | bytes 1271816 | tf_op jit(solution)/shard_map/ppermute | solution.py:165
  84.6 31.6 %collective-permute-start.5 = (bf16[1,184,1152]{2,1,0:T(8,128)(2,1)}, bf16[1,184,1152]{2,1,0:T(8,128)(2,1)}, u32[]{:S(2)}, u32[]{:S(2)}) collective-permute-start(bf16[1,184,1152]{2,1,0:T(8,128)(2,1)} %get-tuple-element.124), channel_id=1, source_target_pairs={{1,0},{2,1},{3,2},{4,7},{6,5},{7,6},{9,8},{10,9},{11,10},{12,15},{... | collective-permute-start | bytes 1271816 | tf_op jit(solution)/shard_map/ppermute | solution.py:165
  105.4 31.2 %collective-permute-start.6 = (bf16[4,144,1152]{2,1,0:T(8,128)(2,1)}, bf16[4,144,1152]{2,1,0:T(8,128)(2,1)}, u32[]{:S(2)}, u32[]{:S(2)}) collective-permute-start(bf16[4,144,1152]{2,1,0:T(8,128)(2,1)} %bitcast.6.refs_0_), channel_id=1, source_target_pairs={{0,8},{4,12},{8,0},{12,4},{16,24},{20,28},{24,16},{28,20},{1,9},{5... | collective-permute-start | bytes 3981320 | tf_op jit(solution)/shard_map/ppermute | solution.py:149
  117.3 149.4 %all-gather.11.cloned.1.call-start = ((), (), s32[]{:S(2)}) async-start(), calls=%async_computation.4 | async-start | bytes 1566720 | tf_op jit(solution)/shard_map/all_gather | solution.py:191
  119.5 43.7 %collective-permute-start.10 = (bf16[4,144,1152]{2,1,0:T(8,128)(2,1)}, bf16[4,144,1152]{2,1,0:T(8,128)(2,1)S(1)}, u32[]{:S(2)}, u32[]{:S(2)}) collective-permute-start(bf16[4,144,1152]{2,1,0:T(8,128)(2,1)} %bitcast.6.refs_0_), channel_id=1, source_target_pairs={{0,4},{4,0},{8,12},{12,8},{16,20},{20,16},{24,28},{28,24},{1,5},{5... | collective-permute-start | bytes 3981320 | tf_op jit(solution)/shard_map/ppermute | solution.py:149
  163.3 103.4 %collective-permute-start.19 = (bf16[4,72,2176]{2,1,0:T(8,128)(2,1)}, bf16[4,72,2176]{2,1,0:T(8,128)(2,1)}, u32[]{:S(2)}, u32[]{:S(2)}) collective-permute-start(bf16[4,72,2176]{2,1,0:T(8,128)(2,1)} %bitcast.226), channel_id=1, source_target_pairs={{0,4},{4,0},{8,12},{12,8},{16,20},{20,16},{24,28},{28,24},{1,5},{5... | collective-permute-start | bytes 3760136 | tf_op jit(solution)/shard_map/ppermute | solution.py:149
  163.4 75.2 %collective-permute-start.16 = (bf16[4,72,2176]{2,1,0:T(8,128)(2,1)}, bf16[4,72,2176]{2,1,0:T(8,128)(2,1)}, u32[]{:S(2)}, u32[]{:S(2)}) collective-permute-start(bf16[4,72,2176]{2,1,0:T(8,128)(2,1)} %bitcast.227), channel_id=1, source_target_pairs={{0,16},{4,20},{8,24},{12,28},{16,0},{20,4},{24,8},{28,12},{1,17},{... | collective-permute-start | bytes 3760136 | tf_op jit(solution)/shard_map/ppermute | solution.py:149
  165.5 76.8 %collective-permute-start.15 = (bf16[4,72,2176]{2,1,0:T(8,128)(2,1)}, bf16[4,72,2176]{2,1,0:T(8,128)(2,1)}, u32[]{:S(2)}, u32[]{:S(2)}) collective-permute-start(bf16[4,72,2176]{2,1,0:T(8,128)(2,1)} %bitcast.228), channel_id=1, source_target_pairs={{0,8},{4,12},{8,0},{12,4},{16,24},{20,28},{24,16},{28,20},{1,9},{5... | collective-permute-start | bytes 3760136 | tf_op jit(solution)/shard_map/ppermute | solution.py:149
  266.7 59.9 %collective-permute-start.28 = (bf16[4,136,1152]{2,1,0:T(8,128)(2,1)}, bf16[4,136,1152]{2,1,0:T(8,128)(2,1)}, u32[]{:S(2)}, u32[]{:S(2)}) collective-permute-start(bf16[4,136,1152]{2,1,0:T(8,128)(2,1)} %bitcast.230), channel_id=1, source_target_pairs={{0,4},{4,0},{8,12},{12,8},{16,20},{20,16},{24,28},{28,24},{1,5},{5... | collective-permute-start | bytes 3760136 | tf_op jit(solution)/shard_map/ppermute | solution.py:149
  267.2 31.7 %collective-permute-start.25 = (bf16[4,136,1152]{2,1,0:T(8,128)(2,1)}, bf16[4,136,1152]{2,1,0:T(8,128)(2,1)}, u32[]{:S(2)}, u32[]{:S(2)}) collective-permute-start(bf16[4,136,1152]{2,1,0:T(8,128)(2,1)} %bitcast.231), channel_id=1, source_target_pairs={{0,16},{4,20},{8,24},{12,28},{16,0},{20,4},{24,8},{28,12},{1,17},{... | collective-permute-start | bytes 3760136 | tf_op jit(solution)/shard_map/ppermute | solution.py:149
  267.5 34.3 %collective-permute-start.24 = (bf16[4,136,1152]{2,1,0:T(8,128)(2,1)}, bf16[4,136,1152]{2,1,0:T(8,128)(2,1)}, u32[]{:S(2)}, u32[]{:S(2)}) collective-permute-start(bf16[4,136,1152]{2,1,0:T(8,128)(2,1)} %bitcast.232), channel_id=1, source_target_pairs={{0,8},{4,12},{8,0},{12,4},{16,24},{20,28},{24,16},{28,20},{1,9},{5... | collective-permute-start | bytes 3760136 | tf_op jit(solution)/shard_map/ppermute | solution.py:149
  441.6 100.8 %collective-permute-start.41 = (bf16[128,512]{1,0:T(8,128)(2,1)}, bf16[128,512]{1,0:T(8,128)(2,1)S(1)}, u32[]{:S(2)}, u32[]{:S(2)}) collective-permute-start(bf16[128,512]{1,0:T(8,128)(2,1)} %reshape.216), channel_id=1, source_target_pairs={{0,3},{1,0},{2,1},{3,2},{4,7},{5,4},{6,5},{7,6},{8,11},{9,8},{10,9... | collective-permute-start | bytes 393224 | tf_op jit(solution)/shard_map/ppermute | solution.py:244
  444.7 96.7 %collective-permute-start.40 = (bf16[128,512]{1,0:T(8,128)(2,1)}, bf16[128,512]{1,0:T(8,128)(2,1)}, u32[]{:S(2)}, u32[]{:S(2)}) collective-permute-start(bf16[128,512]{1,0:T(8,128)(2,1)} %reshape.216), channel_id=1, source_target_pairs={{0,2},{1,3},{2,0},{3,1},{4,6},{5,7},{6,4},{7,5},{8,10},{9,11},{10,... | collective-permute-start | bytes 393224 | tf_op jit(solution)/shard_map/ppermute | solution.py:244
  445.8 94.6 %collective-permute-start.39 = (bf16[128,512]{1,0:T(8,128)(2,1)}, bf16[128,512]{1,0:T(8,128)(2,1)}, u32[]{:S(2)}, u32[]{:S(2)}) collective-permute-start(bf16[128,512]{1,0:T(8,128)(2,1)} %reshape.216), channel_id=1, source_target_pairs={{0,1},{1,2},{2,3},{3,0},{4,5},{5,6},{6,7},{7,4},{8,9},{9,10},{10,1... | collective-permute-start | bytes 393224 | tf_op jit(solution)/shard_map/ppermute | solution.py:244
  502.0 43.4 %all-to-all-start.1 = ((bf16[32,16,256]{2,1,0:T(8,128)(2,1)}), bf16[32,16,256]{2,1,0:T(8,128)(2,1)}, u32[]{:S(2)}, u32[]{:S(2)}) async-start(bf16[32,16,256]{2,1,0:T(8,128)(2,1)} %bitcast.235), calls=%async_computation.1 | async-start | bytes 524288 | tf_op jit(solution)/shard_map/all_to_all | solution.py:288
  510.5 49.8 %collective-permute-start.35 = (bf16[1,184,1152]{2,1,0:T(8,128)(2,1)}, bf16[1,184,1152]{2,1,0:T(8,128)(2,1)}, u32[]{:S(2)}, u32[]{:S(2)}) collective-permute-start(bf16[1,184,1152]{2,1,0:T(8,128)(2,1)} %get-tuple-element.118), channel_id=1, source_target_pairs={{0,3},{1,0},{2,1},{5,4},{6,5},{7,6},{8,11},{9,8},{10,9},{13,12},{1... | collective-permute-start | bytes 1271816 | tf_op jit(solution)/shard_map/ppermute | solution.py:185
  543.9 55.8 %collective-permute-start.42 = (bf16[4,128,512]{2,1,0:T(8,128)(2,1)S(1)}, bf16[4,128,512]{2,1,0:T(8,128)(2,1)S(1)}, u32[]{:S(2)}, u32[]{:S(2)}) collective-permute-start(bf16[4,128,512]{2,1,0:T(8,128)(2,1)S(1)} %bitcast_dynamic-update-slice_fusion.refs_0_), channel_id=1, source_target_pairs={{0,8},{4,12},{8,0},{12,4},{16,24},{20,28},{24,16},{28,20},{1,9},{5... | collective-permute-start | bytes 1572872 | tf_op jit(solution)/shard_map/ppermute | solution.py:149
  565.5 32.7 %collective-permute-start.37 = (bf16[1,184,1152]{2,1,0:T(8,128)(2,1)}, bf16[1,184,1152]{2,1,0:T(8,128)(2,1)}, u32[]{:S(2)}, u32[]{:S(2)}) collective-permute-start(bf16[1,184,1152]{2,1,0:T(8,128)(2,1)} %get-tuple-element.115), channel_id=1, source_target_pairs={{0,2},{1,3},{2,0},{5,7},{6,4},{7,5},{8,10},{9,11},{10,8},{13,15},{... | collective-permute-start | bytes 1271816 | tf_op jit(solution)/shard_map/ppermute | solution.py:185
  568.4 31.4 %collective-permute-start.55 = (bf16[4,128,256]{2,1,0:T(8,128)(2,1)S(1)}, bf16[4,128,256]{2,1,0:T(8,128)(2,1)}, u32[]{:S(2)}, u32[]{:S(2)}) collective-permute-start(bf16[4,128,256]{2,1,0:T(8,128)(2,1)S(1)} %bitcast_dynamic-update-slice_fusion.4.refs_0_), channel_id=1, source_target_pairs={{0,16},{4,20},{8,24},{12,28},{16,0},{20,4},{24,8},{28,12},{1,17},{... | collective-permute-start | bytes 786440 | tf_op jit(solution)/shard_map/ppermute | solution.py:149
  568.5 33.9 %collective-permute-start.54 = (bf16[4,128,256]{2,1,0:T(8,128)(2,1)S(1)}, bf16[4,128,256]{2,1,0:T(8,128)(2,1)S(1)}, u32[]{:S(2)}, u32[]{:S(2)}) collective-permute-start(bf16[4,128,256]{2,1,0:T(8,128)(2,1)S(1)} %bitcast_dynamic-update-slice_fusion.4.refs_0_), channel_id=1, source_target_pairs={{0,8},{4,12},{8,0},{12,4},{16,24},{20,28},{24,16},{28,20},{1,9},{5... | collective-permute-start | bytes 786440 | tf_op jit(solution)/shard_map/ppermute | solution.py:149
  (159 other events, 2373.4 us)
Sparse Core Ops, SparseCore 0:
  11.5 57.6 all-gather.6
  117.4 35.8 all-gather.8
  163.4 31.8 all-gather.10

commit v5 on v4

--- a/solution.py
+++ b/solution.py
@@ -42,10 +42,6 @@
         return layer_norm(inner_values, gain, shift)
 
     return jax.vjp(local_norm, values)[1](grad)[0]
-
-
-def gelu_tanh(values):
-    return jax.nn.gelu(values, approximate=True)
 
 
 def masked_scores(key_rows, queries, mask):
@@ -128,6 +124,94 @@
         out_shape=[jax.ShapeDtypeStruct((width, length), BF)] * 3,
         name="attend_grads",
     )(queries, key_rows, value_rows, mask, log_total, grad_out)
+
+
+def run_mlp(normed, top_grad, rank_one, inner_two, weights, bias):
+    first, second, up, down = weights
+    length, width = normed.shape
+    rank, total = up.shape
+    size = 256
+    steps = total // size
+    scale = (2.0 / jnp.pi) ** 0.5
+
+    def body(
+        normed_ref, grad_ref, rank_ref, inner_ref, rank_t_ref, inner_t_ref,
+        first_ref, second_ref, up_ref, down_ref, bias_ref,
+        branch_ref, rank_two_ref, back_ref, inner_one_ref, down_grad_ref, up_grad_ref,
+    ):
+        first, second, up, down = first_ref[...], second_ref[...], up_ref[...], down_ref[...]
+        hidden = dot(normed_ref[...], first, ((1,), (0,))) + bias_ref[...]
+        hidden = hidden + dot(rank_ref[...], up, ((1,), (0,)))
+        act_grad = dot(grad_ref[...], second, ((1,), (1,)))
+        act_grad = act_grad + dot(inner_ref[...], down, ((1,), (0,)))
+        square = hidden * hidden
+        bent = jnp.tanh(scale * hidden * (1.0 + 0.044715 * square))
+        side = 0.5 * (1.0 + bent)
+        activated = (hidden * side).astype(BF)
+        slope = side + 0.5 * hidden * (1.0 - bent * bent) * (scale * (1.0 + 0.134145 * square))
+        hidden_grad = (act_grad * slope).astype(BF)
+        down_grad_ref[...] = dot(inner_t_ref[...], activated, ((1,), (0,)))
+        up_grad_ref[...] = dot(rank_t_ref[...], hidden_grad, ((1,), (0,)))
+        sums = (
+            (branch_ref, dot(activated, second, ((1,), (0,)))),
+            (rank_two_ref, dot(activated, down, ((1,), (1,)))),
+            (back_ref, dot(hidden_grad, first, ((1,), (1,)))),
+            (inner_one_ref, dot(hidden_grad, up, ((1,), (1,)))),
+        )
+
+        @pl.when(pl.program_id(0) == 0)
+        def _():
+            for ref, value in sums:
+                ref[...] = value
+
+        @pl.when(pl.program_id(0) > 0)
+        def _():
+            for ref, value in sums:
+                ref[...] += value
+
+    def whole(rows, cols):
+        return pl.BlockSpec((rows, cols), lambda n: (0, 0))
+
+    def tile(rows):
+        return pl.BlockSpec((rows, size), lambda n: (0, n))
+
+    return pl.pallas_call(
+        body,
+        grid=(steps,),
+        in_specs=[
+            whole(length, width),
+            whole(length, width),
+            whole(length, rank),
+            whole(length, rank),
+            whole(rank, length),
+            whole(rank, length),
+            tile(width),
+            pl.BlockSpec((size, width), lambda n: (n, 0)),
+            tile(rank),
+            tile(rank),
+            tile(1),
+        ],
+        out_specs=[
+            whole(length, width),
+            whole(length, rank),
+            whole(length, width),
+            whole(length, rank),
+            tile(rank),
+            tile(rank),
+        ],
+        out_shape=[
+            jax.ShapeDtypeStruct((length, width), F32),
+            jax.ShapeDtypeStruct((length, rank), F32),
+            jax.ShapeDtypeStruct((length, width), F32),
+            jax.ShapeDtypeStruct((length, rank), F32),
+            jax.ShapeDtypeStruct((rank, total), F32),
+            jax.ShapeDtypeStruct((rank, total), F32),
+        ],
+        name="run_mlp",
+    )(
+        normed, top_grad, rank_one, inner_two, rank_one.T, inner_two.T,
+        first, second, up, down, bias[None],
+    )
 
 
 class Place:
@@ -410,15 +494,17 @@
     side = hidden_pad // 2
     fc1_full = place.gather_rest(
         fc1_own,
-        [(seq_size, 4, quarter, side)] * 2,
-        lambda part, at: (part % 2, (at, part // 2)),
-    )
-    fc1_full = [values.reshape(width, side) for values in fc1_full]
+        [(seq_size, 4, quarter, hidden_pad)],
+        lambda part, at: (
+            0,
+            (at, part // 2, slice(None), pl.ds(pl.multiple_of(part % 2 * side, 128), side)),
+        ),
+    )[0].reshape(width, hidden_pad)
     fc2_full = place.gather_rest(
         fc2_own,
         [(seq_size, 8, padded // 8, width)],
         lambda part, at: (0, (at, part)),
-    )[0].reshape(2, side, width)
+    )[0].reshape(hidden_pad, width)
 
     def take(values, axis):
         return lax.dynamic_slice_in_dim(values, adapter * RANK, RANK, axis=axis)
@@ -453,31 +539,16 @@
     rank_one = product(normed_two, down_1).astype(BF)
     two_grad = top_grad.astype(BF)
     inner_two = product_back(two_grad, up_2).astype(BF)
-    branch_two = proj_bias[3]
-    rank_two = 0.0
-    inner_one = 0.0
-    normed_two_grad = 0.0
-    down_2_halves = []
-    up_1_halves = []
-    for index in range(2):
-        at = slice(index * side, (index + 1) * side)
-        hidden = product(normed_two, fc1_full[index]) + product(rank_one, up_1[:, at]) + bias_1[at]
-        activated = gelu_tanh(hidden).astype(BF)
-        rank_two = rank_two + product(activated, down_2[at])
-        branch_two = branch_two + product(activated, fc2_full[index])
-        down_2_halves.append(outer_sum(inner_two, activated))
-        act_grad = product_back(two_grad, fc2_full[index]) + product_back(inner_two, down_2[at])
-        hidden_grad = jax.vjp(gelu_tanh, hidden)[1](act_grad)[0].astype(BF)
-        inner_one = inner_one + product_back(hidden_grad, up_1[:, at])
-        up_1_halves.append(outer_sum(rank_one, hidden_grad))
-        normed_two_grad = normed_two_grad + product_back(hidden_grad, fc1_full[index])
+    branch_two, rank_two, normed_two_grad, inner_one, down_2_grad, up_1_grad = run_mlp(
+        normed_two, two_grad, rank_one, inner_two, (fc1_full, fc2_full, up_1, down_2.T), bias_1
+    )
     rank_two = rank_two.astype(BF)
-    branch_two = branch_two + product(rank_two, up_2)
+    branch_two = branch_two + product(rank_two, up_2) + proj_bias[3]
     result = ((resid + branch_two) * live).astype(BF)
     up_2_grad = outer_sum(rank_two, two_grad)
-    down_2_grad = cut_blocks(jnp.concatenate(down_2_halves, axis=1), 1, seq_size, shard)
+    down_2_grad = cut_blocks(down_2_grad, 1, seq_size, shard)
     inner_one = inner_one.astype(BF)
-    up_1_grad = cut_blocks(jnp.concatenate(up_1_halves, axis=1), 1, seq_size, shard)
+    up_1_grad = cut_blocks(up_1_grad, 1, seq_size, shard)
     down_1_grad = outer_sum(inner_one, normed_two)
     normed_two_grad = normed_two_grad + product_back(inner_one, down_1)
     resid_grad = top_grad + norm_back(resid, norm_gain[1], norm_bias[1], normed_two_grad)

time: 659 us -> 615 us (0.933)
  matrix products: 189 us -> 91.4 us
  Pallas kernels: 94 us -> 164 us
  waiting for transfers between devices: 123 us -> 92.9 us
  starting transfers between devices: 90.1 us -> 103 us
    dot_general x60 -> x40, matrix products: 189 us -> 91.4 us  [dot(): lax.dot_general(left, right, (dims, ((), ())), preferred_element_type=F32)]
    pallas_call x0 -> x1, Pallas kernels: none -> 70.2 us  [run_mlp(): pl.pallas_call(body, grid=(steps,), in_specs=[whole(length, width), whole...]
    ppermute x6, waiting for transfers between devices: 18.5 us -> 3.96 us  [to_tokens(): part = lax.ppermute(part, ('dp', 'seq'), pairs)]
    ppermute x6, starting transfers between devices: 5.15 us -> 17.8 us  [gather_all(): part = lax.ppermute(values, 'seq', pairs)]
    slice x6 -> x1, local copies, waits for them, and re-layouts: 9.5 us -> 0.05 us  [local(): branch_two = branch_two + product(rank_two, up_2) + proj_bias[3]]
    all_to_all x2, waiting for transfers between devices: 0.8 us -> 9.73 us  [exchange(): lax.all_to_all(pieces, ('dp', 'seq'), split_axis=0, concat_axis=0, tiled=...]
    ppermute x45, waiting for transfers between devices: 55.8 us -> 46.9 us  [flip(): return lax.ppermute(values, 'dp', pairs)]
    ppermute x6, waiting for transfers between devices: 34.7 us -> 26.6 us  [to_image(): part = lax.ppermute(part, ('dp', 'seq'), pairs)]
  transfers between devices with their start and end apart: 68 -> 68, of which waited for: 22 -> 14; matrix products, arithmetic and copies ran while one was open for 34% -> 30% of each run, Pallas kernels for 11% -> 12%
where the time goes in v5:
time: 615 us; the launch traced here: 605 us
  Pallas kernels  164 us (27%)
  starting transfers between devices  103 us (17%)
  local copies, waits for them, and re-layouts  95.5 us (16%)
  waiting for transfers between devices  92.9 us (15%)
  matrix products  91.4 us (15%)
  other arithmetic  40.3 us (7%)
  between operations  17.2 us (3%)
    dot_general x40, matrix products, dot(): lax.dot_general(left, right, (dims, ((), ())), preferred_element_type=F32)  91.4 us
    pallas_call x1, Pallas kernels, run_mlp(): pl.pallas_call(body, grid=(steps,), in_specs=[whole(length, width), whole...  70.2 us
    ppermute x45, waiting for transfers between devices, flip(): return lax.ppermute(values, 'dp', pairs)  46.9 us
    ppermute x45, starting transfers between devices, flip(): return lax.ppermute(values, 'dp', pairs)  36.8 us
    pallas_call x1, Pallas kernels, attend_grads(): pl.pallas_call(body, grid=(pairs,), in_specs=[block, block, block, pl.Blo...  34 us
    pallas_call x5, Pallas kernels, gather_rest(): pl.pallas_call(body, grid_spec=pltpu.PrefetchScalarGridSpec(num_scalar_pr...  30.8 us
    ppermute x6, waiting for transfers between devices, to_image(): part = lax.ppermute(part, ('dp', 'seq'), pairs)  26.6 us
    ppermute x6, starting transfers between devices, to_tokens(): part = lax.ppermute(part, ('dp', 'seq'), pairs)  22.6 us
  transfers between devices with their start and end apart: 68, of which 14 were waited for; matrix products, arithmetic and copies ran while one was open for 30% of the time, Pallas kernels for 12%

profile of v5, /device:TPU:0, one launch (start us, length us, event | category | flops | bytes accessed | tf_op | source)
XLA Modules:
  0.0 605.1 jit_solution(12231016723396007253)
XLA Ops:
  37.5 25.8 %collective-permute-done.1 = bf16[1,184,1152]{2,1,0:T(8,128)(2,1)} collective-permute-done((bf16[1,184,1152]{2,1,0:T(8,128)(2,1)}, bf16[1,184,1152]{2,1,0:T(8,128)(2,1)}, u32[]{:S(2)}, u32[]{:S(2)}) %collective-permute-start.1) | collective-permute-done | bytes 423968 | tf_op jit(solution)/shard_map/ppermute | solution.py:249
  77.8 7.8 %collective-permute-start.12 = (bf16[1,184,1152]{2,1,0:T(8,128)(2,1)}, bf16[1,184,1152]{2,1,0:T(8,128)(2,1)}, u32[]{:S(2)}, u32[]{:S(2)}) collective-permute-start(bf16[1,184,1152]{2,1,0:T(8,128)(2,1)} %get-tuple-element.132), channel_id=1, source_target_pairs={{0,1},{1,2},{3,0},{4,5},{5,6},{6,7},{8,9},{9,10},{11,8},{12,13},{1... | collective-permute-start | bytes 1271816 | tf_op jit(solution)/shard_map/ppermute | solution.py:249
  112.8 11.1 %collective-permute-done.3.refs_1_ = bf16[4,144,1152]{2,1,0:T(8,128)(2,1)} collective-permute-done((bf16[4,144,1152]{2,1,0:T(8,128)(2,1)}, bf16[4,144,1152]{2,1,0:T(8,128)(2,1)}, u32[]{:S(2)}, u32[]{:S(2)}) %collective-permute-start.3) | collective-permute-done | bytes 1327136 | tf_op jit(solution)/shard_map/ppermute | solution.py:233
  133.3 8.5 %collective-permute-done.5.refs_3_ = bf16[2,144,1152]{2,1,0:T(8,128)(2,1)} collective-permute-done((bf16[2,144,1152]{2,1,0:T(8,128)(2,1)S(1)}, bf16[2,144,1152]{2,1,0:T(8,128)(2,1)}, u32[]{:S(2)}, u32[]{:S(2)}) %collective-permute-start.5) | collective-permute-done | bytes 663584 | tf_op jit(solution)/shard_map/ppermute | solution.py:233
  153.4 8.2 %assemble.5 = (bf16[4,2,144,1152]{3,2,1,0:T(8,128)(2,1)}, bf16[4,2,144,1152]{3,2,1,0:T(8,128)(2,1)}, bf16[4,2,144,1152]{3,2,1,0:T(8,128)(2,1)}, bf16[4,2,144,1152]{3,2,1,0:T(8,128)(2,1)}) custom-call(s32[1]{0:T(128)} %bitcast.1.at_ref, bf16[4,144,1152]{2,1,0:T(8,128)(2,1)} %bitcast.179, bf16[4,144,1152]{2,1,0:T(8,128)(2,1)} %collective-permute-done.3.refs_1_, ...), custom_call_target="tpu_custom_call" | custom-call | tf_op jit(solution)/shard_map/assemble/pallas_call | solution.py:306
  161.6 6.5 %convolution_add_fusion.3 = f32[1152,736]{0,1:T(8,128)} fusion(f32[1152,736]{0,1:T(8,128)} %fusion.31, bf16[736,1152]{1,0:T(8,128)(2,1)S(1)} %get-tuple-element.40, bf16[1152,1152]{1,0:T(8,128)(2,1)} %bitcast.193), kind=kOutput, calls=%fused_computation.7 | convolution fusion | flops 1954344960 | bytes 11132928 | tf_op jit(solution)/shard_map/dot_general | solution.py:17
  182.8 5.3 add_convert_fusion
  195.1 5.9 convolution_add_fusion.2
  204.9 21.7 %attend.1 = (bf16[1152,736]{1,0:T(8,128)(2,1)}, f32[8,2,736]{2,1,0:T(2,128)}) custom-call(bf16[1152,736]{1,0:T(8,128)(2,1)} %get-tuple-element.141.q_ref, bf16[1152,736]{1,0:T(8,128)(2,1)} %copy.91.k_ref, bf16[1152,736]{1,0:T(8,128)(2,1)} %get-tuple-element.140.v_ref, s32[736,1]{1,0:T(8,128)} %copy.93.mask_ref), custom_call_target="tpu_custom_call" | custom-call | tf_op jit(solution)/shard_map/attend/pallas_call | solution.py:71
  230.8 5.7 collective-permute-done.24.refs_1_
  246.6 14.0 %collective-permute-done.26.refs_3_ = bf16[2,136,1152]{2,1,0:T(8,128)(2,1)} collective-permute-done((bf16[2,136,1152]{2,1,0:T(8,128)(2,1)S(1)}, bf16[2,136,1152]{2,1,0:T(8,128)(2,1)}, u32[]{:S(2)}, u32[]{:S(2)}) %collective-permute-start.26) | collective-permute-done | bytes 626720 | tf_op jit(solution)/shard_map/ppermute | solution.py:233
  263.6 7.8 %assemble.6 = bf16[4,4,72,4352]{3,2,1,0:T(8,128)(2,1)} custom-call(s32[1]{0:T(128)} %bitcast.1.at_ref, bf16[4,72,2176]{2,1,0:T(8,128)(2,1)} %bitcast.183, bf16[4,72,2176]{2,1,0:T(8,128)(2,1)} %copy-done.24, bf16[4,72,2176]{2,1,0:T(8,128)(2,1)} %collective-permute-done.16.refs_2_, bf16[2,72,2176]{2,1,0:T(8,128)(2,1)} %collective-permute-done.17.refs_3_, ...), custom_call_target="tpu_custom_call" | custom-call | tf_op jit(solution)/shard_map/assemble/pallas_call | solution.py:306
  271.4 7.8 %assemble.7 = bf16[4,8,136,1152]{3,2,1,0:T(8,128)(2,1)} custom-call(s32[1]{0:T(128)} %bitcast.1.at_ref, bf16[4,136,1152]{2,1,0:T(8,128)(2,1)} %bitcast.24.refs_0_, bf16[4,136,1152]{2,1,0:T(8,128)(2,1)} %collective-permute-done.24.refs_1_, bf16[4,136,1152]{2,1,0:T(8,128)(2,1)} %collective-permute-done.25.refs_2_, ...), custom_call_target="tpu_custom_call" | custom-call | tf_op jit(solution)/shard_map/assemble/pallas_call | solution.py:306
  279.2 70.2 %run_mlp.1 = (f32[736,1152]{1,0:T(8,128)}, f32[736,16]{1,0:T(8,128)}, f32[736,1152]{1,0:T(8,128)}, f32[736,16]{1,0:T(8,128)}, f32[16,4352]{1,0:T(8,128)}, /*index=5*/f32[16,4352]{1,0:T(8,128)}) custom-call(bf16[736,1152]{1,0:T(8,128)(2,1)} %copy-done.8, bf16[736,1152]{1,0:T(8,128)(2,1)} %bitcast_convert_fusion.grad_ref, bf16[736,16]{1,0:T(8,128)(2,1)} %copy.96.rank_ref, ...), custom_call_target="tpu_custom_call" | custom-call | tf_op jit(solution)/shard_map/run_mlp/pallas_call | solution.py:178
  353.2 5.3 multiply_convert_fusion
  384.3 5.6 fusion.6
  389.9 9.7 %all-to-all-done = bf16[32,16,640]{2,1,0:T(8,128)(2,1)S(1)} async-done(((bf16[32,16,640]{2,1,0:T(8,128)(2,1)}), bf16[32,16,640]{2,1,0:T(8,128)(2,1)S(1)}, u32[]{:S(2)}, u32[]{:S(2)}) %all-to-all-start) | async-done | bytes 655392 | tf_op jit(solution)/shard_map/all_to_all | solution.py:372
  408.0 34.0 %attend_grads.1 = (bf16[1152,736]{1,0:T(8,128)(2,1)}, bf16[1152,736]{1,0:T(8,128)(2,1)}, bf16[1152,736]{1,0:T(8,128)(2,1)}) custom-call(bf16[1152,736]{1,0:T(8,128)(2,1)} %get-tuple-element.141.q_ref, bf16[1152,736]{1,0:T(8,128)(2,1)} %copy.91.k_ref, bf16[1152,736]{1,0:T(8,128)(2,1)} %get-tuple-element.140.v_ref, s32[736,1]{1,0:T(8,128)} %copy.93.mask_ref, ...), custom_call_target="tpu_custom_call" | custom-call | tf_op jit(solution)/shard_map/attend_grads/pallas_call | solution.py:112
  444.0 6.4 %fusion.65 = f32[736,1152]{1,0:T(8,128)} fusion(bf16[1152,736]{1,0:T(8,128)(2,1)S(1)} %copy-done.17, bf16[1152,1152]{1,0:T(8,128)(2,1)} %bitcast.196), kind=kOutput, calls=%fused_computation.189 | convolution fusion | flops 1953497088 | bytes 7741440 | tf_op jit(solution)/shard_map/dot_general | solution.py:17
  469.0 8.1 %fusion.3 = f32[736,1152]{1,0:T(8,128)S(1)} fusion(f32[736,1152]{1,0:T(8,128)} %fusion.23, f32[736,1152]{1,0:T(8,128)} %fusion.65, f32[736,1152]{1,0:T(8,128)} %fusion.19, bf16[1152,736]{1,0:T(8,128)(2,1)} %get-tuple-element.58, bf16[1152,1152]{1,0:T(8,128)(2,1)} %bitcast.194), kind=kOutput, calls=%fused_computation.13 | convolution fusion | flops 1956040704 | bytes 17915904 | tf_op jit(solution)/shard_map/dot_general | solution.py:17
  520.7 8.1 %collective-permute-start.52 = (bf16[128,256]{1,0:T(8,128)(2,1)}, bf16[128,256]{1,0:T(8,128)(2,1)S(1)}, u32[]{:S(2)}, u32[]{:S(2)}) collective-permute-start(bf16[128,256]{1,0:T(8,128)(2,1)} %reshape.209), channel_id=1, source_target_pairs={{0,2},{1,3},{2,0},{3,1},{4,6},{5,7},{6,4},{7,5},{8,10},{9,11},{10,... | collective-permute-start | bytes 196616 | tf_op jit(solution)/shard_map/ppermute | solution.py:328
  547.7 6.2 %collective-permute-start.35 = (bf16[1,184,1152]{2,1,0:T(8,128)(2,1)}, bf16[1,184,1152]{2,1,0:T(8,128)(2,1)S(1)}, u32[]{:S(2)}, u32[]{:S(2)}) collective-permute-start(bf16[1,184,1152]{2,1,0:T(8,128)(2,1)} %get-tuple-element.126), channel_id=1, source_target_pairs={{0,3},{1,0},{2,1},{5,4},{6,5},{7,6},{8,11},{9,8},{10,9},{13,12},{1... | collective-permute-start | bytes 1271816 | tf_op jit(solution)/shard_map/ppermute | solution.py:269
  568.9 5.4 collective-permute-done.45.refs_4_
  587.3 7.6 %write_grads.1 = (f32[4,1152,128]{2,1,0:T(8,128)}, f32[4,128,1152]{2,1,0:T(8,128)}, f32[1152,128]{1,0:T(8,128)}, f32[128,4304]{1,0:T(8,128)}, f32[4304,128]{1,0:T(8,128)}, /*index=5*/f32[128,1152]{1,0:T(8,128)}) custom-call(bf16[32,128,512]{2,1,0:T(8,128)(2,1)} %bitcast.167, bf16[32,128,256]{2,1,0:T(8,128)(2,1)} %bitcast.168), custom_call_target="tpu_custom_call" | custom-call | tf_op jit(solution)/shard_map/write_grads/pallas_call | solution.py:415
  (448 shorter events, 285.4 us)
Async XLA Ops:
  7.2 86.7 %all-gather.7.cloned.1.call-start = ((), (), s32[]{:S(2)}) async-start(), calls=%async_computation.2 | async-start | bytes 1658880 | tf_op jit(solution)/shard_map/all_gather | solution.py:275
  10.5 140.8 %all-gather.9.cloned.1.call-start = ((), (), s32[]{:S(2)}) async-start(), calls=%async_computation.3 | async-start | bytes 1566720 | tf_op jit(solution)/shard_map/all_gather | solution.py:275
  18.6 44.7 %collective-permute-start.1 = (bf16[1,184,1152]{2,1,0:T(8,128)(2,1)}, bf16[1,184,1152]{2,1,0:T(8,128)(2,1)}, u32[]{:S(2)}, u32[]{:S(2)}) collective-permute-start(bf16[1,184,1152]{2,1,0:T(8,128)(2,1)} %get-tuple-element.137), channel_id=1, source_target_pairs={{0,2},{2,0},{3,1},{4,6},{5,7},{7,5},{8,10},{10,8},{11,9},{12,14},{... | collective-permute-start | bytes 1271816 | tf_op jit(solution)/shard_map/ppermute | solution.py:249
  21.0 44.2 %collective-permute-start.2 = (bf16[1,184,1152]{2,1,0:T(8,128)(2,1)}, bf16[1,184,1152]{2,1,0:T(8,128)(2,1)}, u32[]{:S(2)}, u32[]{:S(2)}) collective-permute-start(bf16[1,184,1152]{2,1,0:T(8,128)(2,1)} %get-tuple-element.134), channel_id=1, source_target_pairs={{1,0},{2,1},{3,2},{4,7},{6,5},{7,6},{9,8},{10,9},{11,10},{12,15},{... | collective-permute-start | bytes 1271816 | tf_op jit(solution)/shard_map/ppermute | solution.py:249
  77.8 28.9 %collective-permute-start.12 = (bf16[1,184,1152]{2,1,0:T(8,128)(2,1)}, bf16[1,184,1152]{2,1,0:T(8,128)(2,1)}, u32[]{:S(2)}, u32[]{:S(2)}) collective-permute-start(bf16[1,184,1152]{2,1,0:T(8,128)(2,1)} %get-tuple-element.132), channel_id=1, source_target_pairs={{0,1},{1,2},{3,0},{4,5},{5,6},{6,7},{8,9},{9,10},{11,8},{12,13},{1... | collective-permute-start | bytes 1271816 | tf_op jit(solution)/shard_map/ppermute | solution.py:249
  93.9 30.0 %collective-permute-start.3 = (bf16[4,144,1152]{2,1,0:T(8,128)(2,1)}, bf16[4,144,1152]{2,1,0:T(8,128)(2,1)}, u32[]{:S(2)}, u32[]{:S(2)}) collective-permute-start(bf16[4,144,1152]{2,1,0:T(8,128)(2,1)} %bitcast.176), channel_id=1, source_target_pairs={{0,8},{4,12},{8,0},{12,4},{16,24},{20,28},{24,16},{28,20},{1,9},{5... | collective-permute-start | bytes 3981320 | tf_op jit(solution)/shard_map/ppermute | solution.py:233
  96.2 31.6 %collective-permute-start.4 = (bf16[4,144,1152]{2,1,0:T(8,128)(2,1)}, bf16[4,144,1152]{2,1,0:T(8,128)(2,1)}, u32[]{:S(2)}, u32[]{:S(2)}) collective-permute-start(bf16[4,144,1152]{2,1,0:T(8,128)(2,1)} %bitcast.177), channel_id=1, source_target_pairs={{0,16},{4,20},{8,24},{12,28},{16,0},{20,4},{24,8},{28,12},{1,17},{... | collective-permute-start | bytes 3981320 | tf_op jit(solution)/shard_map/ppermute | solution.py:233
  107.8 85.3 %all-gather.11.cloned.1.call-start = ((), (), s32[]{:S(2)}) async-start(), calls=%async_computation.4 | async-start | bytes 1566720 | tf_op jit(solution)/shard_map/all_gather | solution.py:275
  110.9 40.4 %collective-permute-start.7 = (bf16[4,144,1152]{2,1,0:T(8,128)(2,1)}, bf16[4,144,1152]{2,1,0:T(8,128)(2,1)}, u32[]{:S(2)}, u32[]{:S(2)}) collective-permute-start(bf16[4,144,1152]{2,1,0:T(8,128)(2,1)} %bitcast.178), channel_id=1, source_target_pairs={{0,4},{4,0},{8,12},{12,8},{16,20},{20,16},{24,28},{28,24},{1,5},{5... | collective-permute-start | bytes 3981320 | tf_op jit(solution)/shard_map/ppermute | solution.py:233
  151.2 36.9 %collective-permute-start.15 = (bf16[4,72,2176]{2,1,0:T(8,128)(2,1)}, bf16[4,72,2176]{2,1,0:T(8,128)(2,1)S(1)}, u32[]{:S(2)}, u32[]{:S(2)}) collective-permute-start(bf16[4,72,2176]{2,1,0:T(8,128)(2,1)} %bitcast.180), channel_id=1, source_target_pairs={{0,8},{4,12},{8,0},{12,4},{16,24},{20,28},{24,16},{28,20},{1,9},{5... | collective-permute-start | bytes 3760136 | tf_op jit(solution)/shard_map/ppermute | solution.py:233
  153.3 37.7 %collective-permute-start.16 = (bf16[4,72,2176]{2,1,0:T(8,128)(2,1)}, bf16[4,72,2176]{2,1,0:T(8,128)(2,1)}, u32[]{:S(2)}, u32[]{:S(2)}) collective-permute-start(bf16[4,72,2176]{2,1,0:T(8,128)(2,1)} %bitcast.181), channel_id=1, source_target_pairs={{0,16},{4,20},{8,24},{12,28},{16,0},{20,4},{24,8},{28,12},{1,17},{... | collective-permute-start | bytes 3760136 | tf_op jit(solution)/shard_map/ppermute | solution.py:233
  153.4 91.0 %collective-permute-start.19 = (bf16[4,72,2176]{2,1,0:T(8,128)(2,1)}, bf16[4,72,2176]{2,1,0:T(8,128)(2,1)}, u32[]{:S(2)}, u32[]{:S(2)}) collective-permute-start(bf16[4,72,2176]{2,1,0:T(8,128)(2,1)} %bitcast.182), channel_id=1, source_target_pairs={{0,4},{4,0},{8,12},{12,8},{16,20},{20,16},{24,28},{28,24},{1,5},{5... | collective-permute-start | bytes 3760136 | tf_op jit(solution)/shard_map/ppermute | solution.py:233
  189.1 39.7 %collective-permute-start.17 = (bf16[2,72,2176]{2,1,0:T(8,128)(2,1)}, bf16[2,72,2176]{2,1,0:T(8,128)(2,1)}, u32[]{:S(2)}, u32[]{:S(2)}) collective-permute-start(bf16[2,72,2176]{2,1,0:T(8,128)(2,1)} %slice.142), channel_id=1, source_target_pairs={{0,16},{4,20},{8,24},{12,28},{16,0},{20,4},{24,8},{28,12},{1,17},{... | collective-permute-start | bytes 1880072 | tf_op jit(solution)/shard_map/ppermute | solution.py:233
  193.0 35.9 %collective-permute-start.18 = (bf16[2,72,2176]{2,1,0:T(8,128)(2,1)}, bf16[2,72,2176]{2,1,0:T(8,128)(2,1)}, u32[]{:S(2)}, u32[]{:S(2)}) collective-permute-start(bf16[2,72,2176]{2,1,0:T(8,128)(2,1)} %slice.143), channel_id=1, source_target_pairs={{0,8},{4,12},{8,0},{12,4},{16,24},{20,28},{24,16},{28,20},{1,9},{5... | collective-permute-start | bytes 1880072 | tf_op jit(solution)/shard_map/ppermute | solution.py:233
  193.0 43.4 %collective-permute-start.24 = (bf16[4,136,1152]{2,1,0:T(8,128)(2,1)}, bf16[4,136,1152]{2,1,0:T(8,128)(2,1)}, u32[]{:S(2)}, u32[]{:S(2)}) collective-permute-start(bf16[4,136,1152]{2,1,0:T(8,128)(2,1)} %bitcast.24.refs_0_), channel_id=1, source_target_pairs={{0,8},{4,12},{8,0},{12,4},{16,24},{20,28},{24,16},{28,20},{1,9},{5... | collective-permute-start | bytes 3760136 | tf_op jit(solution)/shard_map/ppermute | solution.py:233
  195.1 41.4 %collective-permute-start.25 = (bf16[4,136,1152]{2,1,0:T(8,128)(2,1)}, bf16[4,136,1152]{2,1,0:T(8,128)(2,1)}, u32[]{:S(2)}, u32[]{:S(2)}) collective-permute-start(bf16[4,136,1152]{2,1,0:T(8,128)(2,1)} %bitcast.24.refs_0_), channel_id=1, source_target_pairs={{0,16},{4,20},{8,24},{12,28},{16,0},{20,4},{24,8},{28,12},{1,17},{... | collective-permute-start | bytes 3760136 | tf_op jit(solution)/shard_map/ppermute | solution.py:233
  402.8 101.5 %collective-permute-start.39 = (bf16[128,512]{1,0:T(8,128)(2,1)}, bf16[128,512]{1,0:T(8,128)(2,1)}, u32[]{:S(2)}, u32[]{:S(2)}) collective-permute-start(bf16[128,512]{1,0:T(8,128)(2,1)} %reshape.203), channel_id=1, source_target_pairs={{0,1},{1,2},{2,3},{3,0},{4,5},{5,6},{6,7},{7,4},{8,9},{9,10},{10,1... | collective-permute-start | bytes 393224 | tf_op jit(solution)/shard_map/ppermute | solution.py:328
  405.7 102.1 %collective-permute-start.40 = (bf16[128,512]{1,0:T(8,128)(2,1)}, bf16[128,512]{1,0:T(8,128)(2,1)}, u32[]{:S(2)}, u32[]{:S(2)}) collective-permute-start(bf16[128,512]{1,0:T(8,128)(2,1)} %reshape.203), channel_id=1, source_target_pairs={{0,2},{1,3},{2,0},{3,1},{4,6},{5,7},{6,4},{7,5},{8,10},{9,11},{10,... | collective-permute-start | bytes 393224 | tf_op jit(solution)/shard_map/ppermute | solution.py:328
  406.5 102.8 %collective-permute-start.41 = (bf16[128,512]{1,0:T(8,128)(2,1)}, bf16[128,512]{1,0:T(8,128)(2,1)}, u32[]{:S(2)}, u32[]{:S(2)}) collective-permute-start(bf16[128,512]{1,0:T(8,128)(2,1)} %reshape.203), channel_id=1, source_target_pairs={{0,3},{1,0},{2,1},{3,2},{4,7},{5,4},{6,5},{7,6},{8,11},{9,8},{10,9... | collective-permute-start | bytes 393224 | tf_op jit(solution)/shard_map/ppermute | solution.py:328
  465.4 47.0 %all-to-all-start.1 = ((bf16[32,16,256]{2,1,0:T(8,128)(2,1)}), bf16[32,16,256]{2,1,0:T(8,128)(2,1)}, u32[]{:S(2)}, u32[]{:S(2)}) async-start(bf16[32,16,256]{2,1,0:T(8,128)(2,1)} %bitcast.161), calls=%async_computation.1 | async-start | bytes 524288 | tf_op jit(solution)/shard_map/all_to_all | solution.py:372
  492.6 42.5 %collective-permute-start.36 = (bf16[1,184,1152]{2,1,0:T(8,128)(2,1)}, bf16[1,184,1152]{2,1,0:T(8,128)(2,1)}, u32[]{:S(2)}, u32[]{:S(2)}) collective-permute-start(bf16[1,184,1152]{2,1,0:T(8,128)(2,1)} %get-tuple-element.124), channel_id=1, source_target_pairs={{0,1},{1,2},{2,3},{5,6},{6,7},{7,4},{8,9},{9,10},{10,11},{13,14},{... | collective-permute-start | bytes 1271816 | tf_op jit(solution)/shard_map/ppermute | solution.py:269
  497.0 42.4 %collective-permute-start.37 = (bf16[1,184,1152]{2,1,0:T(8,128)(2,1)}, bf16[1,184,1152]{2,1,0:T(8,128)(2,1)}, u32[]{:S(2)}, u32[]{:S(2)}) collective-permute-start(bf16[1,184,1152]{2,1,0:T(8,128)(2,1)} %get-tuple-element.123), channel_id=1, source_target_pairs={{0,2},{1,3},{2,0},{5,7},{6,4},{7,5},{8,10},{9,11},{10,8},{13,15},{... | collective-permute-start | bytes 1271816 | tf_op jit(solution)/shard_map/ppermute | solution.py:269
  504.3 36.6 %collective-permute-start.38 = (bf16[1,184,1152]{2,1,0:T(8,128)(2,1)}, bf16[1,184,1152]{2,1,0:T(8,128)(2,1)}, u32[]{:S(2)}, u32[]{:S(2)}) collective-permute-start(bf16[1,184,1152]{2,1,0:T(8,128)(2,1)} %get-tuple-element.122), channel_id=1, source_target_pairs={{0,3},{1,0},{2,1},{5,4},{6,5},{7,6},{8,11},{9,8},{10,9},{13,12},{1... | collective-permute-start | bytes 1271816 | tf_op jit(solution)/shard_map/ppermute | solution.py:269
  510.9 30.5 %collective-permute-start.42 = (bf16[4,128,512]{2,1,0:T(8,128)(2,1)}, bf16[4,128,512]{2,1,0:T(8,128)(2,1)}, u32[]{:S(2)}, u32[]{:S(2)}) collective-permute-start(bf16[4,128,512]{2,1,0:T(8,128)(2,1)} %bitcast_dynamic-update-slice_fusion.refs_0_), channel_id=1, source_target_pairs={{0,8},{4,12},{8,0},{12,4},{16,24},{20,28},{24,16},{28,20},{1,9},{5... | collective-permute-start | bytes 1572872 | tf_op jit(solution)/shard_map/ppermute | solution.py:233
  (123 other events, 1122.7 us)
Sparse Core Ops, SparseCore 0:
  10.6 56.3 all-gather.6
  107.9 35.8 all-gather.8
  151.4 30.7 all-gather.10
